TPU v7x, 1024 devices: a whole 8x8x8 slice. The times are simulated.
1024 devices in a mesh: dom: 16 (over x, core), bucket: 64 (over y, z).
Axes of the slice: x: 8, y: 8, z: 8, core: 2. Of those that a mesh axis runs over, the one named last changes fastest.
Arguments:
- emb_table: float32 [262144, 400], P(('dom', 'bucket')), may hold values from -1.6 to 1.6
- rel_diag: float32 [256, 400], replicated, may hold values from 0.5 to 1.5
- send_rows: int32 [16, 64, 16, 32], P('dom', 'bucket'), may hold values from -1 to 255, as said below
- src_slot: int32 [16, 64, 256], P('dom', 'bucket'), may hold values from 0 to 511, as said below
- dst_slot: int32 [16, 64, 256], P('dom', 'bucket'), may hold values from 0 to 511, as said below
- neg_rows: int32 [16, 64, 2, 2], P('dom', 'bucket'), may hold values from 0 to 255
- block_rel: int32 [16, 64, 2], P('dom', 'bucket'), may hold values from 0 to 255
Outputs:
- emb_grad: float32 [262144, 400], P(('dom', 'bucket'))
Inputs may be any that keep to these rules, and one draw needn't show every extreme that they name: `send_rows`: entries of one owner, column and bucket device are live (not -1) for slots 0 to some count - 1 and -1 after; at most 32 live rows go from one owner to one bucket device, and every owner fills all 32 slots for some bucket device of its column. `src_slot`: every edge's source slot is a live slot of the received rows. `dst_slot`: every edge's destination slot is a live slot of the received rows.
All inputs are finite; a program needn't handle non-finite values.
Results may differ from a plain program's by a relative error of at most 0.0003.
Values sent between devices are 32-bit elements; how exact they have to be, the bound alone decides.
No kernel may reach another device: no remote copies, remote signals or barrier semaphores. Data moves between devices by JAX's collectives and lax.ppermute only.
A program may use at most 32 MiB of HBM per device.

v0:
```python
import jax
import jax.numpy as jnp
from jax import lax
from jax.sharding import PartitionSpec as P


def block_grads(sources, targets, negatives, relation):
    highest = lax.Precision.HIGHEST
    query = sources * relation
    positive = jnp.sum(query * targets, axis=-1)
    scores = jnp.einsum("cek,cjk->cej", query, negatives, precision=highest)
    largest = jnp.maximum(jnp.max(scores, axis=-1), positive)
    pos_exp = jnp.exp(positive - largest)
    neg_exp = jnp.exp(scores - largest[..., None])
    total = pos_exp + jnp.sum(neg_exp, axis=-1)
    pos_weight = pos_exp / total - 1.0
    neg_weight = neg_exp / total[..., None]
    query_grad = pos_weight[..., None] * targets + jnp.einsum(
        "cej,cjk->cek", neg_weight, negatives, precision=highest
    )
    neg_grad = jnp.einsum("cej,cek->cjk", neg_weight, query, precision=highest)
    return (query_grad * relation, pos_weight[..., None] * query, neg_grad)


def on_device(emb_table, rel_diag, send_rows, src_slot, dst_slot, neg_rows, block_rel):
    ent_dev, width = emb_table.shape
    send_list = send_rows[0, 0]
    owners, slot_cap = send_list.shape
    alive = send_list >= 0
    picked = jnp.where(alive[..., None], emb_table[jnp.maximum(send_list, 0)], jnp.float32(0.0))
    incoming = lax.all_to_all(picked, "dom", split_axis=0, concat_axis=0, tiled=True).reshape(
        owners * slot_cap, width
    )
    blocks = block_rel.shape[2]
    source_idx = src_slot[0, 0]
    target_idx = dst_slot[0, 0]
    sources = incoming[source_idx].reshape(blocks, -1, width)
    targets = incoming[target_idx].reshape(blocks, -1, width)
    relation = rel_diag[block_rel[0, 0]][:, None, :]
    own_negs = emb_table[neg_rows[0, 0]]

    def one_block(carry, inputs):
        block_src, block_dst, block_negs, block_relation = inputs
        negatives = lax.all_gather(block_negs, "bucket", axis=0, tiled=True)
        src_part, dst_part, neg_part = block_grads(
            block_src[None], block_dst[None], negatives[None], block_relation[None]
        )
        returned = lax.psum_scatter(neg_part[0], "bucket", scatter_dimension=0, tiled=True)
        return (carry, (src_part[0], dst_part[0], returned))

    _, (src_grad, dst_grad, own_grad) = lax.scan(
        one_block, jnp.float32(0.0), (sources, targets, own_negs, relation)
    )
    slot_grads = jnp.zeros((owners * slot_cap, width), jnp.float32)
    slot_grads = slot_grads.at[source_idx].add(src_grad.reshape(-1, width))
    slot_grads = slot_grads.at[target_idx].add(dst_grad.reshape(-1, width))
    returned_rows = lax.all_to_all(
        slot_grads.reshape(owners, slot_cap, width), "dom", split_axis=0, concat_axis=0, tiled=True
    )
    row_targets = jnp.where(alive, send_list, ent_dev).reshape(-1)
    result = jnp.zeros((ent_dev, width), jnp.float32)
    result = result.at[row_targets].add(returned_rows.reshape(-1, width), mode="drop")
    result = result.at[neg_rows[0, 0].reshape(-1)].add(own_grad.reshape(-1, width))
    return result


def solution(mesh):
    placed = (
        P(("dom", "bucket"), None),
        P(),
        P("dom", "bucket", None, None),
        P("dom", "bucket", None),
        P("dom", "bucket", None),
        P("dom", "bucket", None, None),
        P("dom", "bucket", None),
    )
    return jax.shard_map(
        on_device, mesh=mesh, in_specs=placed, out_specs=P(("dom", "bucket"), None), check_vma=False
    )
```

profile of v0, /device:TPU:1, one launch (start us, length us, event | category | flops | bytes accessed | tf_op | source)
XLA Modules:
  0.0 544.0 jit_solution(9202954090741363334)
XLA Ops:
  6.5 0.8 broadcast_maximum_fusion
  7.3 1.2 copy.39
  8.6 1.6 gather_fusion
  10.2 1.1 broadcast_select_fusion
  11.4 17.7 %all-to-all-start = ((f32[16,32,400]{2,1,0:T(8,128)}), f32[16,32,400]{2,1,0:T(8,128)S(1)}, u32[]{:S(2)}, u32[]{:S(2)}) async-start(f32[16,32,400]{2,1,0:T(8,128)} %broadcast_select_fusion), calls=%async_computation | async-start | bytes 2097152 | tf_op jit(solution)/shard_map/all_to_all | solution.py:31
  29.1 0.7 copy-done.4
  29.9 0.6 gather_fusion.4
  30.7 0.6 copy-done.5
  32.1 0.7 copy-done.3
  32.7 24.3 %all-to-all-done = f32[16,32,400]{2,1,0:T(8,128)S(1)} async-done(((f32[16,32,400]{2,1,0:T(8,128)}), f32[16,32,400]{2,1,0:T(8,128)S(1)}, u32[]{:S(2)}, u32[]{:S(2)}) %all-to-all-start) | async-done | bytes 819232 | tf_op jit(solution)/shard_map/all_to_all | solution.py:31
  57.1 1.0 gather_fusion.1
  58.2 1.0 gather_fusion.3
  59.4 425.0 %while.16 = (s32[]{:T(128)}, f32[2,128,400]{1,2,0:T(8,128)S(1)}, f32[2,128,400]{1,2,0:T(8,128)S(1)}, f32[2,2,400]{2,1,0:T(2,128)S(1)}, f32[2,128,400]{1,2,0:T(8,...) while((s32[]{:T(128)}, f32[2,128,400]{1,2,0:T(8,128)S(1)}, ...), condition=%wide.region_5.6_spmd, body=%wide.region_0.5_spmd.sunk | while | flops 236607744 | bytes 4518585 | solution.py:51
  59.5 42.0 %all-gather.2 = f32[1,128,400]{2,0,1:T(1,128)S(1)} all-gather(f32[1,2,400]{2,0,1:T(1,128)S(1)} %copy.59), channel_id=2, replica_groups=mesh['dom'=16,'bucket'=64] {'bucket'}, dimensions={1}, use_global_device_ids=true | all-gather | bytes 208000 | tf_op jit(solution)/shard_map/while/body/eval_jaxpr/all_gather | solution.py:44
  101.7 0.7 fusion.40
  102.6 1.2 fusion.44
  103.8 1.3 dynamic-slice.8
  106.3 163.5 %all-reduce.5.cloned.1.call-done = f32[128,400]{1,0:T(8,128)} async-done(((f32[128,400]{1,0:T(8,128)}), f32[128,400]{1,0:T(8,128)}) %all-reduce.5.cloned.1.call-update) | async-done | bytes 204816 | tf_op jit(solution)/shard_map/while
  269.8 0.7 fusion.45
  270.5 35.7 %all-gather.2 = f32[1,128,400]{2,0,1:T(1,128)S(1)} all-gather(f32[1,2,400]{2,0,1:T(1,128)S(1)} %copy.59), channel_id=2, replica_groups=mesh['dom'=16,'bucket'=64] {'bucket'}, dimensions={1}, use_global_device_ids=true | all-gather | bytes 208000 | tf_op jit(solution)/shard_map/while/body/eval_jaxpr/all_gather | solution.py:44
  306.3 0.7 fusion.40
  307.3 1.2 fusion.44
  308.5 1.3 dynamic-slice.8
  310.9 172.8 %all-reduce.5.cloned.1.call-done = f32[128,400]{1,0:T(8,128)} async-done(((f32[128,400]{1,0:T(8,128)}), f32[128,400]{1,0:T(8,128)}) %all-reduce.5.cloned.1.call-update) | async-done | bytes 204816 | tf_op jit(solution)/shard_map/while
  483.7 0.7 fusion.45
  484.9 3.1 scatter_custom_fusion
  487.9 4.2 scatter_fusion
  492.2 11.5 %all-to-all-start.1 = ((f32[16,32,400]{2,1,0:T(8,128)}), f32[16,32,400]{2,1,0:T(8,128)S(1)}, u32[]{:S(2)}, u32[]{:S(2)}) async-start(f32[16,32,400]{2,1,0:T(8,128)} %bitcast.21), calls=%async_computation.1 | async-start | bytes 2097152 | tf_op jit(solution)/shard_map/all_to_all | solution.py:57
  503.9 27.7 %all-to-all-done.1 = f32[16,32,400]{2,1,0:T(8,128)S(1)} async-done(((f32[16,32,400]{2,1,0:T(8,128)}), f32[16,32,400]{2,1,0:T(8,128)S(1)}, u32[]{:S(2)}, u32[]{:S(2)}) %all-to-all-start.1) | async-done | bytes 819232 | tf_op jit(solution)/shard_map/all_to_all | solution.py:57
  531.6 3.7 scatter_custom_fusion.2
  535.3 0.8 scatter_fusion.1
  536.2 0.9 copy.50
  (60 shorter events, 3.8 us)
Async XLA Ops:
  6.5 0.8 copy-start.1
  11.4 19.1 %copy-start = (f32[256,400]{0,1:T(8,128)S(1)}, f32[256,400]{0,1:T(8,128)}, u32[]{:S(2)}) copy-start(f32[256,400]{0,1:T(8,128)} %param.10) | copy-start | bytes 1228804
  11.4 45.7 %all-to-all-start = ((f32[16,32,400]{2,1,0:T(8,128)}), f32[16,32,400]{2,1,0:T(8,128)S(1)}, u32[]{:S(2)}, u32[]{:S(2)}) async-start(f32[16,32,400]{2,1,0:T(8,128)} %broadcast_select_fusion), calls=%async_computation | async-start | bytes 2097152 | tf_op jit(solution)/shard_map/all_to_all | solution.py:31
  29.1 0.7 copy-start.4
  30.7 0.7 copy-start.5
  31.4 0.7 copy-start.2
  32.0 0.7 copy-start.3
  59.4 210.3 %all-reduce.5.cloned.1.call-start = ((), (), s32[]{:S(2)}) async-start(), calls=%async_computation.2 | async-start | bytes 524288 | tf_op jit(solution)/shard_map/while
  270.5 213.2 %all-reduce.5.cloned.1.call-start = ((), (), s32[]{:S(2)}) async-start(), calls=%async_computation.2 | async-start | bytes 524288 | tf_op jit(solution)/shard_map/while
  492.2 39.4 %all-to-all-start.1 = ((f32[16,32,400]{2,1,0:T(8,128)}), f32[16,32,400]{2,1,0:T(8,128)S(1)}, u32[]{:S(2)}, u32[]{:S(2)}) async-start(f32[16,32,400]{2,1,0:T(8,128)} %bitcast.21), calls=%async_computation.1 | async-start | bytes 2097152 | tf_op jit(solution)/shard_map/all_to_all | solution.py:57
Sparse Core Ops, SparseCore 0:
  104.0 165.7 all-reduce.4
  308.6 175.0 all-reduce.4
where the time goes:
time: 545 us; the launch traced here: 544 us
  waiting for transfers between devices  388 us (71%)
  blocking collectives  77.7 us (14%)
  starting transfers between devices  29.3 us (5%)
  local copies, waits for them, and re-layouts  14.7 us (3%)
  other arithmetic  14.5 us (3%)
  between operations  13.5 us (2%)
    while x4, waiting for transfers between devices  336 us
    all_gather x2, blocking collectives, one_block(): negatives = lax.all_gather(block_negs, 'bucket', axis=0, tiled=True)  77.7 us
    all_to_all x1, waiting for transfers between devices, on_device(): lax.all_to_all(slot_grads.reshape(owners, slot_cap, width), 'dom', split_...  27.7 us
    all_to_all x1, waiting for transfers between devices, on_device(): lax.all_to_all(picked, 'dom', split_axis=0, concat_axis=0, tiled=True)  24.3 us
    all_to_all x1, starting transfers between devices, on_device(): lax.all_to_all(picked, 'dom', split_axis=0, concat_axis=0, tiled=True)  17.7 us
    all_to_all x1, starting transfers between devices, on_device(): lax.all_to_all(slot_grads.reshape(owners, slot_cap, width), 'dom', split_...  11.5 us
  transfers between devices with their start and end apart: 4, of which 4 were waited for; matrix products, arithmetic and copies ran while one was open for 1% of the time, Pallas kernels for 0%

commit v1 on v0

--- a/solution.py
+++ b/solution.py
@@ -38,19 +38,15 @@
     targets = incoming[target_idx].reshape(blocks, -1, width)
     relation = rel_diag[block_rel[0, 0]][:, None, :]
     own_negs = emb_table[neg_rows[0, 0]]
-
-    def one_block(carry, inputs):
-        block_src, block_dst, block_negs, block_relation = inputs
-        negatives = lax.all_gather(block_negs, "bucket", axis=0, tiled=True)
-        src_part, dst_part, neg_part = block_grads(
-            block_src[None], block_dst[None], negatives[None], block_relation[None]
-        )
-        returned = lax.psum_scatter(neg_part[0], "bucket", scatter_dimension=0, tiled=True)
-        return (carry, (src_part[0], dst_part[0], returned))
-
-    _, (src_grad, dst_grad, own_grad) = lax.scan(
-        one_block, jnp.float32(0.0), (sources, targets, own_negs, relation)
-    )
+    columns = lax.axis_size("bucket")
+    neg_dev = own_negs.shape[1]
+    sent = jnp.broadcast_to(own_negs[None], (columns, blocks, neg_dev, width))
+    gathered = lax.all_to_all(sent, "bucket", split_axis=0, concat_axis=0, tiled=True)
+    negatives = jnp.transpose(gathered, (1, 0, 2, 3)).reshape(blocks, columns * neg_dev, width)
+    src_grad, dst_grad, neg_part = block_grads(sources, targets, negatives, relation)
+    parts = jnp.transpose(neg_part.reshape(blocks, columns, neg_dev, width), (1, 0, 2, 3))
+    returned = lax.all_to_all(parts, "bucket", split_axis=0, concat_axis=0, tiled=True)
+    own_grad = jnp.sum(returned, axis=0)
     slot_grads = jnp.zeros((owners * slot_cap, width), jnp.float32)
     slot_grads = slot_grads.at[source_idx].add(src_grad.reshape(-1, width))
     slot_grads = slot_grads.at[target_idx].add(dst_grad.reshape(-1, width))

time: 545 us -> 150 us (0.28)
  waiting for transfers between devices: 388 us -> 76.5 us
  blocking collectives: 77.7 us -> 0 us
  starting transfers between devices: 29.3 us -> 44.9 us
  between operations: 13.5 us -> 0.2 us
    while x4 -> x0, waiting for transfers between devices: 336 us -> none
    all_gather x2 -> x0, blocking collectives: 77.7 us -> none  [one_block(): negatives = lax.all_gather(block_negs, 'bucket', axis=0, tiled=True)]
    all_to_all x0 -> x2, starting transfers between devices: none -> 29.1 us  [the longest x1 24.1 us: on_device(): lax.all_to_all(sent, 'bucket', split_axis=0, concat_axis=0, tiled=True)]
    all_to_all x0 -> x2, waiting for transfers between devices: none -> 23.3 us  [the longest x1 13.5 us: on_device(): lax.all_to_all(sent, 'bucket', split_axis=0, concat_axis=0, tiled=True)]
    all_to_all x1, starting transfers between devices: 17.7 us -> 10.7 us  [on_device(): lax.all_to_all(picked, 'dom', split_axis=0, concat_axis=0, tiled=True)]
    all_to_all x1, starting transfers between devices: 11.5 us -> 5.13 us  [on_device(): lax.all_to_all(slot_grads.reshape(owners, slot_cap, width), 'dom', split_...]
  transfers between devices with their start and end apart: 4 -> 4, of which waited for: 4 -> 4; matrix products, arithmetic and copies ran while one was open for 1% -> 8% of each run, Pallas kernels for 0% -> 0%
where the time goes in v1:
time: 150 us
  waiting for transfers between devices  76.5 us (51%)
  starting transfers between devices  44.9 us (30%)
  other arithmetic  14.3 us (10%)
  local copies, waits for them, and re-layouts  11.4 us (8%)
  matrix products  2.25 us (2%)
    all_to_all x1, waiting for transfers between devices, on_device(): lax.all_to_all(slot_grads.reshape(owners, slot_cap, width), 'dom', split_...  27.5 us
    all_to_all x1, waiting for transfers between devices, on_device(): lax.all_to_all(picked, 'dom', split_axis=0, concat_axis=0, tiled=True)  25.7 us
    all_to_all x1, starting transfers between devices, on_device(): lax.all_to_all(sent, 'bucket', split_axis=0, concat_axis=0, tiled=True)  24.1 us
    all_to_all x1, waiting for transfers between devices, on_device(): lax.all_to_all(sent, 'bucket', split_axis=0, concat_axis=0, tiled=True)  13.5 us
    all_to_all x1, starting transfers between devices, on_device(): lax.all_to_all(picked, 'dom', split_axis=0, concat_axis=0, tiled=True)  10.7 us
    all_to_all x1, waiting for transfers between devices, on_device(): lax.all_to_all(parts, 'bucket', split_axis=0, concat_axis=0, tiled=True)  9.88 us
    all_to_all x1, starting transfers between devices, on_device(): lax.all_to_all(slot_grads.reshape(owners, slot_cap, width), 'dom', split_...  5.13 us
    all_to_all x1, starting transfers between devices, on_device(): lax.all_to_all(parts, 'bucket', split_axis=0, concat_axis=0, tiled=True)  5.06 us
  transfers between devices with their start and end apart: 4, of which 4 were waited for; matrix products, arithmetic and copies ran while one was open for 8% of the time, Pallas kernels for 0%

profile of v1, /device:TPU:1, one launch (start us, length us, event | category | flops | bytes accessed | tf_op | source)
XLA Modules:
  0.0 149.6 jit_solution(12661186942702612891)
XLA Ops:
  0.0 0.7 compare_select_fusion.4
  0.8 1.2 copy.33
  2.0 0.6 gather_fusion.4
  2.6 1.0 broadcast_in_dim.26
  3.5 24.1 %all-to-all-start.1 = ((f32[64,2,2,400]{3,1,2,0:T(2,128)}), f32[64,2,2,400]{3,1,2,0:T(2,128)S(1)}, u32[]{:S(2)}, u32[]{:S(2)}) async-start(f32[64,2,2,400]{3,1,2,0:T(2,128)} %broadcast_in_dim.26), calls=%async_computation.1 | async-start | bytes 1048576 | tf_op jit(solution)/shard_map/all_to_all | solution.py:44
  27.7 1.6 %gather_fusion = f32[512,400]{1,0:T(8,128)S(1)} fusion(f32[256,400]{1,0:T(8,128)S(1)} %copy.33, s32[1024]{0:T(1024)S(1)} %pad_clamp_fusion.4), kind=kCustom, calls=%fused_computation | custom fusion | bytes 1640448 | tf_op jit(solution)/shard_map/gather | solution.py:30
  29.4 1.1 broadcast_select_fusion
  30.5 13.5 %all-to-all-done.1 = f32[64,2,2,400]{3,1,2,0:T(2,128)S(1)} async-done(((f32[64,2,2,400]{3,1,2,0:T(2,128)}), f32[64,2,2,400]{3,1,2,0:T(2,128)S(1)}, u32[]{:S(2)}, u32[]{:S(2)}) %all-to-all-start.1) | async-done | bytes 409632 | tf_op jit(solution)/shard_map/all_to_all | solution.py:44
  44.0 10.7 %all-to-all-start = ((f32[16,32,400]{2,1,0:T(8,128)}), f32[16,32,400]{2,1,0:T(8,128)S(1)}, u32[]{:S(2)}, u32[]{:S(2)}) async-start(f32[16,32,400]{2,1,0:T(8,128)} %broadcast_select_fusion), calls=%async_computation | async-start | bytes 2097152 | tf_op jit(solution)/shard_map/all_to_all | solution.py:31
  54.6 0.2 copy.35
  54.9 0.4 copy-done.5
  55.3 0.6 gather_fusion.2
  56.0 0.7 copy-done.3
  56.7 0.2 copy.41
  56.9 25.7 %all-to-all-done = f32[16,32,400]{2,1,0:T(8,128)S(1)} async-done(((f32[16,32,400]{2,1,0:T(8,128)}), f32[16,32,400]{2,1,0:T(8,128)S(1)}, u32[]{:S(2)}, u32[]{:S(2)}) %all-to-all-start) | async-done | bytes 819232 | tf_op jit(solution)/shard_map/all_to_all | solution.py:31
  82.6 1.0 gather_fusion.1
  83.5 1.0 gather_fusion.3
  85.1 1.2 fusion.21
  86.3 0.6 fusion.4
  86.9 1.0 copy.50
  87.9 5.1 %all-to-all-start.3 = ((f32[64,2,2,400]{3,1,2,0:T(2,128)}), f32[64,2,2,400]{3,1,2,0:T(2,128)S(1)}, u32[]{:S(2)}, u32[]{:S(2)}) async-start(f32[64,2,2,400]{3,1,2,0:T(2,128)} %bitcast.25), calls=%async_computation.3 | async-start | bytes 1048576 | tf_op jit(solution)/shard_map/all_to_all | solution.py:48
  93.1 0.5 fusion
  93.7 0.2 copy.60
  93.9 3.1 %scatter_custom_fusion = f32[512,400]{1,0:T(8,128)} fusion(s32[256]{0:T(256)S(1)} %bitcast.65, f32[256,400]{1,0:T(8,128)S(1)} %bitcast.61, f32[]{:T(128)} %constant.6.clone.1), kind=kCustom, calls=%fused_computation.14 | custom fusion | flops 102400 | bytes 819204 | tf_op jit(solution)/shard_map/scatter-add | solution.py:51
  96.9 4.2 %scatter_fusion = f32[512,400]{1,0:T(8,128)} fusion(f32[512,400]{1,0:T(8,128)} %scatter_custom_fusion, s32[256]{0:T(256)S(1)} %bitcast.63, f32[256,400]{1,0:T(8,128)S(1)} %fusion.1), kind=kCustom, calls=%fused_computation.6 | custom fusion | flops 102400 | bytes 1229824 | tf_op jit(solution)/shard_map/scatter-add | solution.py:52
  101.2 9.9 %all-to-all-done.3 = f32[64,2,2,400]{3,1,2,0:T(2,128)S(1)} async-done(((f32[64,2,2,400]{3,1,2,0:T(2,128)}), f32[64,2,2,400]{3,1,2,0:T(2,128)S(1)}, u32[]{:S(2)}, u32[]{:S(2)}) %all-to-all-start.3) | async-done | bytes 409632 | tf_op jit(solution)/shard_map/all_to_all | solution.py:48
  111.1 5.1 %all-to-all-start.2 = ((f32[16,32,400]{2,1,0:T(8,128)}), f32[16,32,400]{2,1,0:T(8,128)S(1)}, u32[]{:S(2)}, u32[]{:S(2)}) async-start(f32[16,32,400]{2,1,0:T(8,128)} %bitcast.21), calls=%async_computation.2 | async-start | bytes 2097152 | tf_op jit(solution)/shard_map/all_to_all | solution.py:53
  116.4 0.2 reduce_sum.35
  116.6 27.5 %all-to-all-done.2 = f32[16,32,400]{2,1,0:T(8,128)S(1)} async-done(((f32[16,32,400]{2,1,0:T(8,128)}), f32[16,32,400]{2,1,0:T(8,128)S(1)}, u32[]{:S(2)}, u32[]{:S(2)}) %all-to-all-start.2) | async-done | bytes 819232 | tf_op jit(solution)/shard_map/all_to_all | solution.py:53
  144.1 3.7 %scatter_custom_fusion.2 = f32[256,400]{1,0:T(8,128)S(1)} fusion(s32[512]{0:T(512)S(1)} %bitcast.66, f32[512,400]{1,0:T(8,128)S(1)} %bitcast.60, f32[]{:T(128)} %constant.6.clone.1), kind=kCustom, calls=%fused_computation.21 | custom fusion | flops 204800 | bytes 409604 | tf_op jit(solution)/shard_map/scatter-add | solution.py:58
  147.8 0.8 scatter_fusion.1
  148.7 0.9 copy.52
  (38 shorter events, 1.3 us)
Async XLA Ops:
  3.5 24.1 %copy-start.1 = (s32[1,1,16,32]{3,2,1,0:T(8,128)S(1)}, s32[1,1,16,32]{3,2,1,0:T(8,128)}, u32[]{:S(2)}) copy-start(s32[1,1,16,32]{3,2,1,0:T(8,128)} %param.9) | copy-start | bytes 6148
  3.5 40.4 %all-to-all-start.1 = ((f32[64,2,2,400]{3,1,2,0:T(2,128)}), f32[64,2,2,400]{3,1,2,0:T(2,128)S(1)}, u32[]{:S(2)}, u32[]{:S(2)}) async-start(f32[64,2,2,400]{3,1,2,0:T(2,128)} %broadcast_in_dim.26), calls=%async_computation.1 | async-start | bytes 1048576 | tf_op jit(solution)/shard_map/all_to_all | solution.py:44
  30.5 24.1 %copy-start = (f32[256,400]{0,1:T(8,128)S(1)}, f32[256,400]{0,1:T(8,128)}, u32[]{:S(2)}) copy-start(f32[256,400]{0,1:T(8,128)} %param.8) | copy-start | bytes 1228804
  44.0 38.6 %all-to-all-start = ((f32[16,32,400]{2,1,0:T(8,128)}), f32[16,32,400]{2,1,0:T(8,128)S(1)}, u32[]{:S(2)}, u32[]{:S(2)}) async-start(f32[16,32,400]{2,1,0:T(8,128)} %broadcast_select_fusion), calls=%async_computation | async-start | bytes 2097152 | tf_op jit(solution)/shard_map/all_to_all | solution.py:31
  54.6 0.7 copy-start.5
  55.3 0.7 copy-start.2
  56.0 0.7 copy-start.3
  87.9 23.1 %all-to-all-start.3 = ((f32[64,2,2,400]{3,1,2,0:T(2,128)}), f32[64,2,2,400]{3,1,2,0:T(2,128)S(1)}, u32[]{:S(2)}, u32[]{:S(2)}) async-start(f32[64,2,2,400]{3,1,2,0:T(2,128)} %bitcast.25), calls=%async_computation.3 | async-start | bytes 1048576 | tf_op jit(solution)/shard_map/all_to_all | solution.py:48
  111.1 5.1 %copy-start.4 = (s32[1,1,2,2]{3,2,1,0:T(2,128)S(1)}, s32[1,1,2,2]{3,2,1,0:T(2,128)}, u32[]{:S(2)}) copy-start(s32[1,1,2,2]{3,2,1,0:T(2,128)} %param.12) | copy-start | bytes 52
  111.1 33.1 %all-to-all-start.2 = ((f32[16,32,400]{2,1,0:T(8,128)}), f32[16,32,400]{2,1,0:T(8,128)S(1)}, u32[]{:S(2)}, u32[]{:S(2)}) async-start(f32[16,32,400]{2,1,0:T(8,128)} %bitcast.21), calls=%async_computation.2 | async-start | bytes 2097152 | tf_op jit(solution)/shard_map/all_to_all | solution.py:53

commit v2 on v1

v2 whole, which is shorter than its diff:
```python
import functools

import jax
import jax.numpy as jnp
from jax import lax
from jax.experimental import pallas as pl
from jax.experimental.pallas import tpu as pltpu
from jax.sharding import PartitionSpec as P

LANES = 128
CHUNKS = 4
TAIL = 16
WIDE = CHUNKS * LANES
HIGHEST = lax.Precision.HIGHEST
VMEM = pl.BlockSpec(memory_space=pltpu.VMEM)
SMEM = pl.BlockSpec(memory_space=pltpu.SMEM)


def split(x, terms):
    parts = []
    for _ in range(terms):
        part = x.astype(jnp.bfloat16)
        parts.append(part)
        x = x - part.astype(jnp.float32)
    return parts


def select_rows(onehot, x, terms):
    total = None
    for part in split(x, terms):
        product = jnp.dot(onehot, part, preferred_element_type=jnp.float32)
        total = product if total is None else total + product
    return total


def onehot_of(index, shape, axis):
    return jnp.where(index == lax.broadcasted_iota(jnp.int32, shape, axis), 1.0, 0.0).astype(jnp.bfloat16)


def pack(x, out_ref):
    owners = out_ref.shape[0]
    slots = x.shape[0] // owners
    group = slots // 4
    for j in range(CHUNKS - 1):
        out_ref[:, j * slots : (j + 1) * slots, :] = x[:, j * LANES : (j + 1) * LANES].reshape(owners, slots, LANES)
    tails = x[:, (CHUNKS - 1) * LANES :].reshape(owners, 4, group, LANES)
    tail = tails[:, 0].reshape(owners * group, LANES)
    for q in range(1, 4):
        tail = tail + pltpu.roll(tails[:, q].reshape(owners * group, LANES), TAIL * q, 1)
    out_ref[:, (CHUNKS - 1) * slots :, :] = tail.reshape(owners, group, LANES)


def unpack(ref, out_ref):
    owners = ref.shape[0]
    slots = out_ref.shape[0] // owners
    group = slots // 4
    for j in range(CHUNKS - 1):
        out_ref[:, j * LANES : (j + 1) * LANES] = ref[:, j * slots : (j + 1) * slots, :].reshape(owners * slots, LANES)
    tail = ref[:, (CHUNKS - 1) * slots :, :].reshape(owners * group, LANES)
    live = lax.broadcasted_iota(jnp.int32, tail.shape, 1) < TAIL
    tails = []
    for q in range(4):
        turned = tail if q == 0 else pltpu.roll(tail, LANES - TAIL * q, 1)
        tails.append(jnp.where(live, turned, 0.0).reshape(owners, group, LANES))
    out_ref[:, (CHUNKS - 1) * LANES :] = jnp.stack(tails, axis=1).reshape(owners * slots, LANES)


def widen(ref, out_ref):
    out_ref[:, WIDE - LANES :] = jnp.zeros((out_ref.shape[0], LANES), jnp.float32)
    out_ref[:, : ref.shape[1]] = ref[...]


def pick_kernel(neg_ref, send_ref, table_ref, rows_ref, negs_ref, table):
    widen(table_ref, table)
    for n in range(neg_ref.shape[0]):
        row = table[pl.ds(neg_ref[n], 1), :]
        for j in range(CHUNKS):
            negs_ref[j * 4 + n : j * 4 + n + 1, :] = row[:, j * LANES : (j + 1) * LANES]
    slots, entities = send_ref.shape[0], table_ref.shape[0]
    onehot = onehot_of(send_ref[...], (slots, entities), 1)
    pack(select_rows(onehot, table[...], 3), rows_ref)


def grad_kernel(col_ref, row_ref, rel_ref, got_ref, negs_ref, back_ref, negs_back_ref, rows, negs, grads):
    unpack(got_ref, rows)
    slots, ends = rows.shape[0], col_ref.shape[0]
    edges = ends // 2
    blocks = rel_ref.shape[0]
    block = edges // blocks
    owners = negs_ref.shape[0] // 16
    picked = select_rows(onehot_of(col_ref[...], (ends, slots), 1), rows[...], 3)
    for c in range(blocks):
        for k in range(2):
            for j in range(CHUNKS):
                negs[k * owners : (k + 1) * owners, j * LANES : (j + 1) * LANES] = negs_ref[
                    pl.ds(j * 4 + c * 2 + k, owners, stride=16), :
                ]
        negatives = negs[...]
        relation = rel_ref[c : c + 1, :]
        query = picked[c * block : (c + 1) * block] * relation
        target = picked[edges + c * block : edges + (c + 1) * block]
        positive = jnp.sum(query * target, axis=1, keepdims=True)
        scores = lax.dot_general(
            query, negatives, (((1,), (1,)), ((), ())), precision=HIGHEST, preferred_element_type=jnp.float32
        )
        largest = jnp.maximum(jnp.max(scores, axis=1, keepdims=True), positive)
        pos_exp = jnp.exp(positive - largest)
        neg_exp = jnp.exp(scores - largest)
        total = pos_exp + jnp.sum(neg_exp, axis=1, keepdims=True)
        pos_weight = pos_exp / total - 1.0
        weight = neg_exp / total
        query_grad = pos_weight * target + jnp.dot(
            weight, negatives, precision=HIGHEST, preferred_element_type=jnp.float32
        )
        grads[c * block : (c + 1) * block, :] = query_grad * relation
        grads[edges + c * block : edges + (c + 1) * block, :] = pos_weight * query
        neg_grad = jnp.dot(weight.T, query, precision=HIGHEST, preferred_element_type=jnp.float32)
        for k in range(2):
            for j in range(CHUNKS):
                negs_back_ref[pl.ds(j * 4 + c * 2 + k, owners, stride=16), :] = neg_grad[
                    k * owners : (k + 1) * owners, j * LANES : (j + 1) * LANES
                ]
    pack(select_rows(onehot_of(row_ref[...], (slots, ends), 0), grads[...], 2), back_ref)


def put_kernel(neg_ref, send_ref, got_ref, negs_ref, out_ref, rows):
    unpack(got_ref, rows)
    entities, width = out_ref.shape
    result = select_rows(onehot_of(send_ref[...], (entities, rows.shape[0]), 0), rows[...], 2)
    own = jnp.sum(negs_ref[...], axis=0)
    place = lax.broadcasted_iota(jnp.int32, (entities, LANES), 0)
    for j in range(CHUNKS):
        part = result[:, j * LANES : (j + 1) * LANES]
        for n in range(neg_ref.shape[0]):
            part = part + jnp.where(place == neg_ref[n], own[j * 4 + n : j * 4 + n + 1, :], 0.0)
        stop = min(width, (j + 1) * LANES)
        out_ref[:, j * LANES : stop] = part[:, : stop - j * LANES]


def shaped(*shape):
    return jax.ShapeDtypeStruct(shape, jnp.float32)


def scratch(*shape):
    return pltpu.VMEM(shape, jnp.float32)


def on_device(emb_table, rel_diag, send_rows, src_slot, dst_slot, neg_rows, block_rel):
    entities, width = emb_table.shape
    owners, slots = send_rows.shape[2:]
    columns = lax.axis_size("bucket")
    packed = (owners, (CHUNKS - 1) * slots + slots // 4, LANES)
    send = send_rows.reshape(owners * slots)
    own_rows = neg_rows.reshape(4)
    picked, own_negs = pl.pallas_call(
        pick_kernel,
        out_shape=(shaped(*packed), shaped(16, LANES)),
        in_specs=[SMEM, VMEM, VMEM],
        out_specs=(VMEM, VMEM),
        scratch_shapes=[scratch(entities, WIDE)],
        name="pick",
    )(own_rows, send[:, None], emb_table)
    negs = lax.all_to_all(
        jnp.broadcast_to(own_negs, (columns, 16, LANES)), "bucket", split_axis=0, concat_axis=0, tiled=True
    )
    got = lax.all_to_all(picked, "dom", split_axis=0, concat_axis=0, tiled=True)
    ends = jnp.concatenate([src_slot.reshape(-1), dst_slot.reshape(-1)])
    relation = jnp.pad(rel_diag[block_rel.reshape(-1)], ((0, 0), (0, WIDE - width)))
    back, negs_back = pl.pallas_call(
        grad_kernel,
        out_shape=(shaped(*packed), shaped(columns * 16, LANES)),
        in_specs=[VMEM] * 5,
        out_specs=(VMEM, VMEM),
        scratch_shapes=[
            scratch(owners * slots, WIDE),
            scratch(2 * columns, WIDE),
            scratch(ends.shape[0], WIDE),
        ],
        name="grad",
    )(ends[:, None], ends[None, :], relation, got, negs.reshape(columns * 16, LANES))
    own_grad = lax.all_to_all(
        negs_back.reshape(columns, 16, LANES), "bucket", split_axis=0, concat_axis=0, tiled=True
    )
    returned = lax.all_to_all(back, "dom", split_axis=0, concat_axis=0, tiled=True)
    return pl.pallas_call(
        put_kernel,
        out_shape=shaped(entities, width),
        in_specs=[SMEM, VMEM, VMEM, VMEM],
        out_specs=VMEM,
        scratch_shapes=[scratch(owners * slots, WIDE)],
        name="put",
    )(own_rows, send[None, :], returned, own_grad)


def solution(mesh):
    placed = (
        P(("dom", "bucket"), None),
        P(),
        P("dom", "bucket", None, None),
        P("dom", "bucket", None),
        P("dom", "bucket", None),
        P("dom", "bucket", None, None),
        P("dom", "bucket", None),
    )
    return jax.shard_map(
        on_device, mesh=mesh, in_specs=placed, out_specs=P(("dom", "bucket"), None), check_vma=False
    )
```

time: 150 us -> 148 us (0.987)
  blocking collectives: 0 us -> 63.7 us
  waiting for transfers between devices: 76.5 us -> 43.9 us
  starting transfers between devices: 44.9 us -> 15.3 us
  other arithmetic: 14.3 us -> 0.02 us
  Pallas kernels: 0 us -> 11.8 us
  matrix products: 2.25 us -> 0 us
  local copies, waits for them, and re-layouts: 11.4 us -> 12.9 us
    all_to_all x0 -> x2, blocking collectives: none -> 63.7 us  [the longest x1 40.2 us: on_device(): lax.all_to_all(jnp.broadcast_to(own_negs, (columns, 16, LANES)), 'bucket'...]
    all_to_all x4 -> x2, waiting for transfers between devices: 76.5 us -> 43.9 us  [the longest x1 23.3 us: on_device(): lax.all_to_all(back, 'dom', split_axis=0, concat_axis=0, tiled=True)]
    all_to_all x4 -> x2, starting transfers between devices: 44.9 us -> 15.3 us  [the longest x1 10.8 us: on_device(): got = lax.all_to_all(picked, 'dom', split_axis=0, concat_axis=0, tiled=True)]
    scatter-add x4 -> x0, other arithmetic: 11.9 us -> none  [the longest x1 4.24 us: on_device(): slot_grads = slot_grads.at[target_idx].add(dst_grad.reshape(-1, width))]
    pallas_call x0 -> x3, Pallas kernels: none -> 11.8 us  [the longest x1 6.3 us: on_device(): pl.pallas_call(grad_kernel, out_shape=(shaped(*packed), shaped(columns *...]
    gather x9 -> x1, local copies, waits for them, and re-layouts: 5.1 us -> 0.56 us  [on_device(): rel_diag[block_rel.reshape(-1)]]
    unnamed x14 -> x18, local copies, waits for them, and re-layouts: 2.63 us -> 5.2 us
    dot_general x3 -> x0, matrix products: 2.25 us -> none  [the longest x1 1.16 us: block_grads(): scores = jnp.einsum('cek,cjk->cej', query, negatives, precision=highest)]
  transfers between devices with their start and end apart: 4 -> 2, of which waited for: 4 -> 2; matrix products, arithmetic and copies ran while one was open for 8% -> 2% of each run, Pallas kernels for 0% -> 0%
where the time goes in v2:
time: 148 us
  blocking collectives  63.7 us (43%)
  waiting for transfers between devices  43.9 us (30%)
  starting transfers between devices  15.3 us (10%)
  local copies, waits for them, and re-layouts  12.9 us (9%)
  Pallas kernels  11.8 us (8%)
    all_to_all x1, blocking collectives, on_device(): lax.all_to_all(jnp.broadcast_to(own_negs, (columns, 16, LANES)), 'bucket'...  40.2 us
    all_to_all x1, blocking collectives, on_device(): lax.all_to_all(negs_back.reshape(columns, 16, LANES), 'bucket', split_axi...  23.5 us
    all_to_all x1, waiting for transfers between devices, on_device(): lax.all_to_all(back, 'dom', split_axis=0, concat_axis=0, tiled=True)  23.3 us
    all_to_all x1, waiting for transfers between devices, on_device(): got = lax.all_to_all(picked, 'dom', split_axis=0, concat_axis=0, tiled=True)  20.6 us
    all_to_all x1, starting transfers between devices, on_device(): got = lax.all_to_all(picked, 'dom', split_axis=0, concat_axis=0, tiled=True)  10.8 us
    pallas_call x1, Pallas kernels, on_device(): pl.pallas_call(grad_kernel, out_shape=(shaped(*packed), shaped(columns *...  6.3 us
    unnamed x18, local copies, waits for them, and re-layouts  5.2 us
    all_to_all x1, starting transfers between devices, on_device(): lax.all_to_all(back, 'dom', split_axis=0, concat_axis=0, tiled=True)  4.52 us
  transfers between devices with their start and end apart: 2, of which 2 were waited for; matrix products, arithmetic and copies ran while one was open for 2% of the time, Pallas kernels for 0%

profile of v2, /device:TPU:1, one launch (start us, length us, event | category | flops | bytes accessed | tf_op | source)
XLA Modules:
  0.0 147.7 jit_solution(9175621809818672597)
XLA Ops:
  0.0 1.3 reshape.46.neg_ref
  1.3 2.0 %copy.13.table_ref = f32[256,400]{1,0:T(8,128)} copy(f32[256,400]{0,1:T(8,128)} %param.7) | data formatting | bytes 819200 | tf_op args[0]
  3.4 0.0 copy-done.3
  3.4 1.0 broadcast_in_dim_reshape.8.send_ref
  4.3 2.8 %pick.1 = (f32[16,104,128]{2,1,0:T(8,128)}, f32[16,128]{1,0:T(8,128)}) custom-call(s32[4]{0:T(128)} %reshape.46.neg_ref, s32[512,1]{1,0:T(8,128)} %broadcast_in_dim_reshape.8.send_ref, f32[256,400]{1,0:T(8,128)} %copy.13.table_ref), custom_call_target="tpu_custom_call" | custom-call | tf_op jit(solution)/shard_map/pick/pallas_call | solution.py:155
  7.1 0.7 broadcast_in_dim.12
  7.8 40.2 %all_to_all.20 = f32[64,16,128]{2,1,0:T(8,128)} all-to-all(f32[64,16,128]{2,1,0:T(8,128)S(1)} %broadcast_in_dim.12), channel_id=1, replica_groups=mesh['dom'=16,'bucket'=64] {'bucket'}, dimensions={0} | all-to-all | bytes 1048576 | tf_op jit(solution)/shard_map/all_to_all | solution.py:163
  48.1 0.0 copy-start.6
  48.1 0.0 copy-start.2
  48.1 10.8 %all-to-all-start = ((f32[16,104,128]{2,1,0:T(8,128)}), f32[16,104,128]{2,1,0:T(8,128)S(1)}, u32[]{:S(2)}, u32[]{:S(2)}) async-start(f32[16,104,128]{2,1,0:T(8,128)} %get-tuple-element.9), calls=%async_computation | async-start | bytes 1703936 | tf_op jit(solution)/shard_map/all_to_all | solution.py:166
  58.9 0.0 copy-start.5
  58.9 0.0 copy-done.6
  58.9 0.7 copy-done.5
  59.5 0.0 copy-start.4
  59.5 0.9 copy.14.col_ref
  60.4 0.0 copy-done.4
  60.4 0.0 copy-done.2
  60.4 0.0 copy-start.7
  60.4 0.2 copy.11
  60.6 0.5 copy-done.7
  61.1 0.6 gather_fusion
  61.6 0.6 pad.4.rel_ref
  62.2 20.6 %all-to-all-done.got_ref = f32[16,104,128]{2,1,0:T(8,128)S(1)} async-done(((f32[16,104,128]{2,1,0:T(8,128)}), f32[16,104,128]{2,1,0:T(8,128)S(1)}, u32[]{:S(2)}, u32[]{:S(2)}) %all-to-all-start) | async-done | bytes 852000 | tf_op jit(solution)/shard_map/all_to_all | solution.py:166
  82.8 0.9 copy-done.1
  83.8 6.3 %grad.1 = (f32[16,104,128]{2,1,0:T(8,128)}, f32[1024,128]{1,0:T(8,128)}) custom-call(s32[512,1]{1,0:T(8,128)} %copy.14.col_ref, s32[1,512]{1,0:T(1,128)} %bitcast.17, f32[2,512]{1,0:T(2,128)} %pad.4.rel_ref, f32[16,104,128]{2,1,0:T(8,128)} %copy-done.1, f32[1024,128]{1,0:T(8,128)} %bitcast.14), custom_call_target="tpu_custom_call" | custom-call | tf_op jit(solution)/shard_map/grad/pallas_call | solution.py:169
  90.1 23.5 %all_to_all.21.negs_ref = f32[64,16,128]{2,1,0:T(8,128)} all-to-all(f32[64,16,128]{2,1,0:T(8,128)} %bitcast.15), channel_id=1, replica_groups=mesh['dom'=16,'bucket'=64] {'bucket'}, dimensions={0} | all-to-all | bytes 1048576 | tf_op jit(solution)/shard_map/all_to_all | solution.py:181
  113.6 4.5 %all-to-all-start.2 = ((f32[16,104,128]{2,1,0:T(8,128)}), f32[16,104,128]{2,1,0:T(8,128)S(1)}, u32[]{:S(2)}, u32[]{:S(2)}) async-start(f32[16,104,128]{2,1,0:T(8,128)} %get-tuple-element.11), calls=%async_computation.2 | async-start | bytes 1703936 | tf_op jit(solution)/shard_map/all_to_all | solution.py:184
  118.1 0.7 broadcast_in_dim_reshape.6.send_ref
  118.8 23.3 %all-to-all-done.2.got_ref = f32[16,104,128]{2,1,0:T(8,128)S(1)} async-done(((f32[16,104,128]{2,1,0:T(8,128)}), f32[16,104,128]{2,1,0:T(8,128)S(1)}, u32[]{:S(2)}, u32[]{:S(2)}) %all-to-all-start.2) | async-done | bytes 852000 | tf_op jit(solution)/shard_map/all_to_all | solution.py:184
  142.1 0.9 copy-done
  143.0 2.7 %put.1 = f32[256,400]{1,0:T(8,128)} custom-call(s32[4]{0:T(128)} %reshape.46.neg_ref, s32[1,512]{1,0:T(1,128)} %broadcast_in_dim_reshape.6.send_ref, f32[16,104,128]{2,1,0:T(8,128)} %copy-done, f32[64,16,128]{2,1,0:T(8,128)} %all_to_all.21.negs_ref), custom_call_target="tpu_custom_call" | custom-call | tf_op jit(solution)/shard_map/put/pallas_call | solution.py:185
  145.8 2.0 %copy.15 = f32[256,400]{0,1:T(8,128)} copy(f32[256,400]{1,0:T(8,128)} %put.1) | data formatting | bytes 819200 | tf_op jit(solution)/shard_map/put/pallas_call | solution.py:185
  (6 shorter events, 0.0 us)
Async XLA Ops:
  1.3 2.0 %copy-start.3 = (s32[1,1,16,32]{3,2,1,0:T(8,128)S(1)}, s32[1,1,16,32]{3,2,1,0:T(8,128)}, u32[]{:S(2)}) copy-start(s32[1,1,16,32]{3,2,1,0:T(8,128)} %param.9) | copy-start | bytes 6148
  48.1 10.8 %copy-start.6 = (s32[1,1,256]{2,1,0:T(1,128)S(1)}, s32[1,1,256]{2,1,0:T(1,128)}, u32[]{:S(2)}) copy-start(s32[1,1,256]{2,1,0:T(1,128)} %param.10) | copy-start | bytes 3076
  48.1 12.4 %copy-start.2 = (f32[256,400]{0,1:T(8,128)S(1)}, f32[256,400]{0,1:T(8,128)}, u32[]{:S(2)}) copy-start(f32[256,400]{0,1:T(8,128)} %param.8) | copy-start | bytes 1228804
  48.1 34.8 %all-to-all-start = ((f32[16,104,128]{2,1,0:T(8,128)}), f32[16,104,128]{2,1,0:T(8,128)S(1)}, u32[]{:S(2)}, u32[]{:S(2)}) async-start(f32[16,104,128]{2,1,0:T(8,128)} %get-tuple-element.9), calls=%async_computation | async-start | bytes 1703936 | tf_op jit(solution)/shard_map/all_to_all | solution.py:166
  58.9 0.7 copy-start.5
  59.5 0.9 copy-start.4
  60.4 0.7 copy-start.7
  82.8 0.9 copy-start.1
  113.6 28.5 %all-to-all-start.2 = ((f32[16,104,128]{2,1,0:T(8,128)}), f32[16,104,128]{2,1,0:T(8,128)S(1)}, u32[]{:S(2)}, u32[]{:S(2)}) async-start(f32[16,104,128]{2,1,0:T(8,128)} %get-tuple-element.11), calls=%async_computation.2 | async-start | bytes 1703936 | tf_op jit(solution)/shard_map/all_to_all | solution.py:184
  142.1 0.9 copy-start

commit v3 on v2

--- a/solution.py
+++ b/solution.py
@@ -127,7 +127,7 @@
     unpack(got_ref, rows)
     entities, width = out_ref.shape
     result = select_rows(onehot_of(send_ref[...], (entities, rows.shape[0]), 0), rows[...], 2)
-    own = jnp.sum(negs_ref[...], axis=0)
+    own = negs_ref[...]
     place = lax.broadcasted_iota(jnp.int32, (entities, LANES), 0)
     for j in range(CHUNKS):
         part = result[:, j * LANES : (j + 1) * LANES]
@@ -143,6 +143,44 @@
 
 def scratch(*shape):
     return pltpu.VMEM(shape, jnp.float32)
+
+
+def digits(columns):
+    side = 1
+    while side * side < columns:
+        side *= 2
+    def both(b, s):
+        return b ^ ((s & 1) | ((s >> 1) * side))
+
+    def along_z(b, s):
+        y, z = divmod(b, side)
+        return y * side + (z + 2 * s) % side
+
+    def along_y(b, s):
+        y, z = divmod(b, side)
+        return ((y + 2 * s) % (columns // side)) * side + z
+
+    return along_z, along_y, both
+
+
+def fetch(x, turn, step, columns):
+    return lax.ppermute(x, "bucket", [(turn(b, step), b) for b in range(columns)])
+
+
+def hand(x, turn, step, columns):
+    return lax.ppermute(x, "bucket", [(b, turn(b, step)) for b in range(columns)])
+
+
+def gather_columns(x, columns):
+    for turn in digits(columns):
+        x = jnp.stack([x] + [fetch(x, turn, step, columns) for step in range(1, 4)])
+    return x
+
+
+def sum_columns(x, columns):
+    for turn in reversed(digits(columns)):
+        x = x[0] + sum(hand(x[step], turn, step, columns) for step in range(1, 4))
+    return x
 
 
 def on_device(emb_table, rel_diag, send_rows, src_slot, dst_slot, neg_rows, block_rel):
@@ -160,9 +198,7 @@
         scratch_shapes=[scratch(entities, WIDE)],
         name="pick",
     )(own_rows, send[:, None], emb_table)
-    negs = lax.all_to_all(
-        jnp.broadcast_to(own_negs, (columns, 16, LANES)), "bucket", split_axis=0, concat_axis=0, tiled=True
-    )
+    negs = gather_columns(own_negs, columns)
     got = lax.all_to_all(picked, "dom", split_axis=0, concat_axis=0, tiled=True)
     ends = jnp.concatenate([src_slot.reshape(-1), dst_slot.reshape(-1)])
     relation = jnp.pad(rel_diag[block_rel.reshape(-1)], ((0, 0), (0, WIDE - width)))
@@ -178,9 +214,7 @@
         ],
         name="grad",
     )(ends[:, None], ends[None, :], relation, got, negs.reshape(columns * 16, LANES))
-    own_grad = lax.all_to_all(
-        negs_back.reshape(columns, 16, LANES), "bucket", split_axis=0, concat_axis=0, tiled=True
-    )
+    own_grad = sum_columns(negs_back.reshape(4, 4, 4, 16, LANES), columns)
     returned = lax.all_to_all(back, "dom", split_axis=0, concat_axis=0, tiled=True)
     return pl.pallas_call(
         put_kernel,

time: 148 us -> 143 us (0.966)
  the two profiles are of different devices: /device:TPU:1 before, /device:TPU:2 now
where the time goes in v3:
time: 143 us; the launch traced here: 142 us
  starting transfers between devices  102 us (71%)
  waiting for transfers between devices  15.6 us (11%)
  local copies, waits for them, and re-layouts  11.8 us (8%)
  Pallas kernels  11.7 us (8%)
  other arithmetic  1.53 us (1%)
    ppermute x9, starting transfers between devices, hand(): lax.ppermute(x, 'bucket', [(b, turn(b, step)) for b in range(columns)])  39.2 us
    ppermute x9, starting transfers between devices, fetch(): lax.ppermute(x, 'bucket', [(turn(b, step), b) for b in range(columns)])  38.3 us
    all_to_all x1, starting transfers between devices, on_device(): got = lax.all_to_all(picked, 'dom', split_axis=0, concat_axis=0, tiled=True)  16.7 us
    ppermute x9, waiting for transfers between devices, fetch(): lax.ppermute(x, 'bucket', [(turn(b, step), b) for b in range(columns)])  9.48 us
    all_to_all x1, starting transfers between devices, on_device(): lax.all_to_all(back, 'dom', split_axis=0, concat_axis=0, tiled=True)  7.36 us
    pallas_call x1, Pallas kernels, on_device(): pl.pallas_call(grad_kernel, out_shape=(shaped(*packed), shaped(columns *...  6.3 us
    ppermute x9, waiting for transfers between devices, hand(): lax.ppermute(x, 'bucket', [(b, turn(b, step)) for b in range(columns)])  6.08 us
    unnamed x22, local copies, waits for them, and re-layouts  4.76 us
  transfers between devices with their start and end apart: 20, of which 9 were waited for; matrix products, arithmetic and copies ran while one was open for 3% of the time, Pallas kernels for 0%

profile of v3, /device:TPU:2, one launch (start us, length us, event | category | flops | bytes accessed | tf_op | source)
XLA Modules:
  0.0 142.4 jit_solution(17773325563293325979)
XLA Ops:
  0.0 1.3 reshape.52.neg_ref
  1.3 2.0 %copy.13.table_ref = f32[256,400]{1,0:T(8,128)} copy(f32[256,400]{0,1:T(8,128)} %param.7) | data formatting | bytes 819200 | tf_op args[0]
  4.4 2.8 %pick.1 = (f32[16,104,128]{2,1,0:T(8,128)}, f32[16,128]{1,0:T(8,128)}) custom-call(s32[4]{0:T(128)} %reshape.52.neg_ref, s32[512,1]{1,0:T(8,128)} %broadcast_in_dim_reshape.8.send_ref, f32[256,400]{1,0:T(8,128)} %copy.13.table_ref), custom_call_target="tpu_custom_call" | custom-call | tf_op jit(solution)/shard_map/pick/pallas_call | solution.py:193
  7.2 16.7 %all-to-all-start = ((f32[16,104,128]{2,1,0:T(8,128)}), f32[16,104,128]{2,1,0:T(8,128)S(1)}, u32[]{:S(2)}, u32[]{:S(2)}) async-start(f32[16,104,128]{2,1,0:T(8,128)} %get-tuple-element.9), calls=%async_computation | async-start | bytes 1703936 | tf_op jit(solution)/shard_map/all_to_all | solution.py:202
  23.9 7.2 %collective-permute-start = (f32[16,128]{1,0:T(8,128)S(1)}, f32[16,128]{1,0:T(8,128)S(1)}, u32[]{:S(2)}, u32[]{:S(2)}) collective-permute-start(f32[16,128]{1,0:T(8,128)S(1)} %copy-done.6), channel_id=1, source_target_pairs={{2,0},{3,1},{4,2},{5,3},{6,4},{7,5},{0,6},{1,7},{10,8},{11,9},{12,... | collective-permute-start | bytes 24584 | tf_op jit(solution)/shard_map/ppermute | solution.py:167
  31.1 1.9 %collective-permute-start.1 = (f32[16,128]{1,0:T(8,128)S(1)}, f32[16,128]{1,0:T(8,128)S(1)}, u32[]{:S(2)}, u32[]{:S(2)}) collective-permute-start(f32[16,128]{1,0:T(8,128)S(1)} %copy-done.6), channel_id=1, source_target_pairs={{4,0},{5,1},{6,2},{7,3},{0,4},{1,5},{2,6},{3,7},{12,8},{13,9},{14,... | collective-permute-start | bytes 24584 | tf_op jit(solution)/shard_map/ppermute | solution.py:167
  33.1 4.3 %collective-permute-start.2 = (f32[16,128]{1,0:T(8,128)S(1)}, f32[16,128]{1,0:T(8,128)S(1)}, u32[]{:S(2)}, u32[]{:S(2)}) collective-permute-start(f32[16,128]{1,0:T(8,128)S(1)} %copy-done.6), channel_id=1, source_target_pairs={{6,0},{7,1},{0,2},{1,3},{2,4},{3,5},{4,6},{5,7},{14,8},{15,9},{8,1... | collective-permute-start | bytes 24584 | tf_op jit(solution)/shard_map/ppermute | solution.py:167
  37.4 3.3 %collective-permute-done.1 = f32[16,128]{1,0:T(8,128)S(1)} collective-permute-done((f32[16,128]{1,0:T(8,128)S(1)}, f32[16,128]{1,0:T(8,128)S(1)}, u32[]{:S(2)}, u32[]{:S(2)}) %collective-permute-start.1) | collective-permute-done | bytes 8224 | tf_op jit(solution)/shard_map/ppermute | solution.py:167
  40.7 6.8 %collective-permute-start.3 = (f32[4,16,128]{2,1,0:T(8,128)S(1)}, f32[4,16,128]{2,1,0:T(8,128)S(1)}, u32[]{:S(2)}, u32[]{:S(2)}) collective-permute-start(f32[4,16,128]{2,1,0:T(8,128)S(1)} %get-tuple-element.26), channel_id=1, source_target_pairs={{16,0},{17,1},{18,2},{19,3},{20,4},{21,5},{22,6},{23,7},{24,8},{25... | collective-permute-start | bytes 98312 | tf_op jit(solution)/shard_map/ppermute | solution.py:167
  47.6 3.4 %collective-permute-start.4 = (f32[4,16,128]{2,1,0:T(8,128)S(1)}, f32[4,16,128]{2,1,0:T(8,128)S(1)}, u32[]{:S(2)}, u32[]{:S(2)}) collective-permute-start(f32[4,16,128]{2,1,0:T(8,128)S(1)} %get-tuple-element.26), channel_id=1, source_target_pairs={{32,0},{33,1},{34,2},{35,3},{36,4},{37,5},{38,6},{39,7},{40,8},{41... | collective-permute-start | bytes 98312 | tf_op jit(solution)/shard_map/ppermute | solution.py:167
  50.9 4.7 %collective-permute-start.5 = (f32[4,16,128]{2,1,0:T(8,128)S(1)}, f32[4,16,128]{2,1,0:T(8,128)S(1)}, u32[]{:S(2)}, u32[]{:S(2)}) collective-permute-start(f32[4,16,128]{2,1,0:T(8,128)S(1)} %get-tuple-element.26), channel_id=1, source_target_pairs={{48,0},{49,1},{50,2},{51,3},{52,4},{53,5},{54,6},{55,7},{56,8},{57... | collective-permute-start | bytes 98312 | tf_op jit(solution)/shard_map/ppermute | solution.py:167
  55.7 1.6 %collective-permute-done.4 = f32[4,16,128]{2,1,0:T(8,128)S(1)} collective-permute-done((f32[4,16,128]{2,1,0:T(8,128)S(1)}, f32[4,16,128]{2,1,0:T(8,128)S(1)}, u32[]{:S(2)}, u32[]{:S(2)}) %collective-permute-start.4) | collective-permute-done | bytes 32800 | tf_op jit(solution)/shard_map/ppermute | solution.py:167
  57.3 1.6 %collective-permute-done.5 = f32[4,16,128]{2,1,0:T(8,128)S(1)} collective-permute-done((f32[4,16,128]{2,1,0:T(8,128)S(1)}, f32[4,16,128]{2,1,0:T(8,128)S(1)}, u32[]{:S(2)}, u32[]{:S(2)}) %collective-permute-start.5) | collective-permute-done | bytes 32800 | tf_op jit(solution)/shard_map/ppermute | solution.py:167
  58.9 4.3 %collective-permute-start.6 = (f32[4,4,16,128]{3,2,1,0:T(8,128)S(1)}, f32[4,4,16,128]{3,2,1,0:T(8,128)S(1)}, u32[]{:S(2)}, u32[]{:S(2)}) collective-permute-start(f32[4,4,16,128]{3,2,1,0:T(8,128)S(1)} %get-tuple-element.21), channel_id=1, source_target_pairs={{1,0},{0,1},{3,2},{2,3},{5,4},{4,5},{7,6},{6,7},{9,8},{8,9},{11,10... | collective-permute-start | bytes 393224 | tf_op jit(solution)/shard_map/ppermute | solution.py:167
  63.2 3.7 %collective-permute-start.7 = (f32[4,4,16,128]{3,2,1,0:T(8,128)S(1)}, f32[4,4,16,128]{3,2,1,0:T(8,128)S(1)}, u32[]{:S(2)}, u32[]{:S(2)}) collective-permute-start(f32[4,4,16,128]{3,2,1,0:T(8,128)S(1)} %get-tuple-element.21), channel_id=1, source_target_pairs={{8,0},{9,1},{10,2},{11,3},{12,4},{13,5},{14,6},{15,7},{0,8},{1,9},... | collective-permute-start | bytes 393224 | tf_op jit(solution)/shard_map/ppermute | solution.py:167
  67.0 1.9 %collective-permute-start.8 = (f32[4,4,16,128]{3,2,1,0:T(8,128)S(1)}, f32[4,4,16,128]{3,2,1,0:T(8,128)S(1)}, u32[]{:S(2)}, u32[]{:S(2)}) collective-permute-start(f32[4,4,16,128]{3,2,1,0:T(8,128)S(1)} %get-tuple-element.21), channel_id=1, source_target_pairs={{9,0},{8,1},{11,2},{10,3},{13,4},{12,5},{15,6},{14,7},{1,8},{0,9},... | collective-permute-start | bytes 393224 | tf_op jit(solution)/shard_map/ppermute | solution.py:167
  71.8 2.9 %collective-permute-done.8 = f32[4,4,16,128]{3,2,1,0:T(8,128)S(1)} collective-permute-done((f32[4,4,16,128]{3,2,1,0:T(8,128)S(1)}, f32[4,4,16,128]{3,2,1,0:T(8,128)S(1)}, u32[]{:S(2)}, u32[]{:S(2)}) %collective-permute-start.8) | collective-permute-done | bytes 131104 | tf_op jit(solution)/shard_map/ppermute | solution.py:167
  76.5 6.3 %grad.1 = (f32[16,104,128]{2,1,0:T(8,128)}, f32[1024,128]{1,0:T(8,128)}) custom-call(s32[512,1]{1,0:T(8,128)} %copy.14.col_ref, s32[1,512]{1,0:T(1,128)} %bitcast.63, f32[2,512]{1,0:T(2,128)} %pad.4.rel_ref, f32[16,104,128]{2,1,0:T(8,128)} %copy-done.1, f32[1024,128]{1,0:T(8,128)} %bitcast.51), custom_call_target="tpu_custom_call" | custom-call | tf_op jit(solution)/shard_map/grad/pallas_call | solution.py:205
  82.8 7.4 %all-to-all-start.1 = ((f32[16,104,128]{2,1,0:T(8,128)}), f32[16,104,128]{2,1,0:T(8,128)S(1)}, u32[]{:S(2)}, u32[]{:S(2)}) async-start(f32[16,104,128]{2,1,0:T(8,128)} %get-tuple-element.11), calls=%async_computation.1 | async-start | bytes 1703936 | tf_op jit(solution)/shard_map/all_to_all | solution.py:218
  90.2 2.1 %collective-permute-start.10 = (f32[4,4,16,128]{3,2,1,0:T(8,128)S(1)}, f32[4,4,16,128]{3,2,1,0:T(8,128)S(1)}, u32[]{:S(2)}, u32[]{:S(2)}) collective-permute-start(f32[4,4,16,128]{3,2,1,0:T(8,128)S(1)} %bitcast.58), channel_id=1, source_target_pairs={{0,8},{1,9},{2,10},{3,11},{4,12},{5,13},{6,14},{7,15},{8,0},{9,1},... | collective-permute-start | bytes 393224 | tf_op jit(solution)/shard_map/ppermute | solution.py:171
  92.3 3.1 %collective-permute-start.11 = (f32[4,4,16,128]{3,2,1,0:T(8,128)S(1)}, f32[4,4,16,128]{3,2,1,0:T(8,128)S(1)}, u32[]{:S(2)}, u32[]{:S(2)}) collective-permute-start(f32[4,4,16,128]{3,2,1,0:T(8,128)S(1)} %bitcast.57), channel_id=1, source_target_pairs={{0,9},{1,8},{2,11},{3,10},{4,13},{5,12},{6,15},{7,14},{8,1},{9,0},... | collective-permute-start | bytes 393224 | tf_op jit(solution)/shard_map/ppermute | solution.py:171
  95.5 3.9 %collective-permute-start.9 = (f32[4,4,16,128]{3,2,1,0:T(8,128)S(1)}, f32[4,4,16,128]{3,2,1,0:T(8,128)S(1)}, u32[]{:S(2)}, u32[]{:S(2)}) collective-permute-start(f32[4,4,16,128]{3,2,1,0:T(8,128)S(1)} %bitcast.56), channel_id=1, source_target_pairs={{0,1},{1,0},{2,3},{3,2},{4,5},{5,4},{6,7},{7,6},{8,9},{9,8},{10,11... | collective-permute-start | bytes 393224 | tf_op jit(solution)/shard_map/ppermute | solution.py:171
  100.5 2.7 %collective-permute-done.9 = f32[4,4,16,128]{3,2,1,0:T(8,128)S(1)} collective-permute-done((f32[4,4,16,128]{3,2,1,0:T(8,128)S(1)}, f32[4,4,16,128]{3,2,1,0:T(8,128)S(1)}, u32[]{:S(2)}, u32[]{:S(2)}) %collective-permute-start.9) | collective-permute-done | bytes 131104 | tf_op jit(solution)/shard_map/ppermute | solution.py:171
  103.3 3.4 %collective-permute-start.12 = (f32[4,16,128]{2,1,0:T(8,128)S(1)}, f32[4,16,128]{2,1,0:T(8,128)S(1)}, u32[]{:S(2)}, u32[]{:S(2)}) collective-permute-start(f32[4,16,128]{2,1,0:T(8,128)S(1)} %get-tuple-element.19), channel_id=1, source_target_pairs={{0,16},{1,17},{2,18},{3,19},{4,20},{5,21},{6,22},{7,23},{8,24},{9,... | collective-permute-start | bytes 98312 | tf_op jit(solution)/shard_map/ppermute | solution.py:171
  106.7 4.8 %collective-permute-start.13 = (f32[4,16,128]{2,1,0:T(8,128)S(1)}, f32[4,16,128]{2,1,0:T(8,128)S(1)}, u32[]{:S(2)}, u32[]{:S(2)}) collective-permute-start(f32[4,16,128]{2,1,0:T(8,128)S(1)} %get-tuple-element.17), channel_id=1, source_target_pairs={{0,32},{1,33},{2,34},{3,35},{4,36},{5,37},{6,38},{7,39},{8,40},{9,... | collective-permute-start | bytes 98312 | tf_op jit(solution)/shard_map/ppermute | solution.py:171
  111.5 6.0 %collective-permute-start.14 = (f32[4,16,128]{2,1,0:T(8,128)S(1)}, f32[4,16,128]{2,1,0:T(8,128)S(1)}, u32[]{:S(2)}, u32[]{:S(2)}) collective-permute-start(f32[4,16,128]{2,1,0:T(8,128)S(1)} %get-tuple-element.18), channel_id=1, source_target_pairs={{0,48},{1,49},{2,50},{3,51},{4,52},{5,53},{6,54},{7,55},{8,56},{9,... | collective-permute-start | bytes 98312 | tf_op jit(solution)/shard_map/ppermute | solution.py:171
  117.6 1.6 %collective-permute-done.14 = f32[4,16,128]{2,1,0:T(8,128)S(1)} collective-permute-done((f32[4,16,128]{2,1,0:T(8,128)S(1)}, f32[4,16,128]{2,1,0:T(8,128)S(1)}, u32[]{:S(2)}, u32[]{:S(2)}) %collective-permute-start.14) | collective-permute-done | bytes 32800 | tf_op jit(solution)/shard_map/ppermute | solution.py:171
  119.2 4.0 %collective-permute-start.15 = (f32[16,128]{1,0:T(8,128)S(1)}, f32[16,128]{1,0:T(8,128)S(1)}, u32[]{:S(2)}, u32[]{:S(2)}) collective-permute-start(f32[16,128]{1,0:T(8,128)S(1)} %get-tuple-element.24), channel_id=1, source_target_pairs={{0,2},{1,3},{2,4},{3,5},{4,6},{5,7},{6,0},{7,1},{8,10},{9,11},{10,... | collective-permute-start | bytes 24584 | tf_op jit(solution)/shard_map/ppermute | solution.py:171
  123.2 5.7 %collective-permute-start.16 = (f32[16,128]{1,0:T(8,128)S(1)}, f32[16,128]{1,0:T(8,128)S(1)}, u32[]{:S(2)}, u32[]{:S(2)}) collective-permute-start(f32[16,128]{1,0:T(8,128)S(1)} %get-tuple-element.22), channel_id=1, source_target_pairs={{0,4},{1,5},{2,6},{3,7},{4,0},{5,1},{6,2},{7,3},{8,12},{9,13},{10,... | collective-permute-start | bytes 24584 | tf_op jit(solution)/shard_map/ppermute | solution.py:171
  128.9 6.0 %collective-permute-start.17 = (f32[16,128]{1,0:T(8,128)S(1)}, f32[16,128]{1,0:T(8,128)S(1)}, u32[]{:S(2)}, u32[]{:S(2)}) collective-permute-start(f32[16,128]{1,0:T(8,128)S(1)} %get-tuple-element.23), channel_id=1, source_target_pairs={{0,6},{1,7},{2,0},{3,1},{4,2},{5,3},{6,4},{7,5},{8,14},{9,15},{10,... | collective-permute-start | bytes 24584 | tf_op jit(solution)/shard_map/ppermute | solution.py:171
  137.8 2.6 %put.1 = f32[256,400]{1,0:T(8,128)} custom-call(s32[4]{0:T(128)} %reshape.52.neg_ref, s32[1,512]{1,0:T(1,128)} %broadcast_in_dim_reshape.6.send_ref, f32[16,104,128]{2,1,0:T(8,128)} %copy-done, f32[16,128]{1,0:T(8,128)} %fusion.1.negs_ref), custom_call_target="tpu_custom_call" | custom-call | tf_op jit(solution)/shard_map/put/pallas_call | solution.py:219
  140.4 2.0 %copy.15 = f32[256,400]{0,1:T(8,128)} copy(f32[256,400]{1,0:T(8,128)} %put.1) | data formatting | bytes 819200 | tf_op jit(solution)/shard_map/put/pallas_call | solution.py:219
  (52 shorter events, 9.8 us)
Async XLA Ops:
  1.3 2.0 %copy-start.4 = (s32[1,1,16,32]{3,2,1,0:T(8,128)S(1)}, s32[1,1,16,32]{3,2,1,0:T(8,128)}, u32[]{:S(2)}) copy-start(s32[1,1,16,32]{3,2,1,0:T(8,128)} %param.9) | copy-start | bytes 6148
  7.1 16.7 %copy-start.6 = (f32[16,128]{1,0:T(8,128)S(1)}, f32[16,128]{1,0:T(8,128)}, u32[]{:S(2)}) copy-start(f32[16,128]{1,0:T(8,128)} %get-tuple-element.10) | copy-start | bytes 24580
  7.1 48.5 %copy-start.9 = (s32[1,1,2]{2,1,0:T(1,128)S(1)}, s32[1,1,2]{2,1,0:T(1,128)}, u32[]{:S(2)}) copy-start(s32[1,1,2]{2,1,0:T(1,128)} %param.13) | copy-start | bytes 28
  7.2 68.4 %all-to-all-start = ((f32[16,104,128]{2,1,0:T(8,128)}), f32[16,104,128]{2,1,0:T(8,128)S(1)}, u32[]{:S(2)}, u32[]{:S(2)}) async-start(f32[16,104,128]{2,1,0:T(8,128)} %get-tuple-element.9), calls=%async_computation | async-start | bytes 1703936 | tf_op jit(solution)/shard_map/all_to_all | solution.py:202
  23.9 46.6 %copy-start.3 = (f32[256,400]{0,1:T(8,128)S(1)}, f32[256,400]{0,1:T(8,128)}, u32[]{:S(2)}) copy-start(f32[256,400]{0,1:T(8,128)} %param.8) | copy-start | bytes 1228804
  23.9 13.5 %collective-permute-start = (f32[16,128]{1,0:T(8,128)S(1)}, f32[16,128]{1,0:T(8,128)S(1)}, u32[]{:S(2)}, u32[]{:S(2)}) collective-permute-start(f32[16,128]{1,0:T(8,128)S(1)} %copy-done.6), channel_id=1, source_target_pairs={{2,0},{3,1},{4,2},{5,3},{6,4},{7,5},{0,6},{1,7},{10,8},{11,9},{12,... | collective-permute-start | bytes 24584 | tf_op jit(solution)/shard_map/ppermute | solution.py:167
  31.1 9.5 %collective-permute-start.1 = (f32[16,128]{1,0:T(8,128)S(1)}, f32[16,128]{1,0:T(8,128)S(1)}, u32[]{:S(2)}, u32[]{:S(2)}) collective-permute-start(f32[16,128]{1,0:T(8,128)S(1)} %copy-done.6), channel_id=1, source_target_pairs={{4,0},{5,1},{6,2},{7,3},{0,4},{1,5},{2,6},{3,7},{12,8},{13,9},{14,... | collective-permute-start | bytes 24584 | tf_op jit(solution)/shard_map/ppermute | solution.py:167
  33.1 7.7 %collective-permute-start.2 = (f32[16,128]{1,0:T(8,128)S(1)}, f32[16,128]{1,0:T(8,128)S(1)}, u32[]{:S(2)}, u32[]{:S(2)}) collective-permute-start(f32[16,128]{1,0:T(8,128)S(1)} %copy-done.6), channel_id=1, source_target_pairs={{6,0},{7,1},{0,2},{1,3},{2,4},{3,5},{4,6},{5,7},{14,8},{15,9},{8,1... | collective-permute-start | bytes 24584 | tf_op jit(solution)/shard_map/ppermute | solution.py:167
  40.7 15.0 %collective-permute-start.3 = (f32[4,16,128]{2,1,0:T(8,128)S(1)}, f32[4,16,128]{2,1,0:T(8,128)S(1)}, u32[]{:S(2)}, u32[]{:S(2)}) collective-permute-start(f32[4,16,128]{2,1,0:T(8,128)S(1)} %get-tuple-element.26), channel_id=1, source_target_pairs={{16,0},{17,1},{18,2},{19,3},{20,4},{21,5},{22,6},{23,7},{24,8},{25... | collective-permute-start | bytes 98312 | tf_op jit(solution)/shard_map/ppermute | solution.py:167
  47.6 9.7 %collective-permute-start.4 = (f32[4,16,128]{2,1,0:T(8,128)S(1)}, f32[4,16,128]{2,1,0:T(8,128)S(1)}, u32[]{:S(2)}, u32[]{:S(2)}) collective-permute-start(f32[4,16,128]{2,1,0:T(8,128)S(1)} %get-tuple-element.26), channel_id=1, source_target_pairs={{32,0},{33,1},{34,2},{35,3},{36,4},{37,5},{38,6},{39,7},{40,8},{41... | collective-permute-start | bytes 98312 | tf_op jit(solution)/shard_map/ppermute | solution.py:167
  50.9 8.0 %collective-permute-start.5 = (f32[4,16,128]{2,1,0:T(8,128)S(1)}, f32[4,16,128]{2,1,0:T(8,128)S(1)}, u32[]{:S(2)}, u32[]{:S(2)}) collective-permute-start(f32[4,16,128]{2,1,0:T(8,128)S(1)} %get-tuple-element.26), channel_id=1, source_target_pairs={{48,0},{49,1},{50,2},{51,3},{52,4},{53,5},{54,6},{55,7},{56,8},{57... | collective-permute-start | bytes 98312 | tf_op jit(solution)/shard_map/ppermute | solution.py:167
  58.9 10.0 %copy-start.8 = (s32[1,1,256]{2,1,0:T(1,128)S(1)}, s32[1,1,256]{2,1,0:T(1,128)}, u32[]{:S(2)}) copy-start(s32[1,1,256]{2,1,0:T(1,128)} %param.10) | copy-start | bytes 3076
  58.9 12.9 %collective-permute-start.6 = (f32[4,4,16,128]{3,2,1,0:T(8,128)S(1)}, f32[4,4,16,128]{3,2,1,0:T(8,128)S(1)}, u32[]{:S(2)}, u32[]{:S(2)}) collective-permute-start(f32[4,4,16,128]{3,2,1,0:T(8,128)S(1)} %get-tuple-element.21), channel_id=1, source_target_pairs={{1,0},{0,1},{3,2},{2,3},{5,4},{4,5},{7,6},{6,7},{9,8},{8,9},{11,10... | collective-permute-start | bytes 393224 | tf_op jit(solution)/shard_map/ppermute | solution.py:167
  63.2 8.6 %collective-permute-start.7 = (f32[4,4,16,128]{3,2,1,0:T(8,128)S(1)}, f32[4,4,16,128]{3,2,1,0:T(8,128)S(1)}, u32[]{:S(2)}, u32[]{:S(2)}) collective-permute-start(f32[4,4,16,128]{3,2,1,0:T(8,128)S(1)} %get-tuple-element.21), channel_id=1, source_target_pairs={{8,0},{9,1},{10,2},{11,3},{12,4},{13,5},{14,6},{15,7},{0,8},{1,9},... | collective-permute-start | bytes 393224 | tf_op jit(solution)/shard_map/ppermute | solution.py:167
  67.0 7.8 %collective-permute-start.8 = (f32[4,4,16,128]{3,2,1,0:T(8,128)S(1)}, f32[4,4,16,128]{3,2,1,0:T(8,128)S(1)}, u32[]{:S(2)}, u32[]{:S(2)}) collective-permute-start(f32[4,4,16,128]{3,2,1,0:T(8,128)S(1)} %get-tuple-element.21), channel_id=1, source_target_pairs={{9,0},{8,1},{11,2},{10,3},{13,4},{12,5},{15,6},{14,7},{1,8},{0,9},... | collective-permute-start | bytes 393224 | tf_op jit(solution)/shard_map/ppermute | solution.py:167
  68.9 0.7 copy-start.7
  69.6 0.9 copy-start.5
  75.6 0.9 copy-start.1
  82.8 7.4 %copy-start.2 = (f32[1024,128]{1,0:T(8,128)S(1)}, f32[1024,128]{1,0:T(8,128)}, u32[]{:S(2)}) copy-start(f32[1024,128]{1,0:T(8,128)} %get-tuple-element.12) | copy-start | bytes 1572868
  82.8 54.1 %all-to-all-start.1 = ((f32[16,104,128]{2,1,0:T(8,128)}), f32[16,104,128]{2,1,0:T(8,128)S(1)}, u32[]{:S(2)}, u32[]{:S(2)}) async-start(f32[16,104,128]{2,1,0:T(8,128)} %get-tuple-element.11), calls=%async_computation.1 | async-start | bytes 1703936 | tf_op jit(solution)/shard_map/all_to_all | solution.py:218
  90.2 9.2 %collective-permute-start.10 = (f32[4,4,16,128]{3,2,1,0:T(8,128)S(1)}, f32[4,4,16,128]{3,2,1,0:T(8,128)S(1)}, u32[]{:S(2)}, u32[]{:S(2)}) collective-permute-start(f32[4,4,16,128]{3,2,1,0:T(8,128)S(1)} %bitcast.58), channel_id=1, source_target_pairs={{0,8},{1,9},{2,10},{3,11},{4,12},{5,13},{6,14},{7,15},{8,0},{9,1},... | collective-permute-start | bytes 393224 | tf_op jit(solution)/shard_map/ppermute | solution.py:171
  92.3 8.2 %collective-permute-start.11 = (f32[4,4,16,128]{3,2,1,0:T(8,128)S(1)}, f32[4,4,16,128]{3,2,1,0:T(8,128)S(1)}, u32[]{:S(2)}, u32[]{:S(2)}) collective-permute-start(f32[4,4,16,128]{3,2,1,0:T(8,128)S(1)} %bitcast.57), channel_id=1, source_target_pairs={{0,9},{1,8},{2,11},{3,10},{4,13},{5,12},{6,15},{7,14},{8,1},{9,0},... | collective-permute-start | bytes 393224 | tf_op jit(solution)/shard_map/ppermute | solution.py:171
  95.5 7.8 %collective-permute-start.9 = (f32[4,4,16,128]{3,2,1,0:T(8,128)S(1)}, f32[4,4,16,128]{3,2,1,0:T(8,128)S(1)}, u32[]{:S(2)}, u32[]{:S(2)}) collective-permute-start(f32[4,4,16,128]{3,2,1,0:T(8,128)S(1)} %bitcast.56), channel_id=1, source_target_pairs={{0,1},{1,0},{2,3},{3,2},{4,5},{5,4},{6,7},{7,6},{8,9},{9,8},{10,11... | collective-permute-start | bytes 393224 | tf_op jit(solution)/shard_map/ppermute | solution.py:171
  103.3 14.2 %collective-permute-start.12 = (f32[4,16,128]{2,1,0:T(8,128)S(1)}, f32[4,16,128]{2,1,0:T(8,128)S(1)}, u32[]{:S(2)}, u32[]{:S(2)}) collective-permute-start(f32[4,16,128]{2,1,0:T(8,128)S(1)} %get-tuple-element.19), channel_id=1, source_target_pairs={{0,16},{1,17},{2,18},{3,19},{4,20},{5,21},{6,22},{7,23},{8,24},{9,... | collective-permute-start | bytes 98312 | tf_op jit(solution)/shard_map/ppermute | solution.py:171
  106.7 10.8 %collective-permute-start.13 = (f32[4,16,128]{2,1,0:T(8,128)S(1)}, f32[4,16,128]{2,1,0:T(8,128)S(1)}, u32[]{:S(2)}, u32[]{:S(2)}) collective-permute-start(f32[4,16,128]{2,1,0:T(8,128)S(1)} %get-tuple-element.17), channel_id=1, source_target_pairs={{0,32},{1,33},{2,34},{3,35},{4,36},{5,37},{6,38},{7,39},{8,40},{9,... | collective-permute-start | bytes 98312 | tf_op jit(solution)/shard_map/ppermute | solution.py:171
  111.5 7.6 %collective-permute-start.14 = (f32[4,16,128]{2,1,0:T(8,128)S(1)}, f32[4,16,128]{2,1,0:T(8,128)S(1)}, u32[]{:S(2)}, u32[]{:S(2)}) collective-permute-start(f32[4,16,128]{2,1,0:T(8,128)S(1)} %get-tuple-element.18), channel_id=1, source_target_pairs={{0,48},{1,49},{2,50},{3,51},{4,52},{5,53},{6,54},{7,55},{8,56},{9,... | collective-permute-start | bytes 98312 | tf_op jit(solution)/shard_map/ppermute | solution.py:171
  119.2 16.5 %collective-permute-start.15 = (f32[16,128]{1,0:T(8,128)S(1)}, f32[16,128]{1,0:T(8,128)S(1)}, u32[]{:S(2)}, u32[]{:S(2)}) collective-permute-start(f32[16,128]{1,0:T(8,128)S(1)} %get-tuple-element.24), channel_id=1, source_target_pairs={{0,2},{1,3},{2,4},{3,5},{4,6},{5,7},{6,0},{7,1},{8,10},{9,11},{10,... | collective-permute-start | bytes 24584 | tf_op jit(solution)/shard_map/ppermute | solution.py:171
  123.2 12.5 %collective-permute-start.16 = (f32[16,128]{1,0:T(8,128)S(1)}, f32[16,128]{1,0:T(8,128)S(1)}, u32[]{:S(2)}, u32[]{:S(2)}) collective-permute-start(f32[16,128]{1,0:T(8,128)S(1)} %get-tuple-element.22), channel_id=1, source_target_pairs={{0,4},{1,5},{2,6},{3,7},{4,0},{5,1},{6,2},{7,3},{8,12},{9,13},{10,... | collective-permute-start | bytes 24584 | tf_op jit(solution)/shard_map/ppermute | solution.py:171
  128.9 7.4 %collective-permute-start.17 = (f32[16,128]{1,0:T(8,128)S(1)}, f32[16,128]{1,0:T(8,128)S(1)}, u32[]{:S(2)}, u32[]{:S(2)}) collective-permute-start(f32[16,128]{1,0:T(8,128)S(1)} %get-tuple-element.23), channel_id=1, source_target_pairs={{0,6},{1,7},{2,0},{3,1},{4,2},{5,3},{6,4},{7,5},{8,14},{9,15},{10,... | collective-permute-start | bytes 24584 | tf_op jit(solution)/shard_map/ppermute | solution.py:171
  136.9 0.9 copy-start

commit v4 on v2

--- a/solution.py
+++ b/solution.py
@@ -13,7 +13,6 @@
 WIDE = CHUNKS * LANES
 HIGHEST = lax.Precision.HIGHEST
 VMEM = pl.BlockSpec(memory_space=pltpu.VMEM)
-SMEM = pl.BlockSpec(memory_space=pltpu.SMEM)
 
 
 def split(x, terms):
@@ -66,19 +65,40 @@
 
 
 def widen(ref, out_ref):
-    out_ref[:, WIDE - LANES :] = jnp.zeros((out_ref.shape[0], LANES), jnp.float32)
-    out_ref[:, : ref.shape[1]] = ref[...]
-
-
-def pick_kernel(neg_ref, send_ref, table_ref, rows_ref, negs_ref, table):
+    width = ref.shape[0]
+    out_ref[:width, :] = ref[...]
+    out_ref[width:, :] = jnp.zeros((out_ref.shape[0] - width, out_ref.shape[1]), jnp.float32)
+
+
+def select_columns(onehot, x, terms):
+    total = None
+    for part in split(x, terms):
+        product = lax.dot_general(onehot, part, (((1,), (1,)), ((), ())), preferred_element_type=jnp.float32)
+        total = product if total is None else total + product
+    return total
+
+
+def own_row(neg_ref, n):
+    return neg_ref[0, 0, n // 2 : n // 2 + 1, n % 2 : n % 2 + 1]
+
+
+def negs_kernel(neg_ref, table_ref, out_ref, table):
     widen(table_ref, table)
-    for n in range(neg_ref.shape[0]):
-        row = table[pl.ds(neg_ref[n], 1), :]
-        for j in range(CHUNKS):
-            negs_ref[j * 4 + n : j * 4 + n + 1, :] = row[:, j * LANES : (j + 1) * LANES]
-    slots, entities = send_ref.shape[0], table_ref.shape[0]
-    onehot = onehot_of(send_ref[...], (slots, entities), 1)
-    pack(select_rows(onehot, table[...], 3), rows_ref)
+    entities = table.shape[1]
+    place = lax.broadcasted_iota(jnp.int32, (8, entities), 0)
+    entity = lax.broadcasted_iota(jnp.int32, (8, entities), 1)
+    hit = jnp.zeros((8, entities), jnp.float32)
+    for n in range(4):
+        hit = jnp.where((place == n) & (entity == own_row(neg_ref, n)), 1.0, hit)
+    rows = select_columns(hit.astype(jnp.bfloat16), table[...], 3)
+    for j in range(CHUNKS):
+        out_ref[j * 4 : j * 4 + 4, :] = rows[:4, j * LANES : (j + 1) * LANES]
+
+
+def pick_kernel(send_ref, table_ref, rows_ref, table):
+    widen(table_ref, table)
+    onehot = onehot_of(send_ref[...], (send_ref.shape[0], table.shape[1]), 1)
+    pack(select_columns(onehot, table[...], 3), rows_ref)
 
 
 def grad_kernel(col_ref, row_ref, rel_ref, got_ref, negs_ref, back_ref, negs_back_ref, rows, negs, grads):
@@ -123,18 +143,22 @@
     pack(select_rows(onehot_of(row_ref[...], (slots, ends), 0), grads[...], 2), back_ref)
 
 
-def put_kernel(neg_ref, send_ref, got_ref, negs_ref, out_ref, rows):
+def put_kernel(send_ref, got_ref, out_ref, rows):
     unpack(got_ref, rows)
-    entities, width = out_ref.shape
-    result = select_rows(onehot_of(send_ref[...], (entities, rows.shape[0]), 0), rows[...], 2)
-    own = jnp.sum(negs_ref[...], axis=0)
-    place = lax.broadcasted_iota(jnp.int32, (entities, LANES), 0)
+    entities = out_ref.shape[1]
+    out_ref[...] = select_rows(onehot_of(send_ref[...], (entities, rows.shape[0]), 0), rows[...], 2).T
+
+
+def add_kernel(neg_ref, put_ref, parts_ref, out_ref):
+    own = jnp.sum(parts_ref[...], axis=0).T
+    width, entities = out_ref.shape
     for j in range(CHUNKS):
-        part = result[:, j * LANES : (j + 1) * LANES]
-        for n in range(neg_ref.shape[0]):
-            part = part + jnp.where(place == neg_ref[n], own[j * 4 + n : j * 4 + n + 1, :], 0.0)
-        stop = min(width, (j + 1) * LANES)
-        out_ref[:, j * LANES : stop] = part[:, : stop - j * LANES]
+        stop = min(width, (j + 1) * LANES) - j * LANES
+        part = put_ref[j * LANES : j * LANES + stop, :]
+        entity = lax.broadcasted_iota(jnp.int32, part.shape, 1)
+        for n in range(4):
+            part = part + jnp.where(entity == own_row(neg_ref, n), own[:stop, j * 4 + n : j * 4 + n + 1], 0.0)
+        out_ref[j * LANES : j * LANES + stop, :] = part
 
 
 def shaped(*shape):
@@ -143,6 +167,39 @@
 
 def scratch(*shape):
     return pltpu.VMEM(shape, jnp.float32)
+
+
+def even_groups(columns):
+    side = 1
+    while side * side < columns:
+        side *= 2
+    groups = []
+    for low_y in range(2):
+        for low_z in range(2):
+            ys, zs = range(low_y, columns // side, 2), range(low_z, side, 2)
+            groups.append([y * side + z for y in ys for z in zs])
+    return side, groups
+
+
+def swap(x, bit, columns):
+    return lax.ppermute(x, "bucket", [(b, b ^ bit) for b in range(columns)])
+
+
+def gather_columns(x, columns):
+    side, groups = even_groups(columns)
+    x = jnp.broadcast_to(x, (len(groups[0]), *x.shape))
+    x = lax.all_to_all(x, "bucket", split_axis=0, concat_axis=0, axis_index_groups=groups, tiled=True)
+    for bit in (1, side):
+        x = jnp.stack([x, swap(x, bit, columns)])
+    return x
+
+
+def sum_columns(x, columns):
+    side, groups = even_groups(columns)
+    x = x.reshape(2, 2, len(groups[0]), 16, LANES)
+    for bit in (side, 1):
+        x = x[0] + swap(x[1], bit, columns)
+    return lax.all_to_all(x, "bucket", split_axis=0, concat_axis=0, axis_index_groups=groups, tiled=True)
 
 
 def on_device(emb_table, rel_diag, send_rows, src_slot, dst_slot, neg_rows, block_rel):
@@ -151,18 +208,24 @@
     columns = lax.axis_size("bucket")
     packed = (owners, (CHUNKS - 1) * slots + slots // 4, LANES)
     send = send_rows.reshape(owners * slots)
-    own_rows = neg_rows.reshape(4)
-    picked, own_negs = pl.pallas_call(
+    table = emb_table.T
+    own_negs = pl.pallas_call(
+        negs_kernel,
+        out_shape=shaped(16, LANES),
+        in_specs=[VMEM, VMEM],
+        out_specs=VMEM,
+        scratch_shapes=[scratch(WIDE, entities)],
+        name="negs",
+    )(neg_rows, table)
+    picked = pl.pallas_call(
         pick_kernel,
-        out_shape=(shaped(*packed), shaped(16, LANES)),
-        in_specs=[SMEM, VMEM, VMEM],
-        out_specs=(VMEM, VMEM),
-        scratch_shapes=[scratch(entities, WIDE)],
+        out_shape=shaped(*packed),
+        in_specs=[VMEM, VMEM],
+        out_specs=VMEM,
+        scratch_shapes=[scratch(WIDE, entities)],
         name="pick",
-    )(own_rows, send[:, None], emb_table)
-    negs = lax.all_to_all(
-        jnp.broadcast_to(own_negs, (columns, 16, LANES)), "bucket", split_axis=0, concat_axis=0, tiled=True
-    )
+    )(send[:, None], table)
+    negs = gather_columns(own_negs, columns)
     got = lax.all_to_all(picked, "dom", split_axis=0, concat_axis=0, tiled=True)
     ends = jnp.concatenate([src_slot.reshape(-1), dst_slot.reshape(-1)])
     relation = jnp.pad(rel_diag[block_rel.reshape(-1)], ((0, 0), (0, WIDE - width)))
@@ -178,18 +241,23 @@
         ],
         name="grad",
     )(ends[:, None], ends[None, :], relation, got, negs.reshape(columns * 16, LANES))
-    own_grad = lax.all_to_all(
-        negs_back.reshape(columns, 16, LANES), "bucket", split_axis=0, concat_axis=0, tiled=True
-    )
+    own_grad = sum_columns(negs_back, columns)
     returned = lax.all_to_all(back, "dom", split_axis=0, concat_axis=0, tiled=True)
-    return pl.pallas_call(
+    put = pl.pallas_call(
         put_kernel,
-        out_shape=shaped(entities, width),
-        in_specs=[SMEM, VMEM, VMEM, VMEM],
+        out_shape=shaped(WIDE, entities),
+        in_specs=[VMEM, VMEM],
         out_specs=VMEM,
         scratch_shapes=[scratch(owners * slots, WIDE)],
         name="put",
-    )(own_rows, send[None, :], returned, own_grad)
+    )(send[None, :], returned)
+    return pl.pallas_call(
+        add_kernel,
+        out_shape=shaped(width, entities),
+        in_specs=[VMEM, VMEM, VMEM],
+        out_specs=VMEM,
+        name="add",
+    )(neg_rows, put, own_grad).T
 
 
 def solution(mesh):

time: 148 us -> 123 us (0.83)
  blocking collectives: 63.7 us -> 0 us
  starting transfers between devices: 15.3 us -> 51.3 us
  local copies, waits for them, and re-layouts: 12.9 us -> 7.44 us
  Pallas kernels: 11.8 us -> 15.9 us
  waiting for transfers between devices: 43.9 us -> 46.2 us
  other arithmetic: 0.02 us -> 1.59 us
    all_to_all x2 -> x0, blocking collectives: 63.7 us -> none  [the longest x1 40.2 us: on_device(): lax.all_to_all(jnp.broadcast_to(own_negs, (columns, 16, LANES)), 'bucket'...]
    all_to_all x0 -> x2, starting transfers between devices: none -> 25.8 us  [the longest x1 22.3 us: gather_columns(): lax.all_to_all(x, 'bucket', split_axis=0, concat_axis=0, axis_index_group...]
    ppermute x0 -> x4, waiting for transfers between devices: none -> 18.2 us  [swap(): return lax.ppermute(x, 'bucket', [(b, b ^ bit) for b in range(columns)])]
    all_to_all x1, waiting for transfers between devices: 23.3 us -> 5.73 us  [on_device(): lax.all_to_all(back, 'dom', split_axis=0, concat_axis=0, tiled=True)]
    all_to_all x0 -> x2, waiting for transfers between devices: none -> 16 us  [the longest x1 8.28 us: sum_columns(): lax.all_to_all(x, 'bucket', split_axis=0, concat_axis=0, axis_index_group...]
    all_to_all x1, waiting for transfers between devices: 20.6 us -> 6.2 us  [on_device(): got = lax.all_to_all(picked, 'dom', split_axis=0, concat_axis=0, tiled=True)]
    ppermute x0 -> x4, starting transfers between devices: none -> 12.9 us  [swap(): return lax.ppermute(x, 'bucket', [(b, b ^ bit) for b in range(columns)])]
    pallas_call x2 -> x4, Pallas kernels: 5.53 us -> 9.52 us  [the longest x1 2.69 us: on_device(): pl.pallas_call(pick_kernel, out_shape=shaped(*packed), in_specs=[VMEM, VM...]
  transfers between devices with their start and end apart: 2 -> 8, of which waited for: 2 -> 8; matrix products, arithmetic and copies ran while one was open for 2% -> 4% of each run, Pallas kernels for 0% -> 4%
where the time goes in v4:
time: 123 us
  starting transfers between devices  51.3 us (42%)
  waiting for transfers between devices  46.2 us (38%)
  Pallas kernels  15.9 us (13%)
  local copies, waits for them, and re-layouts  7.44 us (6%)
  other arithmetic  1.59 us (1%)
    all_to_all x1, starting transfers between devices, gather_columns(): lax.all_to_all(x, 'bucket', split_axis=0, concat_axis=0, axis_index_group...  22.3 us
    ppermute x4, waiting for transfers between devices, swap(): return lax.ppermute(x, 'bucket', [(b, b ^ bit) for b in range(columns)])  18.2 us
    ppermute x4, starting transfers between devices, swap(): return lax.ppermute(x, 'bucket', [(b, b ^ bit) for b in range(columns)])  12.9 us
    all_to_all x1, starting transfers between devices, on_device(): got = lax.all_to_all(picked, 'dom', split_axis=0, concat_axis=0, tiled=True)  8.99 us
    all_to_all x1, waiting for transfers between devices, sum_columns(): lax.all_to_all(x, 'bucket', split_axis=0, concat_axis=0, axis_index_group...  8.28 us
    all_to_all x1, waiting for transfers between devices, gather_columns(): lax.all_to_all(x, 'bucket', split_axis=0, concat_axis=0, axis_index_group...  7.76 us
    pallas_call x1, Pallas kernels, on_device(): pl.pallas_call(grad_kernel, out_shape=(shaped(*packed), shaped(columns *...  6.34 us
    all_to_all x1, waiting for transfers between devices, on_device(): got = lax.all_to_all(picked, 'dom', split_axis=0, concat_axis=0, tiled=True)  6.2 us
  transfers between devices with their start and end apart: 8, of which 8 were waited for; matrix products, arithmetic and copies ran while one was open for 4% of the time, Pallas kernels for 4%

profile of v4, /device:TPU:1, one launch (start us, length us, event | category | flops | bytes accessed | tf_op | source)
XLA Modules:
  0.0 122.6 jit_solution(7406739837538270406)
XLA Ops:
  0.0 2.0 %negs.1 = f32[16,128]{1,0:T(8,128)} custom-call(s32[1,1,2,2]{3,2,1,0:T(2,128)} %neg_ref.3, f32[400,256]{1,0:T(8,128)} %bitcast.29), custom_call_target="tpu_custom_call" | custom-call | tf_op jit(solution)/shard_map/negs/pallas_call | solution.py:212
  2.0 1.4 %broadcast_in_dim.12 = f32[16,16,128]{2,1,0:T(8,128)} broadcast(f32[16,128]{1,0:T(8,128)} %negs.1), dimensions={1,2} | broadcast | bytes 139264 | tf_op jit(solution)/shard_map/broadcast_in_dim | solution.py:190
  3.3 22.3 %all-to-all-start.1 = ((f32[16,16,128]{2,1,0:T(8,128)}), f32[16,16,128]{2,1,0:T(8,128)S(1)}, u32[]{:S(2)}, u32[]{:S(2)}) async-start(f32[16,16,128]{2,1,0:T(8,128)} %broadcast_in_dim.12), calls=%async_computation.1 | async-start | bytes 262144 | tf_op jit(solution)/shard_map/all_to_all | solution.py:191
  25.6 1.0 broadcast_in_dim_reshape.8.send_ref
  26.6 2.7 %pick.1 = f32[16,104,128]{2,1,0:T(8,128)} custom-call(s32[512,1]{1,0:T(8,128)} %broadcast_in_dim_reshape.8.send_ref, f32[400,256]{1,0:T(8,128)} %bitcast.30), custom_call_target="tpu_custom_call" | custom-call | tf_op jit(solution)/shard_map/pick/pallas_call | solution.py:220
  29.3 7.8 %all-to-all-done.1 = f32[16,16,128]{2,1,0:T(8,128)S(1)} async-done(((f32[16,16,128]{2,1,0:T(8,128)}), f32[16,16,128]{2,1,0:T(8,128)S(1)}, u32[]{:S(2)}, u32[]{:S(2)}) %all-to-all-start.1) | async-done | bytes 131104 | tf_op jit(solution)/shard_map/all_to_all | solution.py:191
  37.0 9.0 %all-to-all-start = ((f32[16,104,128]{2,1,0:T(8,128)}), f32[16,104,128]{2,1,0:T(8,128)S(1)}, u32[]{:S(2)}, u32[]{:S(2)}) async-start(f32[16,104,128]{2,1,0:T(8,128)} %pick.1), calls=%async_computation | async-start | bytes 1703936 | tf_op jit(solution)/shard_map/all_to_all | solution.py:229
  46.0 4.1 %collective-permute-start = (f32[16,16,128]{2,1,0:T(8,128)S(1)}, f32[16,16,128]{2,1,0:T(8,128)S(1)}, u32[]{:S(2)}, u32[]{:S(2)}) collective-permute-start(f32[16,16,128]{2,1,0:T(8,128)S(1)} %all-to-all-done.1), channel_id=1, source_target_pairs={{0,1},{1,0},{2,3},{3,2},{4,5},{5,4},{6,7},{7,6},{8,9},{9,8},{10,11... | collective-permute-start | bytes 393224 | tf_op jit(solution)/shard_map/ppermute | solution.py:185
  50.2 0.7 copy-done.7
  50.8 0.9 copy.11.col_ref
  51.9 2.0 %collective-permute-done = f32[16,16,128]{2,1,0:T(8,128)S(1)} collective-permute-done((f32[16,16,128]{2,1,0:T(8,128)S(1)}, f32[16,16,128]{2,1,0:T(8,128)S(1)}, u32[]{:S(2)}, u32[]{:S(2)}) %collective-permute-start) | collective-permute-done | bytes 131104 | tf_op jit(solution)/shard_map/ppermute | solution.py:185
  53.9 2.3 %collective-permute-start.1 = (f32[2,16,16,128]{3,2,1,0:T(8,128)S(1)}, f32[2,16,16,128]{3,2,1,0:T(8,128)S(1)}, u32[]{:S(2)}, u32[]{:S(2)}) collective-permute-start(f32[2,16,16,128]{3,2,1,0:T(8,128)S(1)} %get-tuple-element.12), channel_id=1, source_target_pairs={{0,8},{1,9},{2,10},{3,11},{4,12},{5,13},{6,14},{7,15},{8,0},{9,1},... | collective-permute-start | bytes 786440 | tf_op jit(solution)/shard_map/ppermute | solution.py:185
  56.3 0.6 gather_fusion
  56.9 0.6 pad.4.rel_ref
  57.5 5.5 %collective-permute-done.1 = f32[2,16,16,128]{3,2,1,0:T(8,128)S(1)} collective-permute-done((f32[2,16,16,128]{3,2,1,0:T(8,128)S(1)}, f32[2,16,16,128]{3,2,1,0:T(8,128)S(1)}, u32[]{:S(2)}, u32[]{:S(2)}) %collective-permute-start.1) | collective-permute-done | bytes 262176 | tf_op jit(solution)/shard_map/ppermute | solution.py:185
  63.0 0.8 pad_maximum_fusion
  63.8 6.2 %all-to-all-done.got_ref = f32[16,104,128]{2,1,0:T(8,128)S(1)} async-done(((f32[16,104,128]{2,1,0:T(8,128)}), f32[16,104,128]{2,1,0:T(8,128)S(1)}, u32[]{:S(2)}, u32[]{:S(2)}) %all-to-all-start) | async-done | bytes 852000 | tf_op jit(solution)/shard_map/all_to_all | solution.py:229
  70.0 0.9 copy-done
  70.9 6.3 %grad.1 = (f32[16,104,128]{2,1,0:T(8,128)}, f32[1024,128]{1,0:T(8,128)}) custom-call(s32[512,1]{1,0:T(8,128)} %copy.11.col_ref, s32[1,512]{1,0:T(1,128)} %bitcast.37, f32[2,512]{1,0:T(2,128)} %pad.4.rel_ref, f32[16,104,128]{2,1,0:T(8,128)} %copy-done, f32[1024,128]{1,0:T(8,128)} %bitcast.28), custom_call_target="tpu_custom_call" | custom-call | tf_op jit(solution)/shard_map/grad/pallas_call | solution.py:232
  77.3 3.7 %all-to-all-start.2 = ((f32[16,104,128]{2,1,0:T(8,128)}), f32[16,104,128]{2,1,0:T(8,128)S(1)}, u32[]{:S(2)}, u32[]{:S(2)}) async-start(f32[16,104,128]{2,1,0:T(8,128)} %get-tuple-element.7), calls=%async_computation.2 | async-start | bytes 1703936 | tf_op jit(solution)/shard_map/all_to_all | solution.py:245
  81.0 2.4 %collective-permute-start.2 = (f32[2,16,16,128]{3,2,1,0:T(8,128)S(1)}, f32[2,16,16,128]{3,2,1,0:T(8,128)S(1)}, u32[]{:S(2)}, u32[]{:S(2)}) collective-permute-start(f32[2,16,16,128]{3,2,1,0:T(8,128)S(1)} %bitcast.34), channel_id=1, source_target_pairs={{0,8},{1,9},{2,10},{3,11},{4,12},{5,13},{6,14},{7,15},{8,0},{9,1},... | collective-permute-start | bytes 786440 | tf_op jit(solution)/shard_map/ppermute | solution.py:185
  83.4 7.5 %collective-permute-done.2 = f32[2,16,16,128]{3,2,1,0:T(8,128)S(1)} collective-permute-done((f32[2,16,16,128]{3,2,1,0:T(8,128)S(1)}, f32[2,16,16,128]{3,2,1,0:T(8,128)S(1)}, u32[]{:S(2)}, u32[]{:S(2)}) %collective-permute-start.2) | collective-permute-done | bytes 262176 | tf_op jit(solution)/shard_map/ppermute | solution.py:185
  91.0 4.1 %collective-permute-start.3 = (f32[16,16,128]{2,1,0:T(8,128)S(1)}, f32[16,16,128]{2,1,0:T(8,128)S(1)}, u32[]{:S(2)}, u32[]{:S(2)}) collective-permute-start(f32[16,16,128]{2,1,0:T(8,128)S(1)} %slice_bitcast_fusion), channel_id=1, source_target_pairs={{0,1},{1,0},{2,3},{3,2},{4,5},{5,4},{6,7},{7,6},{8,9},{9,8},{10,11... | collective-permute-start | bytes 393224 | tf_op jit(solution)/shard_map/ppermute | solution.py:185
  95.1 3.2 %collective-permute-done.3 = f32[16,16,128]{2,1,0:T(8,128)S(1)} collective-permute-done((f32[16,16,128]{2,1,0:T(8,128)S(1)}, f32[16,16,128]{2,1,0:T(8,128)S(1)}, u32[]{:S(2)}, u32[]{:S(2)}) %collective-permute-start.3) | collective-permute-done | bytes 131104 | tf_op jit(solution)/shard_map/ppermute | solution.py:185
  98.2 0.7 fusion
  98.9 5.7 %all-to-all-done.2.got_ref = f32[16,104,128]{2,1,0:T(8,128)S(1)} async-done(((f32[16,104,128]{2,1,0:T(8,128)}), f32[16,104,128]{2,1,0:T(8,128)S(1)}, u32[]{:S(2)}, u32[]{:S(2)}) %all-to-all-start.2) | async-done | bytes 852000 | tf_op jit(solution)/shard_map/all_to_all | solution.py:245
  104.7 3.5 %all-to-all-start.3 = ((f32[16,16,128]{2,1,0:T(8,128)}), f32[16,16,128]{2,1,0:T(8,128)S(1)}, u32[]{:S(2)}, u32[]{:S(2)}) async-start(f32[16,16,128]{2,1,0:T(8,128)} %fusion), calls=%async_computation.3 | async-start | bytes 262144 | tf_op jit(solution)/shard_map/all_to_all | solution.py:202
  108.2 0.6 broadcast_in_dim_reshape.6.send_ref
  108.8 2.6 %put.1.put_ref = f32[512,256]{1,0:T(8,128)} custom-call(s32[1,512]{1,0:T(1,128)} %broadcast_in_dim_reshape.6.send_ref, f32[16,104,128]{2,1,0:T(8,128)} %copy-done.1), custom_call_target="tpu_custom_call" | custom-call | tf_op jit(solution)/shard_map/put/pallas_call | solution.py:246
  111.4 8.3 %all-to-all-done.3.parts_ref = f32[16,16,128]{2,1,0:T(8,128)S(1)} async-done(((f32[16,16,128]{2,1,0:T(8,128)}), f32[16,16,128]{2,1,0:T(8,128)S(1)}, u32[]{:S(2)}, u32[]{:S(2)}) %all-to-all-start.3) | async-done | bytes 131104 | tf_op jit(solution)/shard_map/all_to_all | solution.py:202
  119.6 0.6 copy-done.2
  120.3 2.3 %add.28 = f32[400,256]{1,0:T(8,128)} custom-call(s32[1,1,2,2]{3,2,1,0:T(2,128)} %neg_ref.3, f32[512,256]{1,0:T(8,128)} %put.1.put_ref, f32[16,16,128]{2,1,0:T(8,128)} %copy-done.2), custom_call_target="tpu_custom_call" | custom-call | tf_op jit(solution)/shard_map/add/pallas_call | solution.py:254
  (25 shorter events, 0.4 us)
Async XLA Ops:
  3.3 22.3 %copy-start.5 = (s32[1,1,16,32]{3,2,1,0:T(8,128)S(1)}, s32[1,1,16,32]{3,2,1,0:T(8,128)}, u32[]{:S(2)}) copy-start(s32[1,1,16,32]{3,2,1,0:T(8,128)} %param.9) | copy-start | bytes 6148
  3.3 33.7 %all-to-all-start.1 = ((f32[16,16,128]{2,1,0:T(8,128)}), f32[16,16,128]{2,1,0:T(8,128)S(1)}, u32[]{:S(2)}, u32[]{:S(2)}) async-start(f32[16,16,128]{2,1,0:T(8,128)} %broadcast_in_dim.12), calls=%async_computation.1 | async-start | bytes 262144 | tf_op jit(solution)/shard_map/all_to_all | solution.py:191
  37.0 13.1 %copy-start.8 = (s32[1,1,256]{2,1,0:T(1,128)S(1)}, s32[1,1,256]{2,1,0:T(1,128)}, u32[]{:S(2)}) copy-start(s32[1,1,256]{2,1,0:T(1,128)} %param.10) | copy-start | bytes 3076
  37.0 14.7 %copy-start.4 = (f32[256,400]{0,1:T(8,128)S(1)}, f32[256,400]{0,1:T(8,128)}, u32[]{:S(2)}) copy-start(f32[256,400]{0,1:T(8,128)} %param.8) | copy-start | bytes 1228804
  37.0 33.0 %all-to-all-start = ((f32[16,104,128]{2,1,0:T(8,128)}), f32[16,104,128]{2,1,0:T(8,128)S(1)}, u32[]{:S(2)}, u32[]{:S(2)}) async-start(f32[16,104,128]{2,1,0:T(8,128)} %pick.1), calls=%async_computation | async-start | bytes 1703936 | tf_op jit(solution)/shard_map/all_to_all | solution.py:229
  46.0 7.8 %collective-permute-start = (f32[16,16,128]{2,1,0:T(8,128)S(1)}, f32[16,16,128]{2,1,0:T(8,128)S(1)}, u32[]{:S(2)}, u32[]{:S(2)}) collective-permute-start(f32[16,16,128]{2,1,0:T(8,128)S(1)} %all-to-all-done.1), channel_id=1, source_target_pairs={{0,1},{1,0},{2,3},{3,2},{4,5},{5,4},{6,7},{7,6},{8,9},{9,8},{10,11... | collective-permute-start | bytes 393224 | tf_op jit(solution)/shard_map/ppermute | solution.py:185
  50.1 0.7 copy-start.7
  50.8 0.9 copy-start.6
  53.9 2.4 %copy-start.9 = (s32[1,1,2]{2,1,0:T(1,128)S(1)}, s32[1,1,2]{2,1,0:T(1,128)}, u32[]{:S(2)}) copy-start(s32[1,1,2]{2,1,0:T(1,128)} %param.13) | copy-start | bytes 28
  53.9 9.1 %collective-permute-start.1 = (f32[2,16,16,128]{3,2,1,0:T(8,128)S(1)}, f32[2,16,16,128]{3,2,1,0:T(8,128)S(1)}, u32[]{:S(2)}, u32[]{:S(2)}) collective-permute-start(f32[2,16,16,128]{3,2,1,0:T(8,128)S(1)} %get-tuple-element.12), channel_id=1, source_target_pairs={{0,8},{1,9},{2,10},{3,11},{4,12},{5,13},{6,14},{7,15},{8,0},{9,1},... | collective-permute-start | bytes 786440 | tf_op jit(solution)/shard_map/ppermute | solution.py:185
  70.0 0.9 copy-start
  77.3 3.7 %copy-start.3 = (f32[1024,128]{1,0:T(8,128)S(1)}, f32[1024,128]{1,0:T(8,128)}, u32[]{:S(2)}) copy-start(f32[1024,128]{1,0:T(8,128)} %get-tuple-element.8) | copy-start | bytes 1572868
  77.3 27.4 %all-to-all-start.2 = ((f32[16,104,128]{2,1,0:T(8,128)}), f32[16,104,128]{2,1,0:T(8,128)S(1)}, u32[]{:S(2)}, u32[]{:S(2)}) async-start(f32[16,104,128]{2,1,0:T(8,128)} %get-tuple-element.7), calls=%async_computation.2 | async-start | bytes 1703936 | tf_op jit(solution)/shard_map/all_to_all | solution.py:245
  81.0 9.9 %collective-permute-start.2 = (f32[2,16,16,128]{3,2,1,0:T(8,128)S(1)}, f32[2,16,16,128]{3,2,1,0:T(8,128)S(1)}, u32[]{:S(2)}, u32[]{:S(2)}) collective-permute-start(f32[2,16,16,128]{3,2,1,0:T(8,128)S(1)} %bitcast.34), channel_id=1, source_target_pairs={{0,8},{1,9},{2,10},{3,11},{4,12},{5,13},{6,14},{7,15},{8,0},{9,1},... | collective-permute-start | bytes 786440 | tf_op jit(solution)/shard_map/ppermute | solution.py:185
  91.0 7.3 %collective-permute-start.3 = (f32[16,16,128]{2,1,0:T(8,128)S(1)}, f32[16,16,128]{2,1,0:T(8,128)S(1)}, u32[]{:S(2)}, u32[]{:S(2)}) collective-permute-start(f32[16,16,128]{2,1,0:T(8,128)S(1)} %slice_bitcast_fusion), channel_id=1, source_target_pairs={{0,1},{1,0},{2,3},{3,2},{4,5},{5,4},{6,7},{7,6},{8,9},{9,8},{10,11... | collective-permute-start | bytes 393224 | tf_op jit(solution)/shard_map/ppermute | solution.py:185
  104.6 4.1 %copy-start.1 = (f32[16,104,128]{2,1,0:T(8,128)}, f32[16,104,128]{2,1,0:T(8,128)S(1)}, u32[]{:S(2)}) copy-start(f32[16,104,128]{2,1,0:T(8,128)S(1)} %all-to-all-done.2.got_ref) | copy-start | bytes 2555908
  104.7 15.0 %all-to-all-start.3 = ((f32[16,16,128]{2,1,0:T(8,128)}), f32[16,16,128]{2,1,0:T(8,128)S(1)}, u32[]{:S(2)}, u32[]{:S(2)}) async-start(f32[16,16,128]{2,1,0:T(8,128)} %fusion), calls=%async_computation.3 | async-start | bytes 262144 | tf_op jit(solution)/shard_map/all_to_all | solution.py:202
  119.6 0.6 copy-start.2

commit v5 on v4

--- a/solution.py
+++ b/solution.py
@@ -92,7 +92,8 @@
         hit = jnp.where((place == n) & (entity == own_row(neg_ref, n)), 1.0, hit)
     rows = select_columns(hit.astype(jnp.bfloat16), table[...], 3)
     for j in range(CHUNKS):
-        out_ref[j * 4 : j * 4 + 4, :] = rows[:4, j * LANES : (j + 1) * LANES]
+        part = rows[:4, j * LANES : (j + 1) * LANES]
+        out_ref[:, j * 4 : j * 4 + 4, :] = jnp.broadcast_to(part, (out_ref.shape[0], 4, LANES))
 
 
 def pick_kernel(send_ref, table_ref, rows_ref, table):
@@ -161,44 +162,49 @@
         out_ref[j * LANES : j * LANES + stop, :] = part
 
 
+def near(x):
+    return pltpu.with_memory_space_constraint(x, pltpu.VMEM)
+
+
 def shaped(*shape):
     return jax.ShapeDtypeStruct(shape, jnp.float32)
 
 
-def scratch(*shape):
+def in_vmem(*shape):
     return pltpu.VMEM(shape, jnp.float32)
 
 
-def even_groups(columns):
+def quarters(columns):
     side = 1
     while side * side < columns:
         side *= 2
-    groups = []
-    for low_y in range(2):
-        for low_z in range(2):
-            ys, zs = range(low_y, columns // side, 2), range(low_z, side, 2)
-            groups.append([y * side + z for y in ys for z in zs])
-    return side, groups
-
-
-def swap(x, bit, columns):
-    return lax.ppermute(x, "bucket", [(b, b ^ bit) for b in range(columns)])
+    depth = columns // side
+    groups = [
+        [y * side + z for y in range(top, top + depth // 2) for z in range(left, left + side // 2)]
+        for top in (0, depth // 2)
+        for left in (0, side // 2)
+    ]
+
+    def mirror(flip_y, flip_z):
+        pairs = []
+        for b in range(columns):
+            y, z = divmod(b, side)
+            pairs.append((b, (depth - 1 - y if flip_y else y) * side + (side - 1 - z if flip_z else z)))
+        return pairs
+
+    return groups, [mirror(False, True), mirror(True, False), mirror(True, True)]
 
 
 def gather_columns(x, columns):
-    side, groups = even_groups(columns)
-    x = jnp.broadcast_to(x, (len(groups[0]), *x.shape))
+    groups, mirrors = quarters(columns)
     x = lax.all_to_all(x, "bucket", split_axis=0, concat_axis=0, axis_index_groups=groups, tiled=True)
-    for bit in (1, side):
-        x = jnp.stack([x, swap(x, bit, columns)])
-    return x
+    return jnp.stack([x] + [lax.ppermute(x, "bucket", pairs) for pairs in mirrors])
 
 
 def sum_columns(x, columns):
-    side, groups = even_groups(columns)
-    x = x.reshape(2, 2, len(groups[0]), 16, LANES)
-    for bit in (side, 1):
-        x = x[0] + swap(x[1], bit, columns)
+    groups, mirrors = quarters(columns)
+    x = x.reshape(4, len(groups[0]), 16, LANES)
+    x = x[0] + sum(lax.ppermute(x[i + 1], "bucket", pairs) for i, pairs in enumerate(mirrors))
     return lax.all_to_all(x, "bucket", split_axis=0, concat_axis=0, axis_index_groups=groups, tiled=True)
 
 
@@ -211,10 +217,10 @@
     table = emb_table.T
     own_negs = pl.pallas_call(
         negs_kernel,
-        out_shape=shaped(16, LANES),
+        out_shape=shaped(columns // 4, 16, LANES),
         in_specs=[VMEM, VMEM],
         out_specs=VMEM,
-        scratch_shapes=[scratch(WIDE, entities)],
+        scratch_shapes=[in_vmem(WIDE, entities)],
         name="negs",
     )(neg_rows, table)
     picked = pl.pallas_call(
@@ -222,7 +228,7 @@
         out_shape=shaped(*packed),
         in_specs=[VMEM, VMEM],
         out_specs=VMEM,
-        scratch_shapes=[scratch(WIDE, entities)],
+        scratch_shapes=[in_vmem(WIDE, entities)],
         name="pick",
     )(send[:, None], table)
     negs = gather_columns(own_negs, columns)
@@ -231,33 +237,33 @@
     relation = jnp.pad(rel_diag[block_rel.reshape(-1)], ((0, 0), (0, WIDE - width)))
     back, negs_back = pl.pallas_call(
         grad_kernel,
-        out_shape=(shaped(*packed), shaped(columns * 16, LANES)),
+        out_shape=(shaped(*packed), in_vmem(columns * 16, LANES)),
         in_specs=[VMEM] * 5,
         out_specs=(VMEM, VMEM),
         scratch_shapes=[
-            scratch(owners * slots, WIDE),
-            scratch(2 * columns, WIDE),
-            scratch(ends.shape[0], WIDE),
+            in_vmem(owners * slots, WIDE),
+            in_vmem(2 * columns, WIDE),
+            in_vmem(ends.shape[0], WIDE),
         ],
         name="grad",
-    )(ends[:, None], ends[None, :], relation, got, negs.reshape(columns * 16, LANES))
+    )(ends[:, None], ends[None, :], relation, near(got), near(negs.reshape(columns * 16, LANES)))
     own_grad = sum_columns(negs_back, columns)
     returned = lax.all_to_all(back, "dom", split_axis=0, concat_axis=0, tiled=True)
     put = pl.pallas_call(
         put_kernel,
-        out_shape=shaped(WIDE, entities),
+        out_shape=in_vmem(WIDE, entities),
         in_specs=[VMEM, VMEM],
         out_specs=VMEM,
-        scratch_shapes=[scratch(owners * slots, WIDE)],
+        scratch_shapes=[in_vmem(owners * slots, WIDE)],
         name="put",
-    )(send[None, :], returned)
+    )(send[None, :], near(returned))
     return pl.pallas_call(
         add_kernel,
         out_shape=shaped(width, entities),
         in_specs=[VMEM, VMEM, VMEM],
         out_specs=VMEM,
         name="add",
-    )(neg_rows, put, own_grad).T
+    )(neg_rows, near(put), near(own_grad)).T
 
 
 def solution(mesh):

time: 123 us -> 112 us (0.911); the launches traced: 123 us -> 110 us
  waiting for transfers between devices: 46.2 us -> 28.4 us
  starting transfers between devices: 51.3 us -> 62.7 us
  local copies, waits for them, and re-layouts: 7.44 us -> 4.53 us
  Pallas kernels: 15.9 us -> 13.7 us
    ppermute x4 -> x6, starting transfers between devices: 12.9 us -> 26.2 us  [the longest x3 15.4 us: gather_columns(): lax.ppermute(x, 'bucket', pairs)]
    all_to_all x1, starting transfers between devices: 22.3 us -> 14.2 us  [gather_columns(): lax.all_to_all(x, 'bucket', split_axis=0, concat_axis=0, axis_index_group...]
    all_to_all x1, waiting for transfers between devices: 6.2 us -> 0.01 us  [on_device(): got = lax.all_to_all(picked, 'dom', split_axis=0, concat_axis=0, tiled=True)]
    ppermute x4 -> x6, waiting for transfers between devices: 18.2 us -> 14.4 us  [the longest x3 8.08 us: sum_columns(): lax.ppermute(x[i + 1], 'bucket', pairs)]
    all_to_all x1, waiting for transfers between devices: 7.76 us -> 4.01 us  [gather_columns(): lax.all_to_all(x, 'bucket', split_axis=0, concat_axis=0, axis_index_group...]
    all_to_all x1, starting transfers between devices: 3.65 us -> 7.33 us  [on_device(): lax.all_to_all(back, 'dom', split_axis=0, concat_axis=0, tiled=True)]
    all_to_all x1, starting transfers between devices: 3.51 us -> 6.14 us  [sum_columns(): lax.all_to_all(x, 'bucket', split_axis=0, concat_axis=0, axis_index_group...]
    all_to_all x1, waiting for transfers between devices: 8.28 us -> 5.67 us  [sum_columns(): lax.all_to_all(x, 'bucket', split_axis=0, concat_axis=0, axis_index_group...]
  transfers between devices with their start and end apart: 8 -> 10, of which waited for: 8 -> 7; matrix products, arithmetic and copies ran while one was open for 4% -> 4% of each run, Pallas kernels for 4% -> 4%
where the time goes in v5:
time: 112 us; the launch traced here: 110 us
  starting transfers between devices  62.7 us (56%)
  waiting for transfers between devices  28.4 us (25%)
  Pallas kernels  13.7 us (12%)
  local copies, waits for them, and re-layouts  4.53 us (4%)
    ppermute x3, starting transfers between devices, gather_columns(): lax.ppermute(x, 'bucket', pairs)  15.4 us
    all_to_all x1, starting transfers between devices, gather_columns(): lax.all_to_all(x, 'bucket', split_axis=0, concat_axis=0, axis_index_group...  14.2 us
    ppermute x3, starting transfers between devices, sum_columns(): lax.ppermute(x[i + 1], 'bucket', pairs)  10.8 us
    all_to_all x1, starting transfers between devices, on_device(): got = lax.all_to_all(picked, 'dom', split_axis=0, concat_axis=0, tiled=True)  8.9 us
    ppermute x3, waiting for transfers between devices, sum_columns(): lax.ppermute(x[i + 1], 'bucket', pairs)  8.08 us
    all_to_all x1, starting transfers between devices, on_device(): lax.all_to_all(back, 'dom', split_axis=0, concat_axis=0, tiled=True)  7.33 us
    ppermute x3, waiting for transfers between devices, gather_columns(): lax.ppermute(x, 'bucket', pairs)  6.35 us
    all_to_all x1, starting transfers between devices, sum_columns(): lax.all_to_all(x, 'bucket', split_axis=0, concat_axis=0, axis_index_group...  6.14 us
  transfers between devices with their start and end apart: 10, of which 7 were waited for; matrix products, arithmetic and copies ran while one was open for 4% of the time, Pallas kernels for 4%

profile of v5, /device:TPU:1, one launch (start us, length us, event | category | flops | bytes accessed | tf_op | source)
XLA Modules:
  0.0 110.3 jit_solution(12429978206677390782)
XLA Ops:
  0.0 2.0 %negs.1 = f32[16,16,128]{2,1,0:T(8,128)} custom-call(s32[1,1,2,2]{3,2,1,0:T(2,128)} %neg_ref.3, f32[400,256]{1,0:T(8,128)} %bitcast.24), custom_call_target="tpu_custom_call" | custom-call | tf_op jit(solution)/shard_map/negs/pallas_call | solution.py:218
  2.0 14.2 %all-to-all-start.1 = ((f32[16,16,128]{2,1,0:T(8,128)}), f32[16,16,128]{2,1,0:T(8,128)S(1)}, u32[]{:S(2)}, u32[]{:S(2)}) async-start(f32[16,16,128]{2,1,0:T(8,128)} %negs.1), calls=%async_computation.1 | async-start | bytes 262144 | tf_op jit(solution)/shard_map/all_to_all | solution.py:200
  16.2 1.0 broadcast_in_dim_reshape.8.send_ref
  17.2 2.7 %pick.1 = f32[16,104,128]{2,1,0:T(8,128)} custom-call(s32[512,1]{1,0:T(8,128)} %broadcast_in_dim_reshape.8.send_ref, f32[400,256]{1,0:T(8,128)} %bitcast.25), custom_call_target="tpu_custom_call" | custom-call | tf_op jit(solution)/shard_map/pick/pallas_call | solution.py:226
  19.9 4.0 %all-to-all-done.1 = f32[16,16,128]{2,1,0:T(8,128)S(1)} async-done(((f32[16,16,128]{2,1,0:T(8,128)}), f32[16,16,128]{2,1,0:T(8,128)S(1)}, u32[]{:S(2)}, u32[]{:S(2)}) %all-to-all-start.1) | async-done | bytes 131104 | tf_op jit(solution)/shard_map/all_to_all | solution.py:200
  23.9 8.9 %all-to-all-start = ((f32[16,104,128]{2,1,0:T(8,128)}), f32[16,104,128]{2,1,0:T(8,128)S(1)}, u32[]{:S(2)}, u32[]{:S(2)}) async-start(f32[16,104,128]{2,1,0:T(8,128)} %pick.1), calls=%async_computation | async-start | bytes 1703936 | tf_op jit(solution)/shard_map/all_to_all | solution.py:235
  32.8 10.2 %collective-permute-start.2 = (f32[16,16,128]{2,1,0:T(8,128)S(1)}, f32[16,16,128]{2,1,0:T(8,128)S(1)}, u32[]{:S(2)}, u32[]{:S(2)}) collective-permute-start(f32[16,16,128]{2,1,0:T(8,128)S(1)} %all-to-all-done.1), channel_id=1, source_target_pairs={{0,63},{1,62},{2,61},{3,60},{4,59},{5,58},{6,57},{7,56},{8,55},{9,... | collective-permute-start | bytes 393224 | tf_op jit(solution)/shard_map/ppermute | solution.py:201
  43.0 1.9 %collective-permute-start = (f32[16,16,128]{2,1,0:T(8,128)S(1)}, f32[16,16,128]{2,1,0:T(8,128)S(1)}, u32[]{:S(2)}, u32[]{:S(2)}) collective-permute-start(f32[16,16,128]{2,1,0:T(8,128)S(1)} %all-to-all-done.1), channel_id=1, source_target_pairs={{0,7},{1,6},{2,5},{3,4},{4,3},{5,2},{6,1},{7,0},{8,15},{9,14},{10,... | collective-permute-start | bytes 393224 | tf_op jit(solution)/shard_map/ppermute | solution.py:201
  44.9 3.3 %collective-permute-start.1 = (f32[16,16,128]{2,1,0:T(8,128)S(1)}, f32[16,16,128]{2,1,0:T(8,128)S(1)}, u32[]{:S(2)}, u32[]{:S(2)}) collective-permute-start(f32[16,16,128]{2,1,0:T(8,128)S(1)} %all-to-all-done.1), channel_id=1, source_target_pairs={{0,56},{1,57},{2,58},{3,59},{4,60},{5,61},{6,62},{7,63},{8,48},{9,... | collective-permute-start | bytes 393224 | tf_op jit(solution)/shard_map/ppermute | solution.py:201
  48.2 0.0 copy-start.3
  48.2 0.7 copy-done.3
  48.9 0.9 copy.11.col_ref
  49.8 0.2 copy.9
  50.0 0.6 gather_fusion
  50.5 0.6 pad.4.rel_ref
  51.1 0.0 collective-permute-done.2
  51.1 6.3 %collective-permute-done = f32[16,16,128]{2,1,0:T(8,128)S(1)} collective-permute-done((f32[16,16,128]{2,1,0:T(8,128)S(1)}, f32[16,16,128]{2,1,0:T(8,128)S(1)}, u32[]{:S(2)}, u32[]{:S(2)}) %collective-permute-start) | collective-permute-done | bytes 131104 | tf_op jit(solution)/shard_map/ppermute | solution.py:201
  57.5 5.9 %grad.1 = (f32[16,104,128]{2,1,0:T(8,128)}, f32[1024,128]{1,0:T(8,128)S(1)}) custom-call(s32[512,1]{1,0:T(8,128)} %copy.11.col_ref, s32[1,512]{1,0:T(1,128)} %bitcast.35, f32[2,512]{1,0:T(2,128)} %pad.4.rel_ref, f32[16,104,128]{2,1,0:T(8,128)S(1)} %all-to-all-done.got_ref, f32[1024,128]{1,0:T(8,128)S(1)} %bitcast.23), custom_call_target="tpu_custom_call" | custom-call | tf_op jit(solution)/shard_map/grad/pallas_call | solution.py:238
  63.4 7.3 %all-to-all-start.2 = ((f32[16,104,128]{2,1,0:T(8,128)}), f32[16,104,128]{2,1,0:T(8,128)S(1)}, u32[]{:S(2)}, u32[]{:S(2)}) async-start(f32[16,104,128]{2,1,0:T(8,128)} %get-tuple-element.7), calls=%async_computation.2 | async-start | bytes 1703936 | tf_op jit(solution)/shard_map/all_to_all | solution.py:251
  70.8 4.6 %collective-permute-start.3 = (f32[16,16,128]{2,1,0:T(8,128)S(1)}, f32[16,16,128]{2,1,0:T(8,128)S(1)}, u32[]{:S(2)}, u32[]{:S(2)}) collective-permute-start(f32[16,16,128]{2,1,0:T(8,128)S(1)} %bitcast.33), channel_id=1, source_target_pairs={{0,7},{1,6},{2,5},{3,4},{4,3},{5,2},{6,1},{7,0},{8,15},{9,14},{10,... | collective-permute-start | bytes 393224 | tf_op jit(solution)/shard_map/ppermute | solution.py:207
  75.3 3.2 %collective-permute-start.4 = (f32[16,16,128]{2,1,0:T(8,128)S(1)}, f32[16,16,128]{2,1,0:T(8,128)S(1)}, u32[]{:S(2)}, u32[]{:S(2)}) collective-permute-start(f32[16,16,128]{2,1,0:T(8,128)S(1)} %bitcast.32), channel_id=1, source_target_pairs={{0,56},{1,57},{2,58},{3,59},{4,60},{5,61},{6,62},{7,63},{8,48},{9,... | collective-permute-start | bytes 393224 | tf_op jit(solution)/shard_map/ppermute | solution.py:207
  78.5 3.1 %collective-permute-start.5 = (f32[16,16,128]{2,1,0:T(8,128)S(1)}, f32[16,16,128]{2,1,0:T(8,128)S(1)}, u32[]{:S(2)}, u32[]{:S(2)}) collective-permute-start(f32[16,16,128]{2,1,0:T(8,128)S(1)} %bitcast.31), channel_id=1, source_target_pairs={{0,63},{1,62},{2,61},{3,60},{4,59},{5,58},{6,57},{7,56},{8,55},{9,... | collective-permute-start | bytes 393224 | tf_op jit(solution)/shard_map/ppermute | solution.py:207
  81.6 0.1 collective-permute-done.3
  81.7 4.5 %collective-permute-done.4 = f32[16,16,128]{2,1,0:T(8,128)S(1)} collective-permute-done((f32[16,16,128]{2,1,0:T(8,128)S(1)}, f32[16,16,128]{2,1,0:T(8,128)S(1)}, u32[]{:S(2)}, u32[]{:S(2)}) %collective-permute-start.4) | collective-permute-done | bytes 131104 | tf_op jit(solution)/shard_map/ppermute | solution.py:207
  86.2 3.5 %collective-permute-done.5 = f32[16,16,128]{2,1,0:T(8,128)S(1)} collective-permute-done((f32[16,16,128]{2,1,0:T(8,128)S(1)}, f32[16,16,128]{2,1,0:T(8,128)S(1)}, u32[]{:S(2)}, u32[]{:S(2)}) %collective-permute-start.5) | collective-permute-done | bytes 131104 | tf_op jit(solution)/shard_map/ppermute | solution.py:207
  89.7 0.7 add_add_fusion
  90.4 4.3 %all-to-all-done.2.got_ref = f32[16,104,128]{2,1,0:T(8,128)S(1)} async-done(((f32[16,104,128]{2,1,0:T(8,128)}), f32[16,104,128]{2,1,0:T(8,128)S(1)}, u32[]{:S(2)}, u32[]{:S(2)}) %all-to-all-start.2) | async-done | bytes 852000 | tf_op jit(solution)/shard_map/all_to_all | solution.py:251
  94.7 6.1 %all-to-all-start.3 = ((f32[16,16,128]{2,1,0:T(8,128)}), f32[16,16,128]{2,1,0:T(8,128)S(1)}, u32[]{:S(2)}, u32[]{:S(2)}) async-start(f32[16,16,128]{2,1,0:T(8,128)} %add_add_fusion), calls=%async_computation.3 | async-start | bytes 262144 | tf_op jit(solution)/shard_map/all_to_all | solution.py:208
  100.8 0.6 broadcast_in_dim_reshape.6.send_ref
  101.5 1.2 %put.1.put_ref = f32[512,256]{1,0:T(8,128)S(1)} custom-call(s32[1,512]{1,0:T(1,128)} %broadcast_in_dim_reshape.6.send_ref, f32[16,104,128]{2,1,0:T(8,128)S(1)} %all-to-all-done.2.got_ref), custom_call_target="tpu_custom_call" | custom-call | tf_op jit(solution)/shard_map/put/pallas_call | solution.py:252
  102.7 5.7 %all-to-all-done.3.parts_ref = f32[16,16,128]{2,1,0:T(8,128)S(1)} async-done(((f32[16,16,128]{2,1,0:T(8,128)}), f32[16,16,128]{2,1,0:T(8,128)S(1)}, u32[]{:S(2)}, u32[]{:S(2)}) %all-to-all-start.3) | async-done | bytes 131104 | tf_op jit(solution)/shard_map/all_to_all | solution.py:208
  108.4 1.9 %add.34 = f32[400,256]{1,0:T(8,128)} custom-call(s32[1,1,2,2]{3,2,1,0:T(2,128)} %neg_ref.3, f32[512,256]{1,0:T(8,128)S(1)} %put.1.put_ref, f32[16,16,128]{2,1,0:T(8,128)S(1)} %all-to-all-done.3.parts_ref), custom_call_target="tpu_custom_call" | custom-call | tf_op jit(solution)/shard_map/add/pallas_call | solution.py:260
  (17 shorter events, 0.1 us)
Async XLA Ops:
  2.0 14.2 %copy-start.1 = (s32[1,1,16,32]{3,2,1,0:T(8,128)S(1)}, s32[1,1,16,32]{3,2,1,0:T(8,128)}, u32[]{:S(2)}) copy-start(s32[1,1,16,32]{3,2,1,0:T(8,128)} %param.9) | copy-start | bytes 6148
  2.0 21.8 %all-to-all-start.1 = ((f32[16,16,128]{2,1,0:T(8,128)}), f32[16,16,128]{2,1,0:T(8,128)S(1)}, u32[]{:S(2)}, u32[]{:S(2)}) async-start(f32[16,16,128]{2,1,0:T(8,128)} %negs.1), calls=%async_computation.1 | async-start | bytes 262144 | tf_op jit(solution)/shard_map/all_to_all | solution.py:200
  19.9 12.9 %copy-start.5 = (s32[1,1,2]{2,1,0:T(1,128)S(1)}, s32[1,1,2]{2,1,0:T(1,128)}, u32[]{:S(2)}) copy-start(s32[1,1,2]{2,1,0:T(1,128)} %param.13) | copy-start | bytes 28
  23.9 24.3 %copy-start.4 = (s32[1,1,256]{2,1,0:T(1,128)S(1)}, s32[1,1,256]{2,1,0:T(1,128)}, u32[]{:S(2)}) copy-start(s32[1,1,256]{2,1,0:T(1,128)} %param.10) | copy-start | bytes 3076
  23.9 25.9 %copy-start = (f32[256,400]{0,1:T(8,128)S(1)}, f32[256,400]{0,1:T(8,128)}, u32[]{:S(2)}) copy-start(f32[256,400]{0,1:T(8,128)} %param.8) | copy-start | bytes 1228804
  23.9 33.7 %all-to-all-start = ((f32[16,104,128]{2,1,0:T(8,128)}), f32[16,104,128]{2,1,0:T(8,128)S(1)}, u32[]{:S(2)}, u32[]{:S(2)}) async-start(f32[16,104,128]{2,1,0:T(8,128)} %pick.1), calls=%async_computation | async-start | bytes 1703936 | tf_op jit(solution)/shard_map/all_to_all | solution.py:235
  32.8 18.3 %collective-permute-start.2 = (f32[16,16,128]{2,1,0:T(8,128)S(1)}, f32[16,16,128]{2,1,0:T(8,128)S(1)}, u32[]{:S(2)}, u32[]{:S(2)}) collective-permute-start(f32[16,16,128]{2,1,0:T(8,128)S(1)} %all-to-all-done.1), channel_id=1, source_target_pairs={{0,63},{1,62},{2,61},{3,60},{4,59},{5,58},{6,57},{7,56},{8,55},{9,... | collective-permute-start | bytes 393224 | tf_op jit(solution)/shard_map/ppermute | solution.py:201
  43.0 14.5 %collective-permute-start = (f32[16,16,128]{2,1,0:T(8,128)S(1)}, f32[16,16,128]{2,1,0:T(8,128)S(1)}, u32[]{:S(2)}, u32[]{:S(2)}) collective-permute-start(f32[16,16,128]{2,1,0:T(8,128)S(1)} %all-to-all-done.1), channel_id=1, source_target_pairs={{0,7},{1,6},{2,5},{3,4},{4,3},{5,2},{6,1},{7,0},{8,15},{9,14},{10,... | collective-permute-start | bytes 393224 | tf_op jit(solution)/shard_map/ppermute | solution.py:201
  44.9 12.6 %collective-permute-start.1 = (f32[16,16,128]{2,1,0:T(8,128)S(1)}, f32[16,16,128]{2,1,0:T(8,128)S(1)}, u32[]{:S(2)}, u32[]{:S(2)}) collective-permute-start(f32[16,16,128]{2,1,0:T(8,128)S(1)} %all-to-all-done.1), channel_id=1, source_target_pairs={{0,56},{1,57},{2,58},{3,59},{4,60},{5,61},{6,62},{7,63},{8,48},{9,... | collective-permute-start | bytes 393224 | tf_op jit(solution)/shard_map/ppermute | solution.py:201
  48.2 0.7 copy-start.3
  48.9 0.9 copy-start.2
  63.4 31.3 %all-to-all-start.2 = ((f32[16,104,128]{2,1,0:T(8,128)}), f32[16,104,128]{2,1,0:T(8,128)S(1)}, u32[]{:S(2)}, u32[]{:S(2)}) async-start(f32[16,104,128]{2,1,0:T(8,128)} %get-tuple-element.7), calls=%async_computation.2 | async-start | bytes 1703936 | tf_op jit(solution)/shard_map/all_to_all | solution.py:251
  70.8 11.0 %collective-permute-start.3 = (f32[16,16,128]{2,1,0:T(8,128)S(1)}, f32[16,16,128]{2,1,0:T(8,128)S(1)}, u32[]{:S(2)}, u32[]{:S(2)}) collective-permute-start(f32[16,16,128]{2,1,0:T(8,128)S(1)} %bitcast.33), channel_id=1, source_target_pairs={{0,7},{1,6},{2,5},{3,4},{4,3},{5,2},{6,1},{7,0},{8,15},{9,14},{10,... | collective-permute-start | bytes 393224 | tf_op jit(solution)/shard_map/ppermute | solution.py:207
  75.3 10.9 %collective-permute-start.4 = (f32[16,16,128]{2,1,0:T(8,128)S(1)}, f32[16,16,128]{2,1,0:T(8,128)S(1)}, u32[]{:S(2)}, u32[]{:S(2)}) collective-permute-start(f32[16,16,128]{2,1,0:T(8,128)S(1)} %bitcast.32), channel_id=1, source_target_pairs={{0,56},{1,57},{2,58},{3,59},{4,60},{5,61},{6,62},{7,63},{8,48},{9,... | collective-permute-start | bytes 393224 | tf_op jit(solution)/shard_map/ppermute | solution.py:207
  78.5 11.2 %collective-permute-start.5 = (f32[16,16,128]{2,1,0:T(8,128)S(1)}, f32[16,16,128]{2,1,0:T(8,128)S(1)}, u32[]{:S(2)}, u32[]{:S(2)}) collective-permute-start(f32[16,16,128]{2,1,0:T(8,128)S(1)} %bitcast.31), channel_id=1, source_target_pairs={{0,63},{1,62},{2,61},{3,60},{4,59},{5,58},{6,57},{7,56},{8,55},{9,... | collective-permute-start | bytes 393224 | tf_op jit(solution)/shard_map/ppermute | solution.py:207
  94.7 13.7 %all-to-all-start.3 = ((f32[16,16,128]{2,1,0:T(8,128)}), f32[16,16,128]{2,1,0:T(8,128)S(1)}, u32[]{:S(2)}, u32[]{:S(2)}) async-start(f32[16,16,128]{2,1,0:T(8,128)} %add_add_fusion), calls=%async_computation.3 | async-start | bytes 262144 | tf_op jit(solution)/shard_map/all_to_all | solution.py:208

commit v6 on v5

--- a/solution.py
+++ b/solution.py
@@ -11,6 +11,7 @@
 CHUNKS = 4
 TAIL = 16
 WIDE = CHUNKS * LANES
+UNIT = 13
 HIGHEST = lax.Precision.HIGHEST
 VMEM = pl.BlockSpec(memory_space=pltpu.VMEM)
 
@@ -30,6 +31,12 @@
         product = jnp.dot(onehot, part, preferred_element_type=jnp.float32)
         total = product if total is None else total + product
     return total
+
+
+def product(a, b):
+    (a_high, a_low), (b_high, b_low) = split(a, 2), split(b, 2)
+    dot = lambda x, y: jnp.dot(x, y, preferred_element_type=jnp.float32)
+    return dot(a_high, b_high) + (dot(a_high, b_low) + dot(a_low, b_high))
 
 
 def onehot_of(index, shape, axis):
@@ -109,6 +116,7 @@
     blocks = rel_ref.shape[0]
     block = edges // blocks
     owners = negs_ref.shape[0] // 16
+    tail = jnp.zeros((owners, LANES), jnp.float32)
     picked = select_rows(onehot_of(col_ref[...], (ends, slots), 1), rows[...], 3)
     for c in range(blocks):
         for k in range(2):
@@ -130,17 +138,18 @@
         total = pos_exp + jnp.sum(neg_exp, axis=1, keepdims=True)
         pos_weight = pos_exp / total - 1.0
         weight = neg_exp / total
-        query_grad = pos_weight * target + jnp.dot(
-            weight, negatives, precision=HIGHEST, preferred_element_type=jnp.float32
-        )
+        query_grad = pos_weight * target + product(weight, negatives)
         grads[c * block : (c + 1) * block, :] = query_grad * relation
         grads[edges + c * block : edges + (c + 1) * block, :] = pos_weight * query
-        neg_grad = jnp.dot(weight.T, query, precision=HIGHEST, preferred_element_type=jnp.float32)
+        neg_grad = product(weight.T, query)
         for k in range(2):
-            for j in range(CHUNKS):
-                negs_back_ref[pl.ds(j * 4 + c * 2 + k, owners, stride=16), :] = neg_grad[
-                    k * owners : (k + 1) * owners, j * LANES : (j + 1) * LANES
-                ]
+            n = c * 2 + k
+            part = neg_grad[k * owners : (k + 1) * owners]
+            for j in range(CHUNKS - 1):
+                negs_back_ref[pl.ds(j * 4 + n, owners, stride=UNIT), :] = part[:, j * LANES : (j + 1) * LANES]
+            last = part[:, (CHUNKS - 1) * LANES :]
+            tail = tail + (pltpu.roll(last, TAIL * n, 1) if n else last)
+    negs_back_ref[pl.ds(UNIT - 1, owners, stride=UNIT), :] = tail
     pack(select_rows(onehot_of(row_ref[...], (slots, ends), 0), grads[...], 2), back_ref)
 
 
@@ -150,16 +159,26 @@
     out_ref[...] = select_rows(onehot_of(send_ref[...], (entities, rows.shape[0]), 0), rows[...], 2).T
 
 
-def add_kernel(neg_ref, put_ref, parts_ref, out_ref):
+def add_kernel(neg_ref, put_ref, parts_ref, out_ref, total, sems):
     own = jnp.sum(parts_ref[...], axis=0).T
     width, entities = out_ref.shape
+    copies = []
     for j in range(CHUNKS):
         stop = min(width, (j + 1) * LANES) - j * LANES
         part = put_ref[j * LANES : j * LANES + stop, :]
         entity = lax.broadcasted_iota(jnp.int32, part.shape, 1)
         for n in range(4):
-            part = part + jnp.where(entity == own_row(neg_ref, n), own[:stop, j * 4 + n : j * 4 + n + 1], 0.0)
-        out_ref[j * LANES : j * LANES + stop, :] = part
+            if stop == LANES:
+                own_part = own[:, j * 4 + n : j * 4 + n + 1]
+            else:
+                own_part = own[TAIL * n : TAIL * n + stop, UNIT - 1 : UNIT]
+            part = part + jnp.where(entity == own_row(neg_ref, n), own_part, 0.0)
+        rows = pl.ds(j * LANES, stop)
+        total[rows, :] = part
+        copies.append(pltpu.make_async_copy(total.at[rows], out_ref.at[rows], sems.at[j]))
+        copies[-1].start()
+    for copy in copies:
+        copy.wait()
 
 
 def near(x):
@@ -203,8 +222,10 @@
 
 def sum_columns(x, columns):
     groups, mirrors = quarters(columns)
-    x = x.reshape(4, len(groups[0]), 16, LANES)
-    x = x[0] + sum(lax.ppermute(x[i + 1], "bucket", pairs) for i, pairs in enumerate(mirrors))
+    x = x.reshape(4, len(groups[0]) * UNIT, LANES)
+    both, up, across = [lax.ppermute(x[i], "bucket", mirrors[i - 1]) for i in (3, 2, 1)]
+    x = ((both + up) + across) + x[0]
+    x = x.reshape(len(groups[0]), UNIT, LANES)
     return lax.all_to_all(x, "bucket", split_axis=0, concat_axis=0, axis_index_groups=groups, tiled=True)
 
 
@@ -237,7 +258,7 @@
     relation = jnp.pad(rel_diag[block_rel.reshape(-1)], ((0, 0), (0, WIDE - width)))
     back, negs_back = pl.pallas_call(
         grad_kernel,
-        out_shape=(shaped(*packed), in_vmem(columns * 16, LANES)),
+        out_shape=(shaped(*packed), in_vmem(columns * UNIT, LANES)),
         in_specs=[VMEM] * 5,
         out_specs=(VMEM, VMEM),
         scratch_shapes=[
@@ -246,7 +267,7 @@
             in_vmem(ends.shape[0], WIDE),
         ],
         name="grad",
-    )(ends[:, None], ends[None, :], relation, near(got), near(negs.reshape(columns * 16, LANES)))
+    )(near(ends[:, None]), near(ends[None, :]), near(relation), near(got), near(negs.reshape(columns * 16, LANES)))
     own_grad = sum_columns(negs_back, columns)
     returned = lax.all_to_all(back, "dom", split_axis=0, concat_axis=0, tiled=True)
     put = pl.pallas_call(
@@ -256,14 +277,15 @@
         out_specs=VMEM,
         scratch_shapes=[in_vmem(owners * slots, WIDE)],
         name="put",
-    )(send[None, :], near(returned))
+    )(near(send[None, :]), near(returned))
     return pl.pallas_call(
         add_kernel,
         out_shape=shaped(width, entities),
         in_specs=[VMEM, VMEM, VMEM],
-        out_specs=VMEM,
+        out_specs=pl.BlockSpec(memory_space=pl.ANY),
+        scratch_shapes=[in_vmem(width, entities), pltpu.SemaphoreType.DMA((CHUNKS,))],
         name="add",
-    )(neg_rows, near(put), near(own_grad)).T
+    )(near(neg_rows), near(put), near(own_grad)).T
 
 
 def solution(mesh):

time: 112 us -> 109 us (0.973)
  Pallas kernels: 13.7 us -> 10.6 us
  waiting for transfers between devices: 28.4 us -> 30.9 us
  local copies, waits for them, and re-layouts: 4.53 us -> 3.33 us
    all_to_all x1, waiting for transfers between devices: 4.33 us -> 6.1 us  [on_device(): lax.all_to_all(back, 'dom', split_axis=0, concat_axis=0, tiled=True)]
    ppermute x3, waiting for transfers between devices: 8.08 us -> 6.31 us  [sum_columns(): lax.ppermute(x[i], 'bucket', mirrors[i - 1])]
    pallas_call x1, Pallas kernels: 5.85 us -> 4.13 us  [on_device(): pl.pallas_call(grad_kernel, out_shape=(shaped(*packed), in_vmem(columns *...]
    ppermute x3, waiting for transfers between devices: 6.35 us -> 7.64 us  [gather_columns(): lax.ppermute(x, 'bucket', pairs)]
    all_to_all x1, waiting for transfers between devices: 5.67 us -> 6.88 us  [sum_columns(): lax.all_to_all(x, 'bucket', split_axis=0, concat_axis=0, axis_index_group...]
  transfers between devices with their start and end apart: 10 -> 10, of which waited for: 7 -> 7; matrix products, arithmetic and copies ran while one was open for 4% -> 3% of each run, Pallas kernels for 4% -> 3%
where the time goes in v6:
time: 109 us; the launch traced here: 108 us
  starting transfers between devices  62.7 us (58%)
  waiting for transfers between devices  30.9 us (28%)
  Pallas kernels  10.6 us (10%)
  local copies, waits for them, and re-layouts  3.33 us (3%)
    ppermute x3, starting transfers between devices, gather_columns(): lax.ppermute(x, 'bucket', pairs)  15.4 us
    all_to_all x1, starting transfers between devices, gather_columns(): lax.all_to_all(x, 'bucket', split_axis=0, concat_axis=0, axis_index_group...  14.2 us
    ppermute x3, starting transfers between devices, sum_columns(): lax.ppermute(x[i], 'bucket', mirrors[i - 1])  10.8 us
    all_to_all x1, starting transfers between devices, on_device(): got = lax.all_to_all(picked, 'dom', split_axis=0, concat_axis=0, tiled=True)  8.9 us
    ppermute x3, waiting for transfers between devices, gather_columns(): lax.ppermute(x, 'bucket', pairs)  7.64 us
    all_to_all x1, starting transfers between devices, on_device(): lax.all_to_all(back, 'dom', split_axis=0, concat_axis=0, tiled=True)  7.34 us
    all_to_all x1, waiting for transfers between devices, sum_columns(): lax.all_to_all(x, 'bucket', split_axis=0, concat_axis=0, axis_index_group...  6.88 us
    ppermute x3, waiting for transfers between devices, sum_columns(): lax.ppermute(x[i], 'bucket', mirrors[i - 1])  6.31 us
  transfers between devices with their start and end apart: 10, of which 7 were waited for; matrix products, arithmetic and copies ran while one was open for 3% of the time, Pallas kernels for 3%

profile of v6, /device:TPU:1, one launch (start us, length us, event | category | flops | bytes accessed | tf_op | source)
XLA Modules:
  0.0 107.8 jit_solution(18086699490652027633)
XLA Ops:
  0.0 2.0 %negs.1 = f32[16,16,128]{2,1,0:T(8,128)} custom-call(s32[1,1,2,2]{3,2,1,0:T(2,128)} %neg_ref.3, f32[400,256]{1,0:T(8,128)} %bitcast.22), custom_call_target="tpu_custom_call" | custom-call | tf_op jit(solution)/shard_map/negs/pallas_call | solution.py:239
  2.0 14.2 %all-to-all-start.1 = ((f32[16,16,128]{2,1,0:T(8,128)}), f32[16,16,128]{2,1,0:T(8,128)S(1)}, u32[]{:S(2)}, u32[]{:S(2)}) async-start(f32[16,16,128]{2,1,0:T(8,128)} %negs.1), calls=%async_computation.1 | async-start | bytes 262144 | tf_op jit(solution)/shard_map/all_to_all | solution.py:219
  16.2 1.0 broadcast_in_dim_reshape.8.send_ref
  17.2 2.7 %pick.1 = f32[16,104,128]{2,1,0:T(8,128)} custom-call(s32[512,1]{1,0:T(8,128)} %broadcast_in_dim_reshape.8.send_ref, f32[400,256]{1,0:T(8,128)} %bitcast.23), custom_call_target="tpu_custom_call" | custom-call | tf_op jit(solution)/shard_map/pick/pallas_call | solution.py:247
  19.9 4.0 %all-to-all-done.1 = f32[16,16,128]{2,1,0:T(8,128)S(1)} async-done(((f32[16,16,128]{2,1,0:T(8,128)}), f32[16,16,128]{2,1,0:T(8,128)S(1)}, u32[]{:S(2)}, u32[]{:S(2)}) %all-to-all-start.1) | async-done | bytes 131104 | tf_op jit(solution)/shard_map/all_to_all | solution.py:219
  23.9 8.9 %all-to-all-start = ((f32[16,104,128]{2,1,0:T(8,128)}), f32[16,104,128]{2,1,0:T(8,128)S(1)}, u32[]{:S(2)}, u32[]{:S(2)}) async-start(f32[16,104,128]{2,1,0:T(8,128)} %pick.1), calls=%async_computation | async-start | bytes 1703936 | tf_op jit(solution)/shard_map/all_to_all | solution.py:256
  32.8 10.2 %collective-permute-start.2 = (f32[16,16,128]{2,1,0:T(8,128)S(1)}, f32[16,16,128]{2,1,0:T(8,128)S(1)}, u32[]{:S(2)}, u32[]{:S(2)}) collective-permute-start(f32[16,16,128]{2,1,0:T(8,128)S(1)} %all-to-all-done.1), channel_id=1, source_target_pairs={{0,63},{1,62},{2,61},{3,60},{4,59},{5,58},{6,57},{7,56},{8,55},{9,... | collective-permute-start | bytes 393224 | tf_op jit(solution)/shard_map/ppermute | solution.py:220
  43.0 1.9 %collective-permute-start = (f32[16,16,128]{2,1,0:T(8,128)S(1)}, f32[16,16,128]{2,1,0:T(8,128)S(1)}, u32[]{:S(2)}, u32[]{:S(2)}) collective-permute-start(f32[16,16,128]{2,1,0:T(8,128)S(1)} %all-to-all-done.1), channel_id=1, source_target_pairs={{0,7},{1,6},{2,5},{3,4},{4,3},{5,2},{6,1},{7,0},{8,15},{9,14},{10,... | collective-permute-start | bytes 393224 | tf_op jit(solution)/shard_map/ppermute | solution.py:220
  44.9 3.3 %collective-permute-start.1 = (f32[16,16,128]{2,1,0:T(8,128)S(1)}, f32[16,16,128]{2,1,0:T(8,128)S(1)}, u32[]{:S(2)}, u32[]{:S(2)}) collective-permute-start(f32[16,16,128]{2,1,0:T(8,128)S(1)} %all-to-all-done.1), channel_id=1, source_target_pairs={{0,56},{1,57},{2,58},{3,59},{4,60},{5,61},{6,62},{7,63},{8,48},{9,... | collective-permute-start | bytes 393224 | tf_op jit(solution)/shard_map/ppermute | solution.py:220
  48.2 0.0 copy-start.3
  48.2 0.7 copy-done.3
  48.9 0.1 copy.11.col_ref
  49.1 0.2 copy.9
  49.3 0.6 gather_fusion
  49.8 0.5 collective-permute-done.2
  50.4 7.1 %collective-permute-done = f32[16,16,128]{2,1,0:T(8,128)S(1)} collective-permute-done((f32[16,16,128]{2,1,0:T(8,128)S(1)}, f32[16,16,128]{2,1,0:T(8,128)S(1)}, u32[]{:S(2)}, u32[]{:S(2)}) %collective-permute-start) | collective-permute-done | bytes 131104 | tf_op jit(solution)/shard_map/ppermute | solution.py:220
  57.5 0.0 collective-permute-done.1
  57.5 0.0 all-to-all-done.got_ref
  57.5 4.1 %grad.1 = (f32[16,104,128]{2,1,0:T(8,128)}, f32[832,128]{1,0:T(8,128)S(1)}) custom-call(s32[512,1]{1,0:T(8,128)S(1)} %copy.11.col_ref, s32[1,512]{1,0:T(1,128)S(1)} %bitcast.21, f32[2,512]{1,0:T(2,128)S(1)} %pad.4.rel_ref, f32[16,104,128]{2,1,0:T(8,128)S(1)} %all-to-all-done.got_ref, f32[1024,128]{1,0:T(8,128)S(1)} %bitcast.19), custom_call_target="tpu_custom_call" | custom-call | tf_op jit(solution)/shard_map/grad/pallas_call | solution.py:259
  61.7 7.3 %all-to-all-start.2 = ((f32[16,104,128]{2,1,0:T(8,128)}), f32[16,104,128]{2,1,0:T(8,128)S(1)}, u32[]{:S(2)}, u32[]{:S(2)}) async-start(f32[16,104,128]{2,1,0:T(8,128)} %get-tuple-element.7), calls=%async_computation.2 | async-start | bytes 1703936 | tf_op jit(solution)/shard_map/all_to_all | solution.py:272
  69.0 5.6 %collective-permute-start.3 = (f32[208,128]{1,0:T(8,128)S(1)}, f32[208,128]{1,0:T(8,128)S(1)}, u32[]{:S(2)}, u32[]{:S(2)}) collective-permute-start(f32[208,128]{1,0:T(8,128)S(1)} %get-tuple-element.11), channel_id=1, source_target_pairs={{0,63},{1,62},{2,61},{3,60},{4,59},{5,58},{6,57},{7,56},{8,55},{9,... | collective-permute-start | bytes 319496 | tf_op jit(solution)/shard_map/ppermute | solution.py:226
  74.6 3.3 %collective-permute-start.4 = (f32[208,128]{1,0:T(8,128)S(1)}, f32[208,128]{1,0:T(8,128)S(1)}, u32[]{:S(2)}, u32[]{:S(2)}) collective-permute-start(f32[208,128]{1,0:T(8,128)S(1)} %get-tuple-element.9), channel_id=1, source_target_pairs={{0,56},{1,57},{2,58},{3,59},{4,60},{5,61},{6,62},{7,63},{8,48},{9,... | collective-permute-start | bytes 319496 | tf_op jit(solution)/shard_map/ppermute | solution.py:226
  77.9 1.9 %collective-permute-start.5 = (f32[208,128]{1,0:T(8,128)S(1)}, f32[208,128]{1,0:T(8,128)S(1)}, u32[]{:S(2)}, u32[]{:S(2)}) collective-permute-start(f32[208,128]{1,0:T(8,128)S(1)} %get-tuple-element.10), channel_id=1, source_target_pairs={{0,7},{1,6},{2,5},{3,4},{4,3},{5,2},{6,1},{7,0},{8,15},{9,14},{10,... | collective-permute-start | bytes 319496 | tf_op jit(solution)/shard_map/ppermute | solution.py:226
  79.9 1.2 %collective-permute-done.3 = f32[208,128]{1,0:T(8,128)S(1)} collective-permute-done((f32[208,128]{1,0:T(8,128)S(1)}, f32[208,128]{1,0:T(8,128)S(1)}, u32[]{:S(2)}, u32[]{:S(2)}) %collective-permute-start.3) | collective-permute-done | bytes 106528 | tf_op jit(solution)/shard_map/ppermute | solution.py:226
  81.1 5.1 %collective-permute-done.4 = f32[208,128]{1,0:T(8,128)S(1)} collective-permute-done((f32[208,128]{1,0:T(8,128)S(1)}, f32[208,128]{1,0:T(8,128)S(1)}, u32[]{:S(2)}, u32[]{:S(2)}) %collective-permute-start.4) | collective-permute-done | bytes 106528 | tf_op jit(solution)/shard_map/ppermute | solution.py:226
  86.2 0.7 reshape.56
  86.9 6.1 %all-to-all-done.2.got_ref = f32[16,104,128]{2,1,0:T(8,128)S(1)} async-done(((f32[16,104,128]{2,1,0:T(8,128)}), f32[16,104,128]{2,1,0:T(8,128)S(1)}, u32[]{:S(2)}, u32[]{:S(2)}) %all-to-all-start.2) | async-done | bytes 852000 | tf_op jit(solution)/shard_map/all_to_all | solution.py:272
  93.0 6.1 %all-to-all-start.3 = ((f32[16,13,128]{2,1,0:T(8,128)}), f32[16,13,128]{2,1,0:T(8,128)S(1)}, u32[]{:S(2)}, u32[]{:S(2)}) async-start(f32[16,13,128]{2,1,0:T(8,128)} %reshape.56), calls=%async_computation.3 | async-start | bytes 262144 | tf_op jit(solution)/shard_map/all_to_all | solution.py:229
  99.1 0.1 broadcast_in_dim_reshape.6.send_ref
  99.2 0.6 put.1.put_ref
  99.8 6.9 %all-to-all-done.3.parts_ref = f32[16,13,128]{2,1,0:T(8,128)S(1)} async-done(((f32[16,13,128]{2,1,0:T(8,128)}), f32[16,13,128]{2,1,0:T(8,128)S(1)}, u32[]{:S(2)}, u32[]{:S(2)}) %all-to-all-start.3) | async-done | bytes 106528 | tf_op jit(solution)/shard_map/all_to_all | solution.py:229
  106.7 1.2 %add.34 = f32[400,256]{1,0:T(8,128)} custom-call(s32[1,1,2,2]{3,2,1,0:T(2,128)S(1)} %copy-done, f32[512,256]{1,0:T(8,128)S(1)} %put.1.put_ref, f32[16,13,128]{2,1,0:T(8,128)S(1)} %all-to-all-done.3.parts_ref), custom_call_target="tpu_custom_call" | custom-call | tf_op jit(solution)/shard_map/add/pallas_call | solution.py:281
  (18 shorter events, 0.1 us)
Async XLA Ops:
  2.0 14.2 %copy-start.2 = (s32[1,1,16,32]{3,2,1,0:T(8,128)S(1)}, s32[1,1,16,32]{3,2,1,0:T(8,128)}, u32[]{:S(2)}) copy-start(s32[1,1,16,32]{3,2,1,0:T(8,128)} %param.9) | copy-start | bytes 6148
  2.0 21.8 %all-to-all-start.1 = ((f32[16,16,128]{2,1,0:T(8,128)}), f32[16,16,128]{2,1,0:T(8,128)S(1)}, u32[]{:S(2)}, u32[]{:S(2)}) async-start(f32[16,16,128]{2,1,0:T(8,128)} %negs.1), calls=%async_computation.1 | async-start | bytes 262144 | tf_op jit(solution)/shard_map/all_to_all | solution.py:219
  19.9 12.9 %copy-start.5 = (s32[1,1,2]{2,1,0:T(1,128)S(1)}, s32[1,1,2]{2,1,0:T(1,128)}, u32[]{:S(2)}) copy-start(s32[1,1,2]{2,1,0:T(1,128)} %param.13) | copy-start | bytes 28
  23.9 24.3 %copy-start.4 = (s32[1,1,256]{2,1,0:T(1,128)S(1)}, s32[1,1,256]{2,1,0:T(1,128)}, u32[]{:S(2)}) copy-start(s32[1,1,256]{2,1,0:T(1,128)} %param.10) | copy-start | bytes 3076
  23.9 25.2 %copy-start.1 = (f32[256,400]{0,1:T(8,128)S(1)}, f32[256,400]{0,1:T(8,128)}, u32[]{:S(2)}) copy-start(f32[256,400]{0,1:T(8,128)} %param.8) | copy-start | bytes 1228804
  23.9 33.7 %all-to-all-start = ((f32[16,104,128]{2,1,0:T(8,128)}), f32[16,104,128]{2,1,0:T(8,128)S(1)}, u32[]{:S(2)}, u32[]{:S(2)}) async-start(f32[16,104,128]{2,1,0:T(8,128)} %pick.1), calls=%async_computation | async-start | bytes 1703936 | tf_op jit(solution)/shard_map/all_to_all | solution.py:256
  32.8 17.6 %collective-permute-start.2 = (f32[16,16,128]{2,1,0:T(8,128)S(1)}, f32[16,16,128]{2,1,0:T(8,128)S(1)}, u32[]{:S(2)}, u32[]{:S(2)}) collective-permute-start(f32[16,16,128]{2,1,0:T(8,128)S(1)} %all-to-all-done.1), channel_id=1, source_target_pairs={{0,63},{1,62},{2,61},{3,60},{4,59},{5,58},{6,57},{7,56},{8,55},{9,... | collective-permute-start | bytes 393224 | tf_op jit(solution)/shard_map/ppermute | solution.py:220
  43.0 14.5 %collective-permute-start = (f32[16,16,128]{2,1,0:T(8,128)S(1)}, f32[16,16,128]{2,1,0:T(8,128)S(1)}, u32[]{:S(2)}, u32[]{:S(2)}) collective-permute-start(f32[16,16,128]{2,1,0:T(8,128)S(1)} %all-to-all-done.1), channel_id=1, source_target_pairs={{0,7},{1,6},{2,5},{3,4},{4,3},{5,2},{6,1},{7,0},{8,15},{9,14},{10,... | collective-permute-start | bytes 393224 | tf_op jit(solution)/shard_map/ppermute | solution.py:220
  44.9 12.6 %collective-permute-start.1 = (f32[16,16,128]{2,1,0:T(8,128)S(1)}, f32[16,16,128]{2,1,0:T(8,128)S(1)}, u32[]{:S(2)}, u32[]{:S(2)}) collective-permute-start(f32[16,16,128]{2,1,0:T(8,128)S(1)} %all-to-all-done.1), channel_id=1, source_target_pairs={{0,56},{1,57},{2,58},{3,59},{4,60},{5,61},{6,62},{7,63},{8,48},{9,... | collective-permute-start | bytes 393224 | tf_op jit(solution)/shard_map/ppermute | solution.py:220
  48.2 0.7 copy-start.3
  61.7 31.3 %all-to-all-start.2 = ((f32[16,104,128]{2,1,0:T(8,128)}), f32[16,104,128]{2,1,0:T(8,128)S(1)}, u32[]{:S(2)}, u32[]{:S(2)}) async-start(f32[16,104,128]{2,1,0:T(8,128)} %get-tuple-element.7), calls=%async_computation.2 | async-start | bytes 1703936 | tf_op jit(solution)/shard_map/all_to_all | solution.py:272
  69.0 12.0 %collective-permute-start.3 = (f32[208,128]{1,0:T(8,128)S(1)}, f32[208,128]{1,0:T(8,128)S(1)}, u32[]{:S(2)}, u32[]{:S(2)}) collective-permute-start(f32[208,128]{1,0:T(8,128)S(1)} %get-tuple-element.11), channel_id=1, source_target_pairs={{0,63},{1,62},{2,61},{3,60},{4,59},{5,58},{6,57},{7,56},{8,55},{9,... | collective-permute-start | bytes 319496 | tf_op jit(solution)/shard_map/ppermute | solution.py:226
  74.6 11.6 %collective-permute-start.4 = (f32[208,128]{1,0:T(8,128)S(1)}, f32[208,128]{1,0:T(8,128)S(1)}, u32[]{:S(2)}, u32[]{:S(2)}) collective-permute-start(f32[208,128]{1,0:T(8,128)S(1)} %get-tuple-element.9), channel_id=1, source_target_pairs={{0,56},{1,57},{2,58},{3,59},{4,60},{5,61},{6,62},{7,63},{8,48},{9,... | collective-permute-start | bytes 319496 | tf_op jit(solution)/shard_map/ppermute | solution.py:226
  77.9 8.2 %collective-permute-start.5 = (f32[208,128]{1,0:T(8,128)S(1)}, f32[208,128]{1,0:T(8,128)S(1)}, u32[]{:S(2)}, u32[]{:S(2)}) collective-permute-start(f32[208,128]{1,0:T(8,128)S(1)} %get-tuple-element.10), channel_id=1, source_target_pairs={{0,7},{1,6},{2,5},{3,4},{4,3},{5,2},{6,1},{7,0},{8,15},{9,14},{10,... | collective-permute-start | bytes 319496 | tf_op jit(solution)/shard_map/ppermute | solution.py:226
  93.0 13.7 %all-to-all-start.3 = ((f32[16,13,128]{2,1,0:T(8,128)}), f32[16,13,128]{2,1,0:T(8,128)S(1)}, u32[]{:S(2)}, u32[]{:S(2)}) async-start(f32[16,13,128]{2,1,0:T(8,128)} %reshape.56), calls=%async_computation.3 | async-start | bytes 262144 | tf_op jit(solution)/shard_map/all_to_all | solution.py:229
  99.2 7.5 %copy-start = (s32[1,1,2,2]{3,2,1,0:T(2,128)S(1)}, s32[1,1,2,2]{3,2,1,0:T(2,128)}, u32[]{:S(2)}) copy-start(s32[1,1,2,2]{3,2,1,0:T(2,128)} %neg_ref.3) | copy-start | bytes 52

commit v7 on v6

--- a/solution.py
+++ b/solution.py
@@ -98,9 +98,14 @@
     for n in range(4):
         hit = jnp.where((place == n) & (entity == own_row(neg_ref, n)), 1.0, hit)
     rows = select_columns(hit.astype(jnp.bfloat16), table[...], 3)
-    for j in range(CHUNKS):
+    for j in range(CHUNKS - 1):
         part = rows[:4, j * LANES : (j + 1) * LANES]
         out_ref[:, j * 4 : j * 4 + 4, :] = jnp.broadcast_to(part, (out_ref.shape[0], 4, LANES))
+    last = rows[:, (CHUNKS - 1) * LANES :]
+    tail = last[:1]
+    for n in range(1, 4):
+        tail = tail + pltpu.roll(last, TAIL * n, 1)[n : n + 1]
+    out_ref[:, UNIT - 1 : UNIT, :] = jnp.broadcast_to(tail, (out_ref.shape[0], 1, LANES))
 
 
 def pick_kernel(send_ref, table_ref, rows_ref, table):
@@ -115,15 +120,20 @@
     edges = ends // 2
     blocks = rel_ref.shape[0]
     block = edges // blocks
-    owners = negs_ref.shape[0] // 16
+    owners = negs_ref.shape[0] // UNIT
+    tails = negs_ref[pl.ds(UNIT - 1, owners, stride=UNIT), :]
+    live = lax.broadcasted_iota(jnp.int32, tails.shape, 1) < TAIL
     tail = jnp.zeros((owners, LANES), jnp.float32)
     picked = select_rows(onehot_of(col_ref[...], (ends, slots), 1), rows[...], 3)
     for c in range(blocks):
         for k in range(2):
-            for j in range(CHUNKS):
+            n = c * 2 + k
+            for j in range(CHUNKS - 1):
                 negs[k * owners : (k + 1) * owners, j * LANES : (j + 1) * LANES] = negs_ref[
-                    pl.ds(j * 4 + c * 2 + k, owners, stride=16), :
+                    pl.ds(j * 4 + n, owners, stride=UNIT), :
                 ]
+            turned = pltpu.roll(tails, LANES - TAIL * n, 1) if n else tails
+            negs[k * owners : (k + 1) * owners, (CHUNKS - 1) * LANES :] = jnp.where(live, turned, 0.0)
         negatives = negs[...]
         relation = rel_ref[c : c + 1, :]
         query = picked[c * block : (c + 1) * block] * relation
@@ -214,10 +224,11 @@
     return groups, [mirror(False, True), mirror(True, False), mirror(True, True)]
 
 
-def gather_columns(x, columns):
+def gather_columns(x, columns, later):
     groups, mirrors = quarters(columns)
     x = lax.all_to_all(x, "bucket", split_axis=0, concat_axis=0, axis_index_groups=groups, tiled=True)
-    return jnp.stack([x] + [lax.ppermute(x, "bucket", pairs) for pairs in mirrors])
+    x, later = lax.optimization_barrier((x.reshape(len(groups[0]) * UNIT, LANES), later))
+    return jnp.stack([x] + [lax.ppermute(x, "bucket", pairs) for pairs in mirrors]), later
 
 
 def sum_columns(x, columns):
@@ -238,7 +249,7 @@
     table = emb_table.T
     own_negs = pl.pallas_call(
         negs_kernel,
-        out_shape=shaped(columns // 4, 16, LANES),
+        out_shape=shaped(columns // 4, UNIT, LANES),
         in_specs=[VMEM, VMEM],
         out_specs=VMEM,
         scratch_shapes=[in_vmem(WIDE, entities)],
@@ -251,11 +262,11 @@
         out_specs=VMEM,
         scratch_shapes=[in_vmem(WIDE, entities)],
         name="pick",
-    )(send[:, None], table)
-    negs = gather_columns(own_negs, columns)
+    )(near(send[:, None]), near(table))
+    negs, (sources, targets, kinds) = gather_columns(own_negs, columns, (src_slot, dst_slot, block_rel))
     got = lax.all_to_all(picked, "dom", split_axis=0, concat_axis=0, tiled=True)
-    ends = jnp.concatenate([src_slot.reshape(-1), dst_slot.reshape(-1)])
-    relation = jnp.pad(rel_diag[block_rel.reshape(-1)], ((0, 0), (0, WIDE - width)))
+    ends = jnp.concatenate([sources.reshape(-1), targets.reshape(-1)])
+    relation = jnp.pad(rel_diag[kinds.reshape(-1)], ((0, 0), (0, WIDE - width)))
     back, negs_back = pl.pallas_call(
         grad_kernel,
         out_shape=(shaped(*packed), in_vmem(columns * UNIT, LANES)),
@@ -267,7 +278,7 @@
             in_vmem(ends.shape[0], WIDE),
         ],
         name="grad",
-    )(near(ends[:, None]), near(ends[None, :]), near(relation), near(got), near(negs.reshape(columns * 16, LANES)))
+    )(near(ends[:, None]), near(ends[None, :]), near(relation), near(got), near(negs.reshape(columns * UNIT, LANES)))
     own_grad = sum_columns(negs_back, columns)
     returned = lax.all_to_all(back, "dom", split_axis=0, concat_axis=0, tiled=True)
     put = pl.pallas_call(

time: 109 us -> 107 us (0.982)
  waiting for transfers between devices: 30.9 us -> 29.3 us
  starting transfers between devices: 62.7 us -> 64.2 us
    ppermute x3, waiting for transfers between devices: 7.64 us -> 4.71 us  [gather_columns(): lax.ppermute(x, 'bucket', pairs)]
    ppermute x3, starting transfers between devices: 10.8 us -> 13.2 us  [sum_columns(): lax.ppermute(x[i], 'bucket', mirrors[i - 1])]
    all_to_all x1, waiting for transfers between devices: 6.1 us -> 3.84 us  [on_device(): lax.all_to_all(back, 'dom', split_axis=0, concat_axis=0, tiled=True)]
    all_to_all x1, waiting for transfers between devices: 4.01 us -> 5.77 us  [gather_columns(): lax.all_to_all(x, 'bucket', split_axis=0, concat_axis=0, axis_index_group...]
    all_to_all x1, waiting for transfers between devices: 0.01 us -> 1.64 us  [on_device(): got = lax.all_to_all(picked, 'dom', split_axis=0, concat_axis=0, tiled=True)]
    all_to_all x1, starting transfers between devices: 7.34 us -> 5.7 us  [on_device(): lax.all_to_all(back, 'dom', split_axis=0, concat_axis=0, tiled=True)]
  transfers between devices with their start and end apart: 10 -> 10, of which waited for: 7 -> 7; matrix products, arithmetic and copies ran while one was open for 3% -> 2% of each run, Pallas kernels for 3% -> 2%
where the time goes in v7:
time: 107 us
  starting transfers between devices  64.2 us (60%)
  waiting for transfers between devices  29.3 us (27%)
  Pallas kernels  9.7 us (9%)
  local copies, waits for them, and re-layouts  3.13 us (3%)
    ppermute x3, starting transfers between devices, gather_columns(): lax.ppermute(x, 'bucket', pairs)  15.4 us
    all_to_all x1, starting transfers between devices, gather_columns(): lax.all_to_all(x, 'bucket', split_axis=0, concat_axis=0, axis_index_group...  14.2 us
    ppermute x3, starting transfers between devices, sum_columns(): lax.ppermute(x[i], 'bucket', mirrors[i - 1])  13.2 us
    all_to_all x1, starting transfers between devices, on_device(): got = lax.all_to_all(picked, 'dom', split_axis=0, concat_axis=0, tiled=True)  8.77 us
    all_to_all x1, waiting for transfers between devices, sum_columns(): lax.all_to_all(x, 'bucket', split_axis=0, concat_axis=0, axis_index_group...  7.16 us
    all_to_all x1, starting transfers between devices, sum_columns(): lax.all_to_all(x, 'bucket', split_axis=0, concat_axis=0, axis_index_group...  6.97 us
    ppermute x3, waiting for transfers between devices, sum_columns(): lax.ppermute(x[i], 'bucket', mirrors[i - 1])  6.2 us
    all_to_all x1, waiting for transfers between devices, gather_columns(): lax.all_to_all(x, 'bucket', split_axis=0, concat_axis=0, axis_index_group...  5.77 us
  transfers between devices with their start and end apart: 10, of which 7 were waited for; matrix products, arithmetic and copies ran while one was open for 2% of the time, Pallas kernels for 2%

profile of v7, /device:TPU:1, one launch (start us, length us, event | category | flops | bytes accessed | tf_op | source)
XLA Modules:
  0.0 106.6 jit_solution(12392394244867693802)
XLA Ops:
  0.0 2.1 %negs.1 = f32[16,13,128]{2,1,0:T(8,128)} custom-call(s32[1,1,2,2]{3,2,1,0:T(2,128)} %neg_ref.3, f32[400,256]{1,0:T(8,128)} %bitcast.20), custom_call_target="tpu_custom_call" | custom-call | tf_op jit(solution)/shard_map/negs/pallas_call | solution.py:250
  2.1 14.2 %all-to-all-start = ((f32[16,13,128]{2,1,0:T(8,128)}), f32[16,13,128]{2,1,0:T(8,128)S(1)}, u32[]{:S(2)}, u32[]{:S(2)}) async-start(f32[16,13,128]{2,1,0:T(8,128)} %negs.1), calls=%async_computation | async-start | bytes 262144 | tf_op jit(solution)/shard_map/all_to_all | solution.py:229
  16.3 0.3 broadcast_in_dim_reshape.8.send_ref
  16.6 1.6 %pick.1 = f32[16,104,128]{2,1,0:T(8,128)} custom-call(s32[512,1]{1,0:T(8,128)S(1)} %broadcast_in_dim_reshape.8.send_ref, f32[400,256]{1,0:T(8,128)S(1)} %bitcast.21), custom_call_target="tpu_custom_call" | custom-call | tf_op jit(solution)/shard_map/pick/pallas_call | solution.py:258
  18.2 5.8 %all-to-all-done = f32[16,13,128]{2,1,0:T(8,128)S(1)} async-done(((f32[16,13,128]{2,1,0:T(8,128)}), f32[16,13,128]{2,1,0:T(8,128)S(1)}, u32[]{:S(2)}, u32[]{:S(2)}) %all-to-all-start) | async-done | bytes 106528 | tf_op jit(solution)/shard_map/all_to_all | solution.py:229
  24.0 8.8 %all-to-all-start.1 = ((f32[16,104,128]{2,1,0:T(8,128)}), f32[16,104,128]{2,1,0:T(8,128)S(1)}, u32[]{:S(2)}, u32[]{:S(2)}) async-start(f32[16,104,128]{2,1,0:T(8,128)} %pick.1), calls=%async_computation.1 | async-start | bytes 1703936 | tf_op jit(solution)/shard_map/all_to_all | solution.py:267
  32.7 0.2 copy.9
  32.9 0.0 copy-start.5
  33.0 10.2 %collective-permute-start.2 = (f32[208,128]{1,0:T(8,128)S(1)}, f32[208,128]{1,0:T(8,128)S(1)}, u32[]{:S(2)}, u32[]{:S(2)}) collective-permute-start(f32[208,128]{1,0:T(8,128)S(1)} %reshape.55), channel_id=1, source_target_pairs={{0,63},{1,62},{2,61},{3,60},{4,59},{5,58},{6,57},{7,56},{8,55},{9,... | collective-permute-start | bytes 319496 | tf_op jit(solution)/shard_map/ppermute | solution.py:231
  43.1 1.9 %collective-permute-start = (f32[208,128]{1,0:T(8,128)S(1)}, f32[208,128]{1,0:T(8,128)S(1)}, u32[]{:S(2)}, u32[]{:S(2)}) collective-permute-start(f32[208,128]{1,0:T(8,128)S(1)} %reshape.55), channel_id=1, source_target_pairs={{0,7},{1,6},{2,5},{3,4},{4,3},{5,2},{6,1},{7,0},{8,15},{9,14},{10,... | collective-permute-start | bytes 319496 | tf_op jit(solution)/shard_map/ppermute | solution.py:231
  45.1 3.3 %collective-permute-start.1 = (f32[208,128]{1,0:T(8,128)S(1)}, f32[208,128]{1,0:T(8,128)S(1)}, u32[]{:S(2)}, u32[]{:S(2)}) collective-permute-start(f32[208,128]{1,0:T(8,128)S(1)} %reshape.55), channel_id=1, source_target_pairs={{0,56},{1,57},{2,58},{3,59},{4,60},{5,61},{6,62},{7,63},{8,48},{9,... | collective-permute-start | bytes 319496 | tf_op jit(solution)/shard_map/ppermute | solution.py:231
  48.4 0.0 copy-start.4
  48.4 0.7 copy-done.4
  49.1 0.1 copy.11.col_ref
  49.2 0.5 copy-done.6
  49.7 0.6 gather_fusion
  50.3 4.7 %collective-permute-done = f32[208,128]{1,0:T(8,128)S(1)} collective-permute-done((f32[208,128]{1,0:T(8,128)S(1)}, f32[208,128]{1,0:T(8,128)S(1)}, u32[]{:S(2)}, u32[]{:S(2)}) %collective-permute-start) | collective-permute-done | bytes 106528 | tf_op jit(solution)/shard_map/ppermute | solution.py:231
  55.1 1.6 %all-to-all-done.1.got_ref = f32[16,104,128]{2,1,0:T(8,128)S(1)} async-done(((f32[16,104,128]{2,1,0:T(8,128)}), f32[16,104,128]{2,1,0:T(8,128)S(1)}, u32[]{:S(2)}, u32[]{:S(2)}) %all-to-all-start.1) | async-done | bytes 852000 | tf_op jit(solution)/shard_map/all_to_all | solution.py:267
  56.7 4.2 %grad.1 = (f32[16,104,128]{2,1,0:T(8,128)}, f32[832,128]{1,0:T(8,128)S(1)}) custom-call(s32[512,1]{1,0:T(8,128)S(1)} %copy.11.col_ref, s32[1,512]{1,0:T(1,128)S(1)} %bitcast.23, f32[2,512]{1,0:T(2,128)S(1)} %pad.4.rel_ref, f32[16,104,128]{2,1,0:T(8,128)S(1)} %all-to-all-done.1.got_ref, f32[832,128]{1,0:T(8,128)S(1)} %bitcast.19), custom_call_target="tpu_custom_call" | custom-call | tf_op jit(solution)/shard_map/grad/pallas_call | solution.py:270
  60.9 5.7 %all-to-all-start.2 = ((f32[16,104,128]{2,1,0:T(8,128)}), f32[16,104,128]{2,1,0:T(8,128)S(1)}, u32[]{:S(2)}, u32[]{:S(2)}) async-start(f32[16,104,128]{2,1,0:T(8,128)} %get-tuple-element.15), calls=%async_computation.2 | async-start | bytes 1703936 | tf_op jit(solution)/shard_map/all_to_all | solution.py:283
  66.7 8.0 %collective-permute-start.3 = (f32[208,128]{1,0:T(8,128)S(1)}, f32[208,128]{1,0:T(8,128)S(1)}, u32[]{:S(2)}, u32[]{:S(2)}) collective-permute-start(f32[208,128]{1,0:T(8,128)S(1)} %get-tuple-element.19), channel_id=1, source_target_pairs={{0,63},{1,62},{2,61},{3,60},{4,59},{5,58},{6,57},{7,56},{8,55},{9,... | collective-permute-start | bytes 319496 | tf_op jit(solution)/shard_map/ppermute | solution.py:237
  74.6 3.3 %collective-permute-start.4 = (f32[208,128]{1,0:T(8,128)S(1)}, f32[208,128]{1,0:T(8,128)S(1)}, u32[]{:S(2)}, u32[]{:S(2)}) collective-permute-start(f32[208,128]{1,0:T(8,128)S(1)} %get-tuple-element.17), channel_id=1, source_target_pairs={{0,56},{1,57},{2,58},{3,59},{4,60},{5,61},{6,62},{7,63},{8,48},{9,... | collective-permute-start | bytes 319496 | tf_op jit(solution)/shard_map/ppermute | solution.py:237
  77.9 1.9 %collective-permute-start.5 = (f32[208,128]{1,0:T(8,128)S(1)}, f32[208,128]{1,0:T(8,128)S(1)}, u32[]{:S(2)}, u32[]{:S(2)}) collective-permute-start(f32[208,128]{1,0:T(8,128)S(1)} %get-tuple-element.18), channel_id=1, source_target_pairs={{0,7},{1,6},{2,5},{3,4},{4,3},{5,2},{6,1},{7,0},{8,15},{9,14},{10,... | collective-permute-start | bytes 319496 | tf_op jit(solution)/shard_map/ppermute | solution.py:237
  79.9 0.5 collective-permute-done.3
  80.4 5.7 %collective-permute-done.4 = f32[208,128]{1,0:T(8,128)S(1)} collective-permute-done((f32[208,128]{1,0:T(8,128)S(1)}, f32[208,128]{1,0:T(8,128)S(1)}, u32[]{:S(2)}, u32[]{:S(2)}) %collective-permute-start.4) | collective-permute-done | bytes 106528 | tf_op jit(solution)/shard_map/ppermute | solution.py:237
  86.1 0.7 reshape.60
  86.8 3.8 %all-to-all-done.2.got_ref = f32[16,104,128]{2,1,0:T(8,128)S(1)} async-done(((f32[16,104,128]{2,1,0:T(8,128)}), f32[16,104,128]{2,1,0:T(8,128)S(1)}, u32[]{:S(2)}, u32[]{:S(2)}) %all-to-all-start.2) | async-done | bytes 852000 | tf_op jit(solution)/shard_map/all_to_all | solution.py:283
  90.6 7.0 %all-to-all-start.3 = ((f32[16,13,128]{2,1,0:T(8,128)}), f32[16,13,128]{2,1,0:T(8,128)S(1)}, u32[]{:S(2)}, u32[]{:S(2)}) async-start(f32[16,13,128]{2,1,0:T(8,128)} %reshape.60), calls=%async_computation.3 | async-start | bytes 262144 | tf_op jit(solution)/shard_map/all_to_all | solution.py:240
  97.6 0.1 broadcast_in_dim_reshape.6.send_ref
  97.7 0.6 put.1.put_ref
  98.3 7.2 %all-to-all-done.3.parts_ref = f32[16,13,128]{2,1,0:T(8,128)S(1)} async-done(((f32[16,13,128]{2,1,0:T(8,128)}), f32[16,13,128]{2,1,0:T(8,128)S(1)}, u32[]{:S(2)}, u32[]{:S(2)}) %all-to-all-start.3) | async-done | bytes 106528 | tf_op jit(solution)/shard_map/all_to_all | solution.py:240
  105.4 1.2 %add.34 = f32[400,256]{1,0:T(8,128)} custom-call(s32[1,1,2,2]{3,2,1,0:T(2,128)S(1)} %copy-done.1, f32[512,256]{1,0:T(8,128)S(1)} %put.1.put_ref, f32[16,13,128]{2,1,0:T(8,128)S(1)} %all-to-all-done.3.parts_ref), custom_call_target="tpu_custom_call" | custom-call | tf_op jit(solution)/shard_map/add/pallas_call | solution.py:292
  (21 shorter events, 0.1 us)
Async XLA Ops:
  0.0 16.6 %copy-start = (f32[256,400]{0,1:T(8,128)S(1)}, f32[256,400]{0,1:T(8,128)}, u32[]{:S(2)}) copy-start(f32[256,400]{0,1:T(8,128)} %param.7) | copy-start | bytes 1228804
  2.1 14.2 %copy-start.3 = (s32[1,1,16,32]{3,2,1,0:T(8,128)S(1)}, s32[1,1,16,32]{3,2,1,0:T(8,128)}, u32[]{:S(2)}) copy-start(s32[1,1,16,32]{3,2,1,0:T(8,128)} %param.9) | copy-start | bytes 6148
  2.1 21.8 %all-to-all-start = ((f32[16,13,128]{2,1,0:T(8,128)}), f32[16,13,128]{2,1,0:T(8,128)S(1)}, u32[]{:S(2)}, u32[]{:S(2)}) async-start(f32[16,13,128]{2,1,0:T(8,128)} %negs.1), calls=%async_computation | async-start | bytes 262144 | tf_op jit(solution)/shard_map/all_to_all | solution.py:229
  18.2 14.5 %copy-start.2 = (f32[256,400]{0,1:T(8,128)S(1)}, f32[256,400]{0,1:T(8,128)}, u32[]{:S(2)}) copy-start(f32[256,400]{0,1:T(8,128)} %param.8) | copy-start | bytes 1228804
  24.0 32.7 %all-to-all-start.1 = ((f32[16,104,128]{2,1,0:T(8,128)}), f32[16,104,128]{2,1,0:T(8,128)S(1)}, u32[]{:S(2)}, u32[]{:S(2)}) async-start(f32[16,104,128]{2,1,0:T(8,128)} %pick.1), calls=%async_computation.1 | async-start | bytes 1703936 | tf_op jit(solution)/shard_map/all_to_all | solution.py:267
  32.9 15.5 %copy-start.5 = (s32[1,1,256]{2,1,0:T(1,128)S(1)}, s32[1,1,256]{2,1,0:T(1,128)}, u32[]{:S(2)}) copy-start(s32[1,1,256]{2,1,0:T(1,128)} %param.10) | copy-start | bytes 3076
  33.0 17.3 %collective-permute-start.2 = (f32[208,128]{1,0:T(8,128)S(1)}, f32[208,128]{1,0:T(8,128)S(1)}, u32[]{:S(2)}, u32[]{:S(2)}) collective-permute-start(f32[208,128]{1,0:T(8,128)S(1)} %reshape.55), channel_id=1, source_target_pairs={{0,63},{1,62},{2,61},{3,60},{4,59},{5,58},{6,57},{7,56},{8,55},{9,... | collective-permute-start | bytes 319496 | tf_op jit(solution)/shard_map/ppermute | solution.py:231
  43.1 11.9 %collective-permute-start = (f32[208,128]{1,0:T(8,128)S(1)}, f32[208,128]{1,0:T(8,128)S(1)}, u32[]{:S(2)}, u32[]{:S(2)}) collective-permute-start(f32[208,128]{1,0:T(8,128)S(1)} %reshape.55), channel_id=1, source_target_pairs={{0,7},{1,6},{2,5},{3,4},{4,3},{5,2},{6,1},{7,0},{8,15},{9,14},{10,... | collective-permute-start | bytes 319496 | tf_op jit(solution)/shard_map/ppermute | solution.py:231
  45.1 10.0 %collective-permute-start.1 = (f32[208,128]{1,0:T(8,128)S(1)}, f32[208,128]{1,0:T(8,128)S(1)}, u32[]{:S(2)}, u32[]{:S(2)}) collective-permute-start(f32[208,128]{1,0:T(8,128)S(1)} %reshape.55), channel_id=1, source_target_pairs={{0,56},{1,57},{2,58},{3,59},{4,60},{5,61},{6,62},{7,63},{8,48},{9,... | collective-permute-start | bytes 319496 | tf_op jit(solution)/shard_map/ppermute | solution.py:231
  48.4 0.7 copy-start.4
  49.1 0.7 copy-start.6
  60.9 29.7 %all-to-all-start.2 = ((f32[16,104,128]{2,1,0:T(8,128)}), f32[16,104,128]{2,1,0:T(8,128)S(1)}, u32[]{:S(2)}, u32[]{:S(2)}) async-start(f32[16,104,128]{2,1,0:T(8,128)} %get-tuple-element.15), calls=%async_computation.2 | async-start | bytes 1703936 | tf_op jit(solution)/shard_map/all_to_all | solution.py:283
  66.7 13.8 %collective-permute-start.3 = (f32[208,128]{1,0:T(8,128)S(1)}, f32[208,128]{1,0:T(8,128)S(1)}, u32[]{:S(2)}, u32[]{:S(2)}) collective-permute-start(f32[208,128]{1,0:T(8,128)S(1)} %get-tuple-element.19), channel_id=1, source_target_pairs={{0,63},{1,62},{2,61},{3,60},{4,59},{5,58},{6,57},{7,56},{8,55},{9,... | collective-permute-start | bytes 319496 | tf_op jit(solution)/shard_map/ppermute | solution.py:237
  74.6 11.4 %collective-permute-start.4 = (f32[208,128]{1,0:T(8,128)S(1)}, f32[208,128]{1,0:T(8,128)S(1)}, u32[]{:S(2)}, u32[]{:S(2)}) collective-permute-start(f32[208,128]{1,0:T(8,128)S(1)} %get-tuple-element.17), channel_id=1, source_target_pairs={{0,56},{1,57},{2,58},{3,59},{4,60},{5,61},{6,62},{7,63},{8,48},{9,... | collective-permute-start | bytes 319496 | tf_op jit(solution)/shard_map/ppermute | solution.py:237
  77.9 8.1 %collective-permute-start.5 = (f32[208,128]{1,0:T(8,128)S(1)}, f32[208,128]{1,0:T(8,128)S(1)}, u32[]{:S(2)}, u32[]{:S(2)}) collective-permute-start(f32[208,128]{1,0:T(8,128)S(1)} %get-tuple-element.18), channel_id=1, source_target_pairs={{0,7},{1,6},{2,5},{3,4},{4,3},{5,2},{6,1},{7,0},{8,15},{9,14},{10,... | collective-permute-start | bytes 319496 | tf_op jit(solution)/shard_map/ppermute | solution.py:237
  90.6 14.8 %all-to-all-start.3 = ((f32[16,13,128]{2,1,0:T(8,128)}), f32[16,13,128]{2,1,0:T(8,128)S(1)}, u32[]{:S(2)}, u32[]{:S(2)}) async-start(f32[16,13,128]{2,1,0:T(8,128)} %reshape.60), calls=%async_computation.3 | async-start | bytes 262144 | tf_op jit(solution)/shard_map/all_to_all | solution.py:240
  97.7 7.7 %copy-start.1 = (s32[1,1,2,2]{3,2,1,0:T(2,128)S(1)}, s32[1,1,2,2]{3,2,1,0:T(2,128)}, u32[]{:S(2)}) copy-start(s32[1,1,2,2]{3,2,1,0:T(2,128)} %neg_ref.3) | copy-start | bytes 52

commit v8 on v7

--- a/solution.py
+++ b/solution.py
@@ -12,7 +12,6 @@
 TAIL = 16
 WIDE = CHUNKS * LANES
 UNIT = 13
-HIGHEST = lax.Precision.HIGHEST
 VMEM = pl.BlockSpec(memory_space=pltpu.VMEM)
 
 
@@ -33,10 +32,16 @@
     return total
 
 
-def product(a, b):
-    (a_high, a_low), (b_high, b_low) = split(a, 2), split(b, 2)
-    dot = lambda x, y: jnp.dot(x, y, preferred_element_type=jnp.float32)
-    return dot(a_high, b_high) + (dot(a_high, b_low) + dot(a_low, b_high))
+def dot_terms(a, b, contract, pairs):
+    total = None
+    for i, j in pairs:
+        part = lax.dot_general(a[i], b[j], (contract, ((), ())), preferred_element_type=jnp.float32)
+        total = part if total is None else total + part
+    return total
+
+
+NEAR = ((0, 1), (1, 0), (0, 0))
+FULL = ((1, 1), (0, 2), (2, 0), (0, 1), (1, 0), (0, 0))
 
 
 def onehot_of(index, shape, axis):
@@ -129,32 +134,34 @@
         for k in range(2):
             n = c * 2 + k
             for j in range(CHUNKS - 1):
-                negs[k * owners : (k + 1) * owners, j * LANES : (j + 1) * LANES] = negs_ref[
+                negs[c, k * owners : (k + 1) * owners, j * LANES : (j + 1) * LANES] = negs_ref[
                     pl.ds(j * 4 + n, owners, stride=UNIT), :
                 ]
             turned = pltpu.roll(tails, LANES - TAIL * n, 1) if n else tails
-            negs[k * owners : (k + 1) * owners, (CHUNKS - 1) * LANES :] = jnp.where(live, turned, 0.0)
-        negatives = negs[...]
-        relation = rel_ref[c : c + 1, :]
-        query = picked[c * block : (c + 1) * block] * relation
-        target = picked[edges + c * block : edges + (c + 1) * block]
-        positive = jnp.sum(query * target, axis=1, keepdims=True)
-        scores = lax.dot_general(
-            query, negatives, (((1,), (1,)), ((), ())), precision=HIGHEST, preferred_element_type=jnp.float32
-        )
-        largest = jnp.maximum(jnp.max(scores, axis=1, keepdims=True), positive)
-        pos_exp = jnp.exp(positive - largest)
-        neg_exp = jnp.exp(scores - largest)
-        total = pos_exp + jnp.sum(neg_exp, axis=1, keepdims=True)
-        pos_weight = pos_exp / total - 1.0
-        weight = neg_exp / total
-        query_grad = pos_weight * target + product(weight, negatives)
-        grads[c * block : (c + 1) * block, :] = query_grad * relation
-        grads[edges + c * block : edges + (c + 1) * block, :] = pos_weight * query
-        neg_grad = product(weight.T, query)
+            negs[c, k * owners : (k + 1) * owners, (CHUNKS - 1) * LANES :] = jnp.where(live, turned, 0.0)
+    every = range(blocks)
+    relation = [rel_ref[c : c + 1, :] for c in every]
+    query = [picked[c * block : (c + 1) * block] * relation[c] for c in every]
+    target = [picked[edges + c * block : edges + (c + 1) * block] for c in every]
+    query_terms = [split(query[c], 3) for c in every]
+    negative_terms = [split(negs[c], 3) for c in every]
+    scores = [dot_terms(query_terms[c], negative_terms[c], ((1,), (1,)), FULL) for c in every]
+    positive = [jnp.sum(query[c] * target[c], axis=1, keepdims=True) for c in every]
+    largest = [jnp.maximum(jnp.max(scores[c], axis=1, keepdims=True), positive[c]) for c in every]
+    pos_exp = [jnp.exp(positive[c] - largest[c]) for c in every]
+    neg_exp = [jnp.exp(scores[c] - largest[c]) for c in every]
+    total = [pos_exp[c] + jnp.sum(neg_exp[c], axis=1, keepdims=True) for c in every]
+    pos_weight = [pos_exp[c] / total[c] - 1.0 for c in every]
+    weight = [neg_exp[c] / total[c] for c in every]
+    pulled = [dot_terms(split(weight[c], 2), negative_terms[c], ((1,), (0,)), NEAR) for c in every]
+    pushed = [dot_terms(split(weight[c].T, 2), query_terms[c], ((1,), (0,)), NEAR) for c in every]
+    for c in every:
+        grads[c * block : (c + 1) * block, :] = (pos_weight[c] * target[c] + pulled[c]) * relation[c]
+        grads[edges + c * block : edges + (c + 1) * block, :] = pos_weight[c] * query[c]
+    for c in every:
         for k in range(2):
             n = c * 2 + k
-            part = neg_grad[k * owners : (k + 1) * owners]
+            part = pushed[c][k * owners : (k + 1) * owners]
             for j in range(CHUNKS - 1):
                 negs_back_ref[pl.ds(j * 4 + n, owners, stride=UNIT), :] = part[:, j * LANES : (j + 1) * LANES]
             last = part[:, (CHUNKS - 1) * LANES :]
@@ -274,7 +281,7 @@
         out_specs=(VMEM, VMEM),
         scratch_shapes=[
             in_vmem(owners * slots, WIDE),
-            in_vmem(2 * columns, WIDE),
+            in_vmem(block_rel.shape[2], 2 * columns, WIDE),
             in_vmem(ends.shape[0], WIDE),
         ],
         name="grad",

time: 107 us -> 107 us (level)
  no operation moved by 1% of the time
where the time goes in v8:
time: 107 us; the launch traced here: 106 us
  starting transfers between devices  64.2 us (60%)
  waiting for transfers between devices  29.3 us (27%)
  Pallas kernels  9.26 us (9%)
  local copies, waits for them, and re-layouts  3.13 us (3%)
    ppermute x3, starting transfers between devices, gather_columns(): lax.ppermute(x, 'bucket', pairs)  15.4 us
    all_to_all x1, starting transfers between devices, gather_columns(): lax.all_to_all(x, 'bucket', split_axis=0, concat_axis=0, axis_index_group...  14.2 us
    ppermute x3, starting transfers between devices, sum_columns(): lax.ppermute(x[i], 'bucket', mirrors[i - 1])  13.2 us
    all_to_all x1, starting transfers between devices, on_device(): got = lax.all_to_all(picked, 'dom', split_axis=0, concat_axis=0, tiled=True)  8.77 us
    all_to_all x1, waiting for transfers between devices, sum_columns(): lax.all_to_all(x, 'bucket', split_axis=0, concat_axis=0, axis_index_group...  7.16 us
    all_to_all x1, starting transfers between devices, sum_columns(): lax.all_to_all(x, 'bucket', split_axis=0, concat_axis=0, axis_index_group...  6.96 us
    ppermute x3, waiting for transfers between devices, sum_columns(): lax.ppermute(x[i], 'bucket', mirrors[i - 1])  6.18 us
    all_to_all x1, waiting for transfers between devices, gather_columns(): lax.all_to_all(x, 'bucket', split_axis=0, concat_axis=0, axis_index_group...  5.77 us
  transfers between devices with their start and end apart: 10, of which 7 were waited for; matrix products, arithmetic and copies ran while one was open for 2% of the time, Pallas kernels for 2%

profile of v8, /device:TPU:1, one launch (start us, length us, event | category | flops | bytes accessed | tf_op | source)
XLA Modules:
  0.0 106.2 jit_solution(17477605936545859962)
XLA Ops:
  0.0 2.1 %negs.1 = f32[16,13,128]{2,1,0:T(8,128)} custom-call(s32[1,1,2,2]{3,2,1,0:T(2,128)} %neg_ref.3, f32[400,256]{1,0:T(8,128)} %bitcast.20), custom_call_target="tpu_custom_call" | custom-call | tf_op jit(solution)/shard_map/negs/pallas_call | solution.py:257
  2.1 14.2 %all-to-all-start = ((f32[16,13,128]{2,1,0:T(8,128)}), f32[16,13,128]{2,1,0:T(8,128)S(1)}, u32[]{:S(2)}, u32[]{:S(2)}) async-start(f32[16,13,128]{2,1,0:T(8,128)} %negs.1), calls=%async_computation | async-start | bytes 262144 | tf_op jit(solution)/shard_map/all_to_all | solution.py:236
  16.3 0.3 broadcast_in_dim_reshape.8.send_ref
  16.6 1.6 %pick.1 = f32[16,104,128]{2,1,0:T(8,128)} custom-call(s32[512,1]{1,0:T(8,128)S(1)} %broadcast_in_dim_reshape.8.send_ref, f32[400,256]{1,0:T(8,128)S(1)} %bitcast.21), custom_call_target="tpu_custom_call" | custom-call | tf_op jit(solution)/shard_map/pick/pallas_call | solution.py:265
  18.2 5.8 %all-to-all-done = f32[16,13,128]{2,1,0:T(8,128)S(1)} async-done(((f32[16,13,128]{2,1,0:T(8,128)}), f32[16,13,128]{2,1,0:T(8,128)S(1)}, u32[]{:S(2)}, u32[]{:S(2)}) %all-to-all-start) | async-done | bytes 106528 | tf_op jit(solution)/shard_map/all_to_all | solution.py:236
  24.0 8.8 %all-to-all-start.1 = ((f32[16,104,128]{2,1,0:T(8,128)}), f32[16,104,128]{2,1,0:T(8,128)S(1)}, u32[]{:S(2)}, u32[]{:S(2)}) async-start(f32[16,104,128]{2,1,0:T(8,128)} %pick.1), calls=%async_computation.1 | async-start | bytes 1703936 | tf_op jit(solution)/shard_map/all_to_all | solution.py:274
  32.7 0.2 copy.9
  32.9 0.0 copy-start.5
  33.0 10.2 %collective-permute-start.2 = (f32[208,128]{1,0:T(8,128)S(1)}, f32[208,128]{1,0:T(8,128)S(1)}, u32[]{:S(2)}, u32[]{:S(2)}) collective-permute-start(f32[208,128]{1,0:T(8,128)S(1)} %reshape.55), channel_id=1, source_target_pairs={{0,63},{1,62},{2,61},{3,60},{4,59},{5,58},{6,57},{7,56},{8,55},{9,... | collective-permute-start | bytes 319496 | tf_op jit(solution)/shard_map/ppermute | solution.py:238
  43.1 1.9 %collective-permute-start = (f32[208,128]{1,0:T(8,128)S(1)}, f32[208,128]{1,0:T(8,128)S(1)}, u32[]{:S(2)}, u32[]{:S(2)}) collective-permute-start(f32[208,128]{1,0:T(8,128)S(1)} %reshape.55), channel_id=1, source_target_pairs={{0,7},{1,6},{2,5},{3,4},{4,3},{5,2},{6,1},{7,0},{8,15},{9,14},{10,... | collective-permute-start | bytes 319496 | tf_op jit(solution)/shard_map/ppermute | solution.py:238
  45.1 3.3 %collective-permute-start.1 = (f32[208,128]{1,0:T(8,128)S(1)}, f32[208,128]{1,0:T(8,128)S(1)}, u32[]{:S(2)}, u32[]{:S(2)}) collective-permute-start(f32[208,128]{1,0:T(8,128)S(1)} %reshape.55), channel_id=1, source_target_pairs={{0,56},{1,57},{2,58},{3,59},{4,60},{5,61},{6,62},{7,63},{8,48},{9,... | collective-permute-start | bytes 319496 | tf_op jit(solution)/shard_map/ppermute | solution.py:238
  48.4 0.0 copy-start.4
  48.4 0.7 copy-done.4
  49.1 0.1 copy.11.col_ref
  49.2 0.5 copy-done.6
  49.7 0.6 gather_fusion
  50.3 4.7 %collective-permute-done = f32[208,128]{1,0:T(8,128)S(1)} collective-permute-done((f32[208,128]{1,0:T(8,128)S(1)}, f32[208,128]{1,0:T(8,128)S(1)}, u32[]{:S(2)}, u32[]{:S(2)}) %collective-permute-start) | collective-permute-done | bytes 106528 | tf_op jit(solution)/shard_map/ppermute | solution.py:238
  55.1 1.6 %all-to-all-done.1.got_ref = f32[16,104,128]{2,1,0:T(8,128)S(1)} async-done(((f32[16,104,128]{2,1,0:T(8,128)}), f32[16,104,128]{2,1,0:T(8,128)S(1)}, u32[]{:S(2)}, u32[]{:S(2)}) %all-to-all-start.1) | async-done | bytes 852000 | tf_op jit(solution)/shard_map/all_to_all | solution.py:274
  56.7 3.8 %grad.1 = (f32[16,104,128]{2,1,0:T(8,128)}, f32[832,128]{1,0:T(8,128)S(1)}) custom-call(s32[512,1]{1,0:T(8,128)S(1)} %copy.11.col_ref, s32[1,512]{1,0:T(1,128)S(1)} %bitcast.23, f32[2,512]{1,0:T(2,128)S(1)} %pad.4.rel_ref, f32[16,104,128]{2,1,0:T(8,128)S(1)} %all-to-all-done.1.got_ref, f32[832,128]{1,0:T(8,128)S(1)} %bitcast.19), custom_call_target="tpu_custom_call" | custom-call | tf_op jit(solution)/shard_map/grad/pallas_call | solution.py:277
  60.5 5.7 %all-to-all-start.2 = ((f32[16,104,128]{2,1,0:T(8,128)}), f32[16,104,128]{2,1,0:T(8,128)S(1)}, u32[]{:S(2)}, u32[]{:S(2)}) async-start(f32[16,104,128]{2,1,0:T(8,128)} %get-tuple-element.15), calls=%async_computation.2 | async-start | bytes 1703936 | tf_op jit(solution)/shard_map/all_to_all | solution.py:290
  66.2 8.0 %collective-permute-start.3 = (f32[208,128]{1,0:T(8,128)S(1)}, f32[208,128]{1,0:T(8,128)S(1)}, u32[]{:S(2)}, u32[]{:S(2)}) collective-permute-start(f32[208,128]{1,0:T(8,128)S(1)} %get-tuple-element.19), channel_id=1, source_target_pairs={{0,63},{1,62},{2,61},{3,60},{4,59},{5,58},{6,57},{7,56},{8,55},{9,... | collective-permute-start | bytes 319496 | tf_op jit(solution)/shard_map/ppermute | solution.py:244
  74.2 3.3 %collective-permute-start.4 = (f32[208,128]{1,0:T(8,128)S(1)}, f32[208,128]{1,0:T(8,128)S(1)}, u32[]{:S(2)}, u32[]{:S(2)}) collective-permute-start(f32[208,128]{1,0:T(8,128)S(1)} %get-tuple-element.17), channel_id=1, source_target_pairs={{0,56},{1,57},{2,58},{3,59},{4,60},{5,61},{6,62},{7,63},{8,48},{9,... | collective-permute-start | bytes 319496 | tf_op jit(solution)/shard_map/ppermute | solution.py:244
  77.6 1.9 %collective-permute-start.5 = (f32[208,128]{1,0:T(8,128)S(1)}, f32[208,128]{1,0:T(8,128)S(1)}, u32[]{:S(2)}, u32[]{:S(2)}) collective-permute-start(f32[208,128]{1,0:T(8,128)S(1)} %get-tuple-element.18), channel_id=1, source_target_pairs={{0,7},{1,6},{2,5},{3,4},{4,3},{5,2},{6,1},{7,0},{8,15},{9,14},{10,... | collective-permute-start | bytes 319496 | tf_op jit(solution)/shard_map/ppermute | solution.py:244
  79.5 0.5 collective-permute-done.3
  80.0 5.7 %collective-permute-done.4 = f32[208,128]{1,0:T(8,128)S(1)} collective-permute-done((f32[208,128]{1,0:T(8,128)S(1)}, f32[208,128]{1,0:T(8,128)S(1)}, u32[]{:S(2)}, u32[]{:S(2)}) %collective-permute-start.4) | collective-permute-done | bytes 106528 | tf_op jit(solution)/shard_map/ppermute | solution.py:244
  85.7 0.7 reshape.60
  86.4 3.8 %all-to-all-done.2.got_ref = f32[16,104,128]{2,1,0:T(8,128)S(1)} async-done(((f32[16,104,128]{2,1,0:T(8,128)}), f32[16,104,128]{2,1,0:T(8,128)S(1)}, u32[]{:S(2)}, u32[]{:S(2)}) %all-to-all-start.2) | async-done | bytes 852000 | tf_op jit(solution)/shard_map/all_to_all | solution.py:290
  90.2 7.0 %all-to-all-start.3 = ((f32[16,13,128]{2,1,0:T(8,128)}), f32[16,13,128]{2,1,0:T(8,128)S(1)}, u32[]{:S(2)}, u32[]{:S(2)}) async-start(f32[16,13,128]{2,1,0:T(8,128)} %reshape.60), calls=%async_computation.3 | async-start | bytes 262144 | tf_op jit(solution)/shard_map/all_to_all | solution.py:247
  97.2 0.1 broadcast_in_dim_reshape.6.send_ref
  97.2 0.6 put.1.put_ref
  97.8 7.2 %all-to-all-done.3.parts_ref = f32[16,13,128]{2,1,0:T(8,128)S(1)} async-done(((f32[16,13,128]{2,1,0:T(8,128)}), f32[16,13,128]{2,1,0:T(8,128)S(1)}, u32[]{:S(2)}, u32[]{:S(2)}) %all-to-all-start.3) | async-done | bytes 106528 | tf_op jit(solution)/shard_map/all_to_all | solution.py:247
  105.0 1.2 %add.34 = f32[400,256]{1,0:T(8,128)} custom-call(s32[1,1,2,2]{3,2,1,0:T(2,128)S(1)} %copy-done.1, f32[512,256]{1,0:T(8,128)S(1)} %put.1.put_ref, f32[16,13,128]{2,1,0:T(8,128)S(1)} %all-to-all-done.3.parts_ref), custom_call_target="tpu_custom_call" | custom-call | tf_op jit(solution)/shard_map/add/pallas_call | solution.py:299
  (21 shorter events, 0.1 us)
Async XLA Ops:
  0.0 16.6 %copy-start = (f32[256,400]{0,1:T(8,128)S(1)}, f32[256,400]{0,1:T(8,128)}, u32[]{:S(2)}) copy-start(f32[256,400]{0,1:T(8,128)} %param.7) | copy-start | bytes 1228804
  2.1 14.2 %copy-start.3 = (s32[1,1,16,32]{3,2,1,0:T(8,128)S(1)}, s32[1,1,16,32]{3,2,1,0:T(8,128)}, u32[]{:S(2)}) copy-start(s32[1,1,16,32]{3,2,1,0:T(8,128)} %param.9) | copy-start | bytes 6148
  2.1 21.8 %all-to-all-start = ((f32[16,13,128]{2,1,0:T(8,128)}), f32[16,13,128]{2,1,0:T(8,128)S(1)}, u32[]{:S(2)}, u32[]{:S(2)}) async-start(f32[16,13,128]{2,1,0:T(8,128)} %negs.1), calls=%async_computation | async-start | bytes 262144 | tf_op jit(solution)/shard_map/all_to_all | solution.py:236
  18.2 14.5 %copy-start.2 = (f32[256,400]{0,1:T(8,128)S(1)}, f32[256,400]{0,1:T(8,128)}, u32[]{:S(2)}) copy-start(f32[256,400]{0,1:T(8,128)} %param.8) | copy-start | bytes 1228804
  24.0 32.7 %all-to-all-start.1 = ((f32[16,104,128]{2,1,0:T(8,128)}), f32[16,104,128]{2,1,0:T(8,128)S(1)}, u32[]{:S(2)}, u32[]{:S(2)}) async-start(f32[16,104,128]{2,1,0:T(8,128)} %pick.1), calls=%async_computation.1 | async-start | bytes 1703936 | tf_op jit(solution)/shard_map/all_to_all | solution.py:274
  32.9 15.5 %copy-start.5 = (s32[1,1,256]{2,1,0:T(1,128)S(1)}, s32[1,1,256]{2,1,0:T(1,128)}, u32[]{:S(2)}) copy-start(s32[1,1,256]{2,1,0:T(1,128)} %param.10) | copy-start | bytes 3076
  33.0 17.3 %collective-permute-start.2 = (f32[208,128]{1,0:T(8,128)S(1)}, f32[208,128]{1,0:T(8,128)S(1)}, u32[]{:S(2)}, u32[]{:S(2)}) collective-permute-start(f32[208,128]{1,0:T(8,128)S(1)} %reshape.55), channel_id=1, source_target_pairs={{0,63},{1,62},{2,61},{3,60},{4,59},{5,58},{6,57},{7,56},{8,55},{9,... | collective-permute-start | bytes 319496 | tf_op jit(solution)/shard_map/ppermute | solution.py:238
  43.1 11.9 %collective-permute-start = (f32[208,128]{1,0:T(8,128)S(1)}, f32[208,128]{1,0:T(8,128)S(1)}, u32[]{:S(2)}, u32[]{:S(2)}) collective-permute-start(f32[208,128]{1,0:T(8,128)S(1)} %reshape.55), channel_id=1, source_target_pairs={{0,7},{1,6},{2,5},{3,4},{4,3},{5,2},{6,1},{7,0},{8,15},{9,14},{10,... | collective-permute-start | bytes 319496 | tf_op jit(solution)/shard_map/ppermute | solution.py:238
  45.1 10.0 %collective-permute-start.1 = (f32[208,128]{1,0:T(8,128)S(1)}, f32[208,128]{1,0:T(8,128)S(1)}, u32[]{:S(2)}, u32[]{:S(2)}) collective-permute-start(f32[208,128]{1,0:T(8,128)S(1)} %reshape.55), channel_id=1, source_target_pairs={{0,56},{1,57},{2,58},{3,59},{4,60},{5,61},{6,62},{7,63},{8,48},{9,... | collective-permute-start | bytes 319496 | tf_op jit(solution)/shard_map/ppermute | solution.py:238
  48.4 0.7 copy-start.4
  49.1 0.7 copy-start.6
  60.5 29.7 %all-to-all-start.2 = ((f32[16,104,128]{2,1,0:T(8,128)}), f32[16,104,128]{2,1,0:T(8,128)S(1)}, u32[]{:S(2)}, u32[]{:S(2)}) async-start(f32[16,104,128]{2,1,0:T(8,128)} %get-tuple-element.15), calls=%async_computation.2 | async-start | bytes 1703936 | tf_op jit(solution)/shard_map/all_to_all | solution.py:290
  66.2 13.7 %collective-permute-start.3 = (f32[208,128]{1,0:T(8,128)S(1)}, f32[208,128]{1,0:T(8,128)S(1)}, u32[]{:S(2)}, u32[]{:S(2)}) collective-permute-start(f32[208,128]{1,0:T(8,128)S(1)} %get-tuple-element.19), channel_id=1, source_target_pairs={{0,63},{1,62},{2,61},{3,60},{4,59},{5,58},{6,57},{7,56},{8,55},{9,... | collective-permute-start | bytes 319496 | tf_op jit(solution)/shard_map/ppermute | solution.py:244
  74.2 11.5 %collective-permute-start.4 = (f32[208,128]{1,0:T(8,128)S(1)}, f32[208,128]{1,0:T(8,128)S(1)}, u32[]{:S(2)}, u32[]{:S(2)}) collective-permute-start(f32[208,128]{1,0:T(8,128)S(1)} %get-tuple-element.17), channel_id=1, source_target_pairs={{0,56},{1,57},{2,58},{3,59},{4,60},{5,61},{6,62},{7,63},{8,48},{9,... | collective-permute-start | bytes 319496 | tf_op jit(solution)/shard_map/ppermute | solution.py:244
  77.6 8.1 %collective-permute-start.5 = (f32[208,128]{1,0:T(8,128)S(1)}, f32[208,128]{1,0:T(8,128)S(1)}, u32[]{:S(2)}, u32[]{:S(2)}) collective-permute-start(f32[208,128]{1,0:T(8,128)S(1)} %get-tuple-element.18), channel_id=1, source_target_pairs={{0,7},{1,6},{2,5},{3,4},{4,3},{5,2},{6,1},{7,0},{8,15},{9,14},{10,... | collective-permute-start | bytes 319496 | tf_op jit(solution)/shard_map/ppermute | solution.py:244
  90.2 14.8 %all-to-all-start.3 = ((f32[16,13,128]{2,1,0:T(8,128)}), f32[16,13,128]{2,1,0:T(8,128)S(1)}, u32[]{:S(2)}, u32[]{:S(2)}) async-start(f32[16,13,128]{2,1,0:T(8,128)} %reshape.60), calls=%async_computation.3 | async-start | bytes 262144 | tf_op jit(solution)/shard_map/all_to_all | solution.py:247
  97.2 7.8 %copy-start.1 = (s32[1,1,2,2]{3,2,1,0:T(2,128)S(1)}, s32[1,1,2,2]{3,2,1,0:T(2,128)}, u32[]{:S(2)}) copy-start(s32[1,1,2,2]{3,2,1,0:T(2,128)} %neg_ref.3) | copy-start | bytes 52

commit v9 on v8

--- a/solution.py
+++ b/solution.py
@@ -58,7 +58,10 @@
     tail = tails[:, 0].reshape(owners * group, LANES)
     for q in range(1, 4):
         tail = tail + pltpu.roll(tails[:, q].reshape(owners * group, LANES), TAIL * q, 1)
-    out_ref[:, (CHUNKS - 1) * slots :, :] = tail.reshape(owners, group, LANES)
+    half = group // 2
+    low = tail.reshape(owners, group, LANES)
+    high = pltpu.roll(tail, LANES // 2, 1).reshape(owners, group, LANES)
+    out_ref[:, (CHUNKS - 1) * slots :, :] = low[:, :half] + high[:, half:]
 
 
 def unpack(ref, out_ref):
@@ -67,7 +70,9 @@
     group = slots // 4
     for j in range(CHUNKS - 1):
         out_ref[:, j * LANES : (j + 1) * LANES] = ref[:, j * slots : (j + 1) * slots, :].reshape(owners * slots, LANES)
-    tail = ref[:, (CHUNKS - 1) * slots :, :].reshape(owners * group, LANES)
+    low = ref[:, (CHUNKS - 1) * slots :, :]
+    high = jnp.concatenate([low[:, :, LANES // 2 :], low[:, :, : LANES // 2]], axis=2)
+    tail = jnp.concatenate([low, high], axis=1).reshape(owners * group, LANES)
     live = lax.broadcasted_iota(jnp.int32, tail.shape, 1) < TAIL
     tails = []
     for q in range(4):
@@ -251,7 +256,7 @@
     entities, width = emb_table.shape
     owners, slots = send_rows.shape[2:]
     columns = lax.axis_size("bucket")
-    packed = (owners, (CHUNKS - 1) * slots + slots // 4, LANES)
+    packed = (owners, (CHUNKS - 1) * slots + slots // 8, LANES)
     send = send_rows.reshape(owners * slots)
     table = emb_table.T
     own_negs = pl.pallas_call(

time: 107 us -> 107 us (level)
  no operation moved by 1% of the time
where the time goes in v9:
time: 107 us; the launch traced here: 106 us
  starting transfers between devices  64.2 us (60%)
  waiting for transfers between devices  29.2 us (27%)
  Pallas kernels  9.51 us (9%)
  local copies, waits for them, and re-layouts  3.13 us (3%)
    ppermute x3, starting transfers between devices, gather_columns(): lax.ppermute(x, 'bucket', pairs)  15.4 us
    all_to_all x1, starting transfers between devices, gather_columns(): lax.all_to_all(x, 'bucket', split_axis=0, concat_axis=0, axis_index_group...  14.2 us
    ppermute x3, starting transfers between devices, sum_columns(): lax.ppermute(x[i], 'bucket', mirrors[i - 1])  13.2 us
    all_to_all x1, starting transfers between devices, on_device(): got = lax.all_to_all(picked, 'dom', split_axis=0, concat_axis=0, tiled=True)  8.77 us
    all_to_all x1, waiting for transfers between devices, sum_columns(): lax.all_to_all(x, 'bucket', split_axis=0, concat_axis=0, axis_index_group...  7.06 us
    all_to_all x1, starting transfers between devices, sum_columns(): lax.all_to_all(x, 'bucket', split_axis=0, concat_axis=0, axis_index_group...  6.98 us
    ppermute x3, waiting for transfers between devices, sum_columns(): lax.ppermute(x[i], 'bucket', mirrors[i - 1])  6.2 us
    all_to_all x1, starting transfers between devices, on_device(): lax.all_to_all(back, 'dom', split_axis=0, concat_axis=0, tiled=True)  5.7 us
  transfers between devices with their start and end apart: 10, of which 7 were waited for; matrix products, arithmetic and copies ran while one was open for 2% of the time, Pallas kernels for 2%

profile of v9, /device:TPU:1, one launch (start us, length us, event | category | flops | bytes accessed | tf_op | source)
XLA Modules:
  0.0 106.2 jit_solution(15747712053950186034)
XLA Ops:
  0.0 2.1 %negs.1 = f32[16,13,128]{2,1,0:T(8,128)} custom-call(s32[1,1,2,2]{3,2,1,0:T(2,128)} %neg_ref.3, f32[400,256]{1,0:T(8,128)} %bitcast.20), custom_call_target="tpu_custom_call" | custom-call | tf_op jit(solution)/shard_map/negs/pallas_call | solution.py:262
  2.1 14.2 %all-to-all-start = ((f32[16,13,128]{2,1,0:T(8,128)}), f32[16,13,128]{2,1,0:T(8,128)S(1)}, u32[]{:S(2)}, u32[]{:S(2)}) async-start(f32[16,13,128]{2,1,0:T(8,128)} %negs.1), calls=%async_computation | async-start | bytes 262144 | tf_op jit(solution)/shard_map/all_to_all | solution.py:241
  16.3 0.3 broadcast_in_dim_reshape.8.send_ref
  16.6 1.7 %pick.1 = f32[16,100,128]{2,1,0:T(8,128)} custom-call(s32[512,1]{1,0:T(8,128)S(1)} %broadcast_in_dim_reshape.8.send_ref, f32[400,256]{1,0:T(8,128)S(1)} %bitcast.21), custom_call_target="tpu_custom_call" | custom-call | tf_op jit(solution)/shard_map/pick/pallas_call | solution.py:270
  18.3 5.7 %all-to-all-done = f32[16,13,128]{2,1,0:T(8,128)S(1)} async-done(((f32[16,13,128]{2,1,0:T(8,128)}), f32[16,13,128]{2,1,0:T(8,128)S(1)}, u32[]{:S(2)}, u32[]{:S(2)}) %all-to-all-start) | async-done | bytes 106528 | tf_op jit(solution)/shard_map/all_to_all | solution.py:241
  24.0 8.8 %all-to-all-start.1 = ((f32[16,100,128]{2,1,0:T(8,128)}), f32[16,100,128]{2,1,0:T(8,128)S(1)}, u32[]{:S(2)}, u32[]{:S(2)}) async-start(f32[16,100,128]{2,1,0:T(8,128)} %pick.1), calls=%async_computation.1 | async-start | bytes 1703936 | tf_op jit(solution)/shard_map/all_to_all | solution.py:279
  32.7 0.2 copy.9
  32.9 0.0 copy-start.5
  33.0 10.2 %collective-permute-start.2 = (f32[208,128]{1,0:T(8,128)S(1)}, f32[208,128]{1,0:T(8,128)S(1)}, u32[]{:S(2)}, u32[]{:S(2)}) collective-permute-start(f32[208,128]{1,0:T(8,128)S(1)} %reshape.55), channel_id=1, source_target_pairs={{0,63},{1,62},{2,61},{3,60},{4,59},{5,58},{6,57},{7,56},{8,55},{9,... | collective-permute-start | bytes 319496 | tf_op jit(solution)/shard_map/ppermute | solution.py:243
  43.1 1.9 %collective-permute-start = (f32[208,128]{1,0:T(8,128)S(1)}, f32[208,128]{1,0:T(8,128)S(1)}, u32[]{:S(2)}, u32[]{:S(2)}) collective-permute-start(f32[208,128]{1,0:T(8,128)S(1)} %reshape.55), channel_id=1, source_target_pairs={{0,7},{1,6},{2,5},{3,4},{4,3},{5,2},{6,1},{7,0},{8,15},{9,14},{10,... | collective-permute-start | bytes 319496 | tf_op jit(solution)/shard_map/ppermute | solution.py:243
  45.1 3.3 %collective-permute-start.1 = (f32[208,128]{1,0:T(8,128)S(1)}, f32[208,128]{1,0:T(8,128)S(1)}, u32[]{:S(2)}, u32[]{:S(2)}) collective-permute-start(f32[208,128]{1,0:T(8,128)S(1)} %reshape.55), channel_id=1, source_target_pairs={{0,56},{1,57},{2,58},{3,59},{4,60},{5,61},{6,62},{7,63},{8,48},{9,... | collective-permute-start | bytes 319496 | tf_op jit(solution)/shard_map/ppermute | solution.py:243
  48.4 0.0 copy-start.4
  48.4 0.7 copy-done.4
  49.1 0.1 copy.11.col_ref
  49.2 0.5 copy-done.6
  49.7 0.6 gather_fusion
  50.3 4.7 %collective-permute-done = f32[208,128]{1,0:T(8,128)S(1)} collective-permute-done((f32[208,128]{1,0:T(8,128)S(1)}, f32[208,128]{1,0:T(8,128)S(1)}, u32[]{:S(2)}, u32[]{:S(2)}) %collective-permute-start) | collective-permute-done | bytes 106528 | tf_op jit(solution)/shard_map/ppermute | solution.py:243
  55.1 1.6 %all-to-all-done.1.got_ref = f32[16,100,128]{2,1,0:T(8,128)S(1)} async-done(((f32[16,100,128]{2,1,0:T(8,128)}), f32[16,100,128]{2,1,0:T(8,128)S(1)}, u32[]{:S(2)}, u32[]{:S(2)}) %all-to-all-start.1) | async-done | bytes 819232 | tf_op jit(solution)/shard_map/all_to_all | solution.py:279
  56.7 3.9 %grad.1 = (f32[16,100,128]{2,1,0:T(8,128)}, f32[832,128]{1,0:T(8,128)S(1)}) custom-call(s32[512,1]{1,0:T(8,128)S(1)} %copy.11.col_ref, s32[1,512]{1,0:T(1,128)S(1)} %bitcast.23, f32[2,512]{1,0:T(2,128)S(1)} %pad.4.rel_ref, f32[16,100,128]{2,1,0:T(8,128)S(1)} %all-to-all-done.1.got_ref, f32[832,128]{1,0:T(8,128)S(1)} %bitcast.19), custom_call_target="tpu_custom_call" | custom-call | tf_op jit(solution)/shard_map/grad/pallas_call | solution.py:282
  60.6 5.7 %all-to-all-start.2 = ((f32[16,100,128]{2,1,0:T(8,128)}), f32[16,100,128]{2,1,0:T(8,128)S(1)}, u32[]{:S(2)}, u32[]{:S(2)}) async-start(f32[16,100,128]{2,1,0:T(8,128)} %get-tuple-element.15), calls=%async_computation.2 | async-start | bytes 1703936 | tf_op jit(solution)/shard_map/all_to_all | solution.py:295
  66.3 8.0 %collective-permute-start.3 = (f32[208,128]{1,0:T(8,128)S(1)}, f32[208,128]{1,0:T(8,128)S(1)}, u32[]{:S(2)}, u32[]{:S(2)}) collective-permute-start(f32[208,128]{1,0:T(8,128)S(1)} %get-tuple-element.19), channel_id=1, source_target_pairs={{0,63},{1,62},{2,61},{3,60},{4,59},{5,58},{6,57},{7,56},{8,55},{9,... | collective-permute-start | bytes 319496 | tf_op jit(solution)/shard_map/ppermute | solution.py:249
  74.3 3.3 %collective-permute-start.4 = (f32[208,128]{1,0:T(8,128)S(1)}, f32[208,128]{1,0:T(8,128)S(1)}, u32[]{:S(2)}, u32[]{:S(2)}) collective-permute-start(f32[208,128]{1,0:T(8,128)S(1)} %get-tuple-element.17), channel_id=1, source_target_pairs={{0,56},{1,57},{2,58},{3,59},{4,60},{5,61},{6,62},{7,63},{8,48},{9,... | collective-permute-start | bytes 319496 | tf_op jit(solution)/shard_map/ppermute | solution.py:249
  77.6 1.9 %collective-permute-start.5 = (f32[208,128]{1,0:T(8,128)S(1)}, f32[208,128]{1,0:T(8,128)S(1)}, u32[]{:S(2)}, u32[]{:S(2)}) collective-permute-start(f32[208,128]{1,0:T(8,128)S(1)} %get-tuple-element.18), channel_id=1, source_target_pairs={{0,7},{1,6},{2,5},{3,4},{4,3},{5,2},{6,1},{7,0},{8,15},{9,14},{10,... | collective-permute-start | bytes 319496 | tf_op jit(solution)/shard_map/ppermute | solution.py:249
  79.5 0.6 collective-permute-done.3
  80.1 5.6 %collective-permute-done.4 = f32[208,128]{1,0:T(8,128)S(1)} collective-permute-done((f32[208,128]{1,0:T(8,128)S(1)}, f32[208,128]{1,0:T(8,128)S(1)}, u32[]{:S(2)}, u32[]{:S(2)}) %collective-permute-start.4) | collective-permute-done | bytes 106528 | tf_op jit(solution)/shard_map/ppermute | solution.py:249
  85.8 0.7 reshape.60
  86.4 3.8 %all-to-all-done.2.got_ref = f32[16,100,128]{2,1,0:T(8,128)S(1)} async-done(((f32[16,100,128]{2,1,0:T(8,128)}), f32[16,100,128]{2,1,0:T(8,128)S(1)}, u32[]{:S(2)}, u32[]{:S(2)}) %all-to-all-start.2) | async-done | bytes 819232 | tf_op jit(solution)/shard_map/all_to_all | solution.py:295
  90.3 7.0 %all-to-all-start.3 = ((f32[16,13,128]{2,1,0:T(8,128)}), f32[16,13,128]{2,1,0:T(8,128)S(1)}, u32[]{:S(2)}, u32[]{:S(2)}) async-start(f32[16,13,128]{2,1,0:T(8,128)} %reshape.60), calls=%async_computation.3 | async-start | bytes 262144 | tf_op jit(solution)/shard_map/all_to_all | solution.py:252
  97.3 0.1 broadcast_in_dim_reshape.6.send_ref
  97.3 0.7 put.1.put_ref
  98.0 7.1 %all-to-all-done.3.parts_ref = f32[16,13,128]{2,1,0:T(8,128)S(1)} async-done(((f32[16,13,128]{2,1,0:T(8,128)}), f32[16,13,128]{2,1,0:T(8,128)S(1)}, u32[]{:S(2)}, u32[]{:S(2)}) %all-to-all-start.3) | async-done | bytes 106528 | tf_op jit(solution)/shard_map/all_to_all | solution.py:252
  105.1 1.2 %add.34 = f32[400,256]{1,0:T(8,128)} custom-call(s32[1,1,2,2]{3,2,1,0:T(2,128)S(1)} %copy-done.1, f32[512,256]{1,0:T(8,128)S(1)} %put.1.put_ref, f32[16,13,128]{2,1,0:T(8,128)S(1)} %all-to-all-done.3.parts_ref), custom_call_target="tpu_custom_call" | custom-call | tf_op jit(solution)/shard_map/add/pallas_call | solution.py:304
  (21 shorter events, 0.1 us)
Async XLA Ops:
  0.0 16.6 %copy-start = (f32[256,400]{0,1:T(8,128)S(1)}, f32[256,400]{0,1:T(8,128)}, u32[]{:S(2)}) copy-start(f32[256,400]{0,1:T(8,128)} %param.7) | copy-start | bytes 1228804
  2.1 14.2 %copy-start.3 = (s32[1,1,16,32]{3,2,1,0:T(8,128)S(1)}, s32[1,1,16,32]{3,2,1,0:T(8,128)}, u32[]{:S(2)}) copy-start(s32[1,1,16,32]{3,2,1,0:T(8,128)} %param.9) | copy-start | bytes 6148
  2.1 21.8 %all-to-all-start = ((f32[16,13,128]{2,1,0:T(8,128)}), f32[16,13,128]{2,1,0:T(8,128)S(1)}, u32[]{:S(2)}, u32[]{:S(2)}) async-start(f32[16,13,128]{2,1,0:T(8,128)} %negs.1), calls=%async_computation | async-start | bytes 262144 | tf_op jit(solution)/shard_map/all_to_all | solution.py:241
  18.3 14.5 %copy-start.2 = (f32[256,400]{0,1:T(8,128)S(1)}, f32[256,400]{0,1:T(8,128)}, u32[]{:S(2)}) copy-start(f32[256,400]{0,1:T(8,128)} %param.8) | copy-start | bytes 1228804
  24.0 32.7 %all-to-all-start.1 = ((f32[16,100,128]{2,1,0:T(8,128)}), f32[16,100,128]{2,1,0:T(8,128)S(1)}, u32[]{:S(2)}, u32[]{:S(2)}) async-start(f32[16,100,128]{2,1,0:T(8,128)} %pick.1), calls=%async_computation.1 | async-start | bytes 1703936 | tf_op jit(solution)/shard_map/all_to_all | solution.py:279
  32.9 15.5 %copy-start.5 = (s32[1,1,256]{2,1,0:T(1,128)S(1)}, s32[1,1,256]{2,1,0:T(1,128)}, u32[]{:S(2)}) copy-start(s32[1,1,256]{2,1,0:T(1,128)} %param.10) | copy-start | bytes 3076
  33.0 17.3 %collective-permute-start.2 = (f32[208,128]{1,0:T(8,128)S(1)}, f32[208,128]{1,0:T(8,128)S(1)}, u32[]{:S(2)}, u32[]{:S(2)}) collective-permute-start(f32[208,128]{1,0:T(8,128)S(1)} %reshape.55), channel_id=1, source_target_pairs={{0,63},{1,62},{2,61},{3,60},{4,59},{5,58},{6,57},{7,56},{8,55},{9,... | collective-permute-start | bytes 319496 | tf_op jit(solution)/shard_map/ppermute | solution.py:243
  43.1 11.9 %collective-permute-start = (f32[208,128]{1,0:T(8,128)S(1)}, f32[208,128]{1,0:T(8,128)S(1)}, u32[]{:S(2)}, u32[]{:S(2)}) collective-permute-start(f32[208,128]{1,0:T(8,128)S(1)} %reshape.55), channel_id=1, source_target_pairs={{0,7},{1,6},{2,5},{3,4},{4,3},{5,2},{6,1},{7,0},{8,15},{9,14},{10,... | collective-permute-start | bytes 319496 | tf_op jit(solution)/shard_map/ppermute | solution.py:243
  45.1 10.0 %collective-permute-start.1 = (f32[208,128]{1,0:T(8,128)S(1)}, f32[208,128]{1,0:T(8,128)S(1)}, u32[]{:S(2)}, u32[]{:S(2)}) collective-permute-start(f32[208,128]{1,0:T(8,128)S(1)} %reshape.55), channel_id=1, source_target_pairs={{0,56},{1,57},{2,58},{3,59},{4,60},{5,61},{6,62},{7,63},{8,48},{9,... | collective-permute-start | bytes 319496 | tf_op jit(solution)/shard_map/ppermute | solution.py:243
  48.4 0.7 copy-start.4
  49.1 0.7 copy-start.6
  60.6 29.7 %all-to-all-start.2 = ((f32[16,100,128]{2,1,0:T(8,128)}), f32[16,100,128]{2,1,0:T(8,128)S(1)}, u32[]{:S(2)}, u32[]{:S(2)}) async-start(f32[16,100,128]{2,1,0:T(8,128)} %get-tuple-element.15), calls=%async_computation.2 | async-start | bytes 1703936 | tf_op jit(solution)/shard_map/all_to_all | solution.py:295
  66.3 13.8 %collective-permute-start.3 = (f32[208,128]{1,0:T(8,128)S(1)}, f32[208,128]{1,0:T(8,128)S(1)}, u32[]{:S(2)}, u32[]{:S(2)}) collective-permute-start(f32[208,128]{1,0:T(8,128)S(1)} %get-tuple-element.19), channel_id=1, source_target_pairs={{0,63},{1,62},{2,61},{3,60},{4,59},{5,58},{6,57},{7,56},{8,55},{9,... | collective-permute-start | bytes 319496 | tf_op jit(solution)/shard_map/ppermute | solution.py:249
  74.3 11.4 %collective-permute-start.4 = (f32[208,128]{1,0:T(8,128)S(1)}, f32[208,128]{1,0:T(8,128)S(1)}, u32[]{:S(2)}, u32[]{:S(2)}) collective-permute-start(f32[208,128]{1,0:T(8,128)S(1)} %get-tuple-element.17), channel_id=1, source_target_pairs={{0,56},{1,57},{2,58},{3,59},{4,60},{5,61},{6,62},{7,63},{8,48},{9,... | collective-permute-start | bytes 319496 | tf_op jit(solution)/shard_map/ppermute | solution.py:249
  77.6 8.1 %collective-permute-start.5 = (f32[208,128]{1,0:T(8,128)S(1)}, f32[208,128]{1,0:T(8,128)S(1)}, u32[]{:S(2)}, u32[]{:S(2)}) collective-permute-start(f32[208,128]{1,0:T(8,128)S(1)} %get-tuple-element.18), channel_id=1, source_target_pairs={{0,7},{1,6},{2,5},{3,4},{4,3},{5,2},{6,1},{7,0},{8,15},{9,14},{10,... | collective-permute-start | bytes 319496 | tf_op jit(solution)/shard_map/ppermute | solution.py:249
  90.3 14.8 %all-to-all-start.3 = ((f32[16,13,128]{2,1,0:T(8,128)}), f32[16,13,128]{2,1,0:T(8,128)S(1)}, u32[]{:S(2)}, u32[]{:S(2)}) async-start(f32[16,13,128]{2,1,0:T(8,128)} %reshape.60), calls=%async_computation.3 | async-start | bytes 262144 | tf_op jit(solution)/shard_map/all_to_all | solution.py:252
  97.3 7.7 %copy-start.1 = (s32[1,1,2,2]{3,2,1,0:T(2,128)S(1)}, s32[1,1,2,2]{3,2,1,0:T(2,128)}, u32[]{:S(2)}) copy-start(s32[1,1,2,2]{3,2,1,0:T(2,128)} %neg_ref.3) | copy-start | bytes 52
